TPU v7x, 512 devices: a whole 4x4x16 slice. The times are simulated.
512 devices in a mesh: tm: 32 (over z, y_hi), feat: 8 (over x, core), rep: 2 (over y_lo).
Axes of the slice: x: 4, y: 4 (y_hi: 2, y_lo: 2; y = y_hi * 2 + y_lo), z: 16, core: 2. Of those that a mesh axis runs over, the one named last changes fastest.
Arguments:
- frames: bfloat16 [2, 8192, 16384], P('rep', 'tm', 'feat'), may hold values from -50 to 50, as said below
- panel_low: bfloat16 [16384, 512], P('feat', 'tm'), may hold values from -0.046875 to 0.046875
- panel_high: bfloat16 [16384, 512], P('feat', 'tm'), may hold values from -0.046875 to 0.046875
- lags: int32 [2], P('rep'), may hold values from 1 to 64, as said below
- seg_lengths: int32 [2, 64], P('rep'), may hold values from 1 to 1024, 8192 in all within a row
- ridge: float32 [32], replicated, may hold values from 0.01 to 10
Outputs:
- covariances: float32 [3, 1024, 1024], P(None, ('tm', 'feat', 'rep'))
- scores: float32 [1024, 32], P(('tm', 'feat', 'rep'))
Inputs may be any that keep to these rules, and one draw needn't show every extreme that they name: The frames of each run follow one trajectory in time. `lags`: one run has the lag 64. `seg_lengths`: each row sums to 8192.
All inputs are finite; a program needn't handle non-finite values.
Results may differ from a plain program's by a relative error of at most 0.003.
Values may be sent and summed in bfloat16 or wider, within the bound.
No kernel may reach another device: no remote copies, remote signals or barrier semaphores. Data moves between devices by JAX's collectives and lax.ppermute only.
A program may use at most 64 MiB of HBM per device.

v0:
```python
import jax
import jax.numpy as jnp
from jax import lax
from jax.sharding import PartitionSpec as P


def passed_along(shard, axis, by):
    length = lax.axis_size(axis)
    pairs = [(i, i + by) for i in range(length) if 0 <= i + by < length]
    return lax.ppermute(shard, axis, pairs)


def local(frames, panel_low, panel_high, lags, seg_lengths, ridge):
    local_frames = frames[0]
    t_local = local_frames.shape[0]
    lag_most = t_local // 4
    n_time = lax.axis_size("tm")
    n_feature = lax.axis_size("feat")
    n_replica = lax.axis_size("rep")
    panel_cols = panel_low.shape[1] * n_time
    basis_width = 2 * panel_cols
    per_device = basis_width // (n_time * n_feature * n_replica)
    time_index = lax.axis_index("tm")
    feature_index = lax.axis_index("feat")
    replica_index = lax.axis_index("rep")
    stacked = jnp.stack([panel_low, panel_high], axis=0)
    partial_sum = jnp.einsum(
        "tf,pfk->tpk",
        local_frames,
        lax.all_gather(stacked, "tm", axis=2, tiled=True),
        preferred_element_type=jnp.float32,
    )
    partial_sum = partial_sum.reshape(local_frames.shape[0], basis_width)
    partial_rounded = partial_sum.astype(jnp.bfloat16)
    summed = lax.psum(partial_rounded, "feat").astype(jnp.float32).astype(jnp.bfloat16)
    next_basis = passed_along(summed[:lag_most], "tm", -1)
    extended = jnp.concatenate([summed, next_basis], axis=0)
    lag_now = lags[0]
    lagged = lax.dynamic_slice_in_dim(extended, lag_now, t_local, 0)
    frame_total = t_local * n_time
    positions = time_index * t_local + jnp.arange(t_local, dtype=jnp.int32)
    seg_ends = jnp.cumsum(seg_lengths[0])
    end_of = jnp.min(
        jnp.where(seg_ends[None, :] > positions[:, None], seg_ends[None, :], frame_total), axis=1
    )
    keep_mask = (positions + lag_now < end_of).astype(jnp.bfloat16)[:, None]
    masked = summed * keep_mask
    lag_masked = lagged * keep_mask

    def own_group(values):
        shaped = values.reshape(t_local, n_time, n_feature, n_replica * per_device)
        return lax.dynamic_index_in_dim(shaped, feature_index, 2, keepdims=False).reshape(
            t_local, -1
        )

    group_masked = own_group(masked)
    group_lagged = own_group(lag_masked)
    term_inst = jnp.einsum("ti,tj->ij", group_masked, summed, preferred_element_type=jnp.float32)
    term_cross = jnp.einsum("ti,tj->ij", group_masked, lagged, preferred_element_type=jnp.float32)
    term_lagged = jnp.einsum("ti,tj->ij", group_lagged, lagged, preferred_element_type=jnp.float32)
    row_block = lax.psum_scatter(
        jnp.stack([term_inst, term_cross, term_lagged], axis=1),
        ("tm", "rep"),
        scatter_dimension=0,
        tiled=True,
    )
    inverse_count = 1.0 / (frame_total * n_replica)
    cov_rows = jnp.transpose(row_block, (1, 0, 2)) * inverse_count
    device_linear = (time_index * n_feature + feature_index) * n_replica + replica_index
    own_index = device_linear * per_device + jnp.arange(per_device, dtype=jnp.int32)
    selector = (jnp.arange(basis_width, dtype=jnp.int32)[None, :] == own_index[:, None]).astype(
        jnp.float32
    )
    diag_inst = jnp.sum(cov_rows[0] * selector, axis=1)
    local_var = jnp.sum(jnp.square(lag_masked.astype(jnp.float32)), axis=0)
    diag_lagged = lax.psum(local_var, ("tm", "rep")) * inverse_count
    inverse_lagged = 1.0 / (diag_lagged[:, None] + ridge[None, :])
    weighted = jnp.dot(
        jnp.square(cov_rows[1]),
        inverse_lagged,
        precision=lax.Precision.HIGHEST,
        preferred_element_type=jnp.float32,
    )
    scores = weighted / (diag_inst[:, None] + ridge[None, :])
    return (cov_rows, scores)


def solution(mesh):
    in_specs = (
        P("rep", "tm", "feat"),
        P("feat", "tm"),
        P("feat", "tm"),
        P("rep"),
        P("rep", None),
        P(),
    )
    out_specs = (P(None, ("tm", "feat", "rep"), None), P(("tm", "feat", "rep"), None))
    return jax.shard_map(local, mesh=mesh, in_specs=in_specs, out_specs=out_specs, check_vma=False)
```

profile of v0, /device:TPU:1, one launch (start us, length us, event | category | flops | bytes accessed | tf_op | source)
XLA Modules:
  0.0 548.0 jit_solution(13129286283907650634)
XLA Ops:
  7.2 1.6 pad_maximum_fusion.1
  8.9 0.7 copy.11
  9.7 0.1 reduce-window.8
  9.8 0.1 reduce
  9.9 162.7 %all-gather.2.cloned.1.call-done = bf16[2,2048,512]{1,2,0:T(8,128)(2,1)} async-done(((bf16[2,2048,16]{1,2,0:T(8,128)(2,1)}), bf16[2,2048,512]{1,2,0:T(8,128)(2,1)}) %all-gather.2.cloned.1.call-update) | async-done | bytes 4194320 | tf_op jit(solution)/shard_map/all_gather | solution.py:30
  172.6 4.3 convolution_convert_fusion
  177.7 76.6 %all-reduce.4.cloned.1.call-done = bf16[256,1024]{0,1:T(8,128)(2,1)} async-done(((bf16[256,1024]{0,1:T(8,128)(2,1)}), bf16[256,1024]{0,1:T(8,128)(2,1)}) %all-reduce.4.cloned.1.call-update) | async-done | bytes 524304 | tf_op jit(solution)/shard_map/psum | solution.py:35
  254.3 1.7 slice.12
  256.1 1.3 collective-permute-start
  257.4 1.1 broadcast_multiply_fusion.1
  258.4 0.1 reshape.65
  258.7 0.3 convolution_bitcast_fusion.2
  259.0 6.4 %collective-permute-done = bf16[64,1024]{0,1:T(8,128)(2,1)S(1)} collective-permute-done((bf16[64,1024]{0,1:T(8,128)(2,1)}, bf16[64,1024]{0,1:T(8,128)(2,1)S(1)}, u32[]{:S(2)}, u32[]{:S(2)}) %collective-permute-start) | collective-permute-done | bytes 131104 | tf_op jit(solution)/shard_map/ppermute | solution.py:10
  265.3 0.7 multiply_reduce_fusion
  266.1 0.1 reshape.67
  266.3 0.3 convolution_bitcast_fusion.1
  266.6 0.3 convolution_bitcast_fusion
  266.9 1.2 pad_maximum_fusion
  268.2 1.3 dynamic-slice
  270.1 113.6 %psum.15 = f32[1024]{0:T(1024)S(1)} all-reduce(f32[1024]{0:T(1024)S(1)} %get-tuple-element.2), channel_id=1, replica_groups=mesh['tm'=32,'feat'=8,'rep'=2] {'tm','rep'}, use_global_device_ids=true, to_apply=%region_5.6 | all-reduce | flops 1024 | bytes 8192 | tf_op jit(solution)/shard_map/psum | solution.py:76
  383.8 155.6 %all-reduce.6.cloned.1.call-done = f32[128,3,1024]{2,0,1:T(8,128)} async-done(((f32[128,3,1024]{2,0,1:T(8,128)}), f32[128,3,1024]{2,0,1:T(8,128)}) %all-reduce.6.cloned.1.call-update) | async-done | bytes 1572880
  539.3 0.9 fusion.5
  540.3 0.2 fusion.6
  540.4 1.1 convolution_divide_fusion
  (23 shorter events, 0.4 us)
Async XLA Ops:
  7.2 165.4 %copy-start = (bf16[1,256,2048]{2,1,0:T(8,128)(2,1)S(1)}, bf16[1,256,2048]{2,1,0:T(8,128)(2,1)}, u32[]{:S(2)}) copy-start(bf16[1,256,2048]{2,1,0:T(8,128)(2,1)} %param.6) | copy-start | bytes 3145732
  7.2 165.4 %all-gather.2.cloned.1.call-start = ((), (), s32[]{:S(2)}) async-start(), calls=%async_computation | async-start | bytes 4325376 | tf_op jit(solution)/shard_map/all_gather | solution.py:30
  8.9 245.5 %all-reduce.4.cloned.1.call-start = ((), (), s32[]{:S(2)}) async-start(), calls=%async_computation.1 | async-start | bytes 1048576 | tf_op jit(solution)/shard_map/psum | solution.py:35
  176.9 362.4 %all-reduce.6.cloned.1.call-start = ((), (), s32[]{:S(2)}) async-start(), calls=%async_computation.2 | async-start | bytes 3145728
  254.3 4.3 copy-start.1
  256.1 9.3 %collective-permute-start = (bf16[64,1024]{0,1:T(8,128)(2,1)}, bf16[64,1024]{0,1:T(8,128)(2,1)S(1)}, u32[]{:S(2)}, u32[]{:S(2)}) collective-permute-start(bf16[64,1024]{0,1:T(8,128)(2,1)} %slice.12), channel_id=1, source_target_pairs={{16,0},{32,16},{48,32},{64,48},{80,64},{96,80},{112,96},{128,112},... | collective-permute-start | bytes 393224 | tf_op jit(solution)/shard_map/ppermute | solution.py:10
  268.1 272.3 %copy-start.3 = (f32[32]{0:T(128)S(1)}, f32[32]{0:T(128)}, u32[]{:S(2)}) copy-start(f32[32]{0:T(128)} %param.11) | copy-start | bytes 388
  540.2 1.3 copy-start.2
Sparse Core Ops, SparseCore 0:
  11.1 161.4 all-gather.1
  177.0 77.2 all-reduce.3
  268.3 271.0 all-reduce.5
where the time goes:
time: 558 us; the launch traced here: 548 us
  waiting for transfers between devices  401 us (72%)
  blocking collectives  114 us (20%)
  between operations  15.2 us (3%)
  matrix products  6.25 us (1%)
  other arithmetic  6.08 us (1%)
    all_gather x1, waiting for transfers between devices, local(): lax.all_gather(stacked, 'tm', axis=2, tiled=True)  163 us
    unnamed x4, waiting for transfers between devices  156 us
    psum x1, blocking collectives, local(): diag_lagged = lax.psum(local_var, ('tm', 'rep')) * inverse_count  114 us
    psum x1, waiting for transfers between devices, local(): lax.psum(partial_rounded, 'feat').astype(jnp.float32).astype(jnp.bfloat16)  76.6 us
  transfers between devices with their start and end apart: 4, of which 4 were waited for; matrix products, arithmetic and copies ran while one was open for 1% of the time, Pallas kernels for 0%

commit v1 on v0

v1 whole, which is shorter than its diff:
```python
import jax
import jax.numpy as jnp
import numpy as np
from jax import lax
from jax.experimental import pallas as pl
from jax.experimental.pallas import tpu as pltpu
from jax.sharding import Mesh, PartitionSpec as P

BF = jnp.bfloat16
F32 = jnp.float32
I32 = jnp.int32
HI = lax.Precision.HIGHEST
NT = (((1,), (1,)), ((), ()))
VMEM = pltpu.CompilerParams(vmem_limit_bytes=48 * 1024 * 1024)

Z = ("zh", "zl")
FE = ("x", "c")
CHUNKS = ("yh", "yl", "x", "c")


def one_hot(rows, cols, hit):
    r = lax.broadcasted_iota(I32, (rows, cols), 0)
    c = lax.broadcasted_iota(I32, (rows, cols), 1)
    return jnp.where(hit(r, c), 1.0, 0.0).astype(BF)


def pack_kernel(yl_ref, low_ref, high_ref, out_ref):
    yl = yl_ref[0]
    src = one_hot(16, 16, lambda r, c: c == ((r >> 1) & 3) * 4 + (r >> 3) * 2 + (r & 1))
    for yh in range(2):
        off = pl.multiple_of((yl * 2 + yh) * 512, 512)
        for half, ref in enumerate((low_ref, high_ref)):
            rows = ref[:, pl.ds(off, 512)]
            out_ref[yh, half] = jnp.dot(src, rows, preferred_element_type=F32).astype(BF)


def project_kernel(pa_ref, pb_ref, frames_ref, out_ref, panel_ref):
    @pl.when(pl.program_id(0) == 0)
    def _():
        for zl in range(4):
            for zh in range(4):
                ref = pa_ref if zh < 2 else pb_ref
                for half in range(2):
                    for yl in range(2):
                        chunk = ((zl & 1) * 2 + yl) * 8 + half * 4 + zh
                        row = chunk * 32 + (zl >> 1) * 16
                        panel_ref[row : row + 16, :] = ref[zl, zh & 1, half, yl]

    out_ref[...] = lax.dot_general(
        panel_ref[...], frames_ref[...], NT, preferred_element_type=F32
    ).astype(BF)


def cov_kernel(lags_ref, place_ref, seg_ref, left_ref, right_ref, out_ref):
    z = place_ref[0]
    perm = one_hot(
        128,
        128,
        lambda r, c: c
        == ((r >> 5) & 1) * 64 + ((r >> 1) & 1) * 32 + (r >> 6) * 16 + ((r >> 2) & 7) * 2 + (r & 1),
    )
    right = jnp.dot(perm, right_ref[...], preferred_element_type=F32)
    halo = right[:, 1024:1152]
    tri = lax.broadcasted_iota(I32, (64, 64), 1) <= lax.broadcasted_iota(I32, (64, 64), 0)
    seg = seg_ref[...].astype(F32)
    keep, keep_end, lagged = [], [], []
    for rep in range(2):
        lag = lags_ref[rep]
        ends = jnp.sum(jnp.where(tri, seg[rep : rep + 1, :], 0.0), axis=1, keepdims=True)
        pos = lax.broadcasted_iota(I32, (1, 512), 1) + z * 512
        here = pos.astype(F32)
        ahead = (pos + lag).astype(F32)
        behind = (pos - lag).astype(F32)
        cut = jnp.where((ends > here) & (ends <= ahead), 1.0, 0.0)
        keep.append(1.0 - jnp.max(cut, axis=0, keepdims=True))
        cut_end = jnp.where((ends > behind) & (ends <= here), 1.0, 0.0)
        inside = jnp.where(behind >= 0.0, 1.0, 0.0)
        keep_end.append((1.0 - jnp.max(cut_end, axis=0, keepdims=True)) * inside)
        tail = halo if rep == 0 else pltpu.roll(halo, 64, 1)
        ext = jnp.concatenate([right[:, rep * 512 : (rep + 1) * 512], tail], axis=1)
        lagged.append(pltpu.roll(ext, 640 - lag, 1)[:, :512].astype(BF))
    keep = jnp.concatenate(keep, axis=1)
    keep_end = jnp.concatenate(keep_end, axis=1)
    lagged = jnp.concatenate(lagged, axis=1)
    now = right[:, :1024]
    now_bf = now.astype(BF)
    left = left_ref[...]
    left_start = left * keep.astype(BF)
    left_end = left * keep_end.astype(BF)
    for m, (lhs, rhs) in enumerate(
        ((left_start, now_bf), (left_start, lagged), (left_end, now_bf))
    ):
        block = lax.dot_general(lhs, rhs, NT, preferred_element_type=F32)
        for d in range(16):
            out_ref[d, m * 16 : (m + 1) * 16, :] = block[d * 16 : (d + 1) * 16, :]
    var = lax.dot_general(
        jnp.ones((8, 1024), F32), now * now * keep_end, NT, precision=HI, preferred_element_type=F32
    )
    for d in range(16):
        out_ref[d, 48:56, :] = var


def rows_kernel(scale, parts_ref, ridge_ref, out_ref):
    total = parts_ref[0]
    for d in range(1, 16):
        total = total + parts_ref[d]
    total = total * scale
    var = total[48:49, :]
    inverse = 1.0 / (var + ridge_ref[...])
    cross = total[16:32, :]
    inverse = jnp.concatenate([inverse, jnp.zeros((96, 128), F32)], axis=0)
    weighted = lax.dot_general(cross * cross, inverse, NT, precision=HI, preferred_element_type=F32)
    for d in range(8):
        for m in range(3):
            out_ref[d, m * 2 : m * 2 + 2, :] = total[m * 16 + d * 2 : m * 16 + d * 2 + 2, :]
        out_ref[d, 6:8, :] = weighted[d * 2 : d * 2 + 2, :]


def final_kernel(place_ref, parts_ref, ridge_ref, cov_ref, score_ref):
    first = place_ref[1]
    weighted = parts_ref[0, 6:8, :]
    for f in range(1, 8):
        weighted = weighted + parts_ref[f, 6:8, :]
    lane = lax.broadcasted_iota(I32, (2, 128), 1)
    row = lax.broadcasted_iota(I32, (2, 128), 0)
    diag = jnp.zeros((2, 1), F32)
    for f in range(8):
        for m in range(3):
            cov_ref[m, :, f * 128 : (f + 1) * 128] = parts_ref[f, m * 2 : m * 2 + 2, :]
        own = lane + f * 128 == first + row
        diag = diag + jnp.sum(
            jnp.where(own, parts_ref[f, 0:2, :], 0.0), axis=1, keepdims=True
        )
    score_ref[...] = weighted[:, :32] / (diag + ridge_ref[...])


def local(frames, panel_low, panel_high, lags, seg_lengths, ridge):
    z = lax.axis_index(Z).astype(I32)
    yl = lax.axis_index("yl").astype(I32)
    own_first = ((z * 2 + lax.axis_index("yh")) * 8 + lax.axis_index(FE)) * 4 + yl * 2
    place = jnp.stack([z, own_first.astype(I32)])
    smem = pl.BlockSpec(memory_space=pltpu.SMEM)
    vmem = pl.BlockSpec(memory_space=pltpu.VMEM)

    mine = jnp.concatenate([lags.reshape(1, 1), seg_lengths], axis=1)
    other = lax.ppermute(mine, "yl", [(0, 1), (1, 0)])
    both = jnp.where(
        yl == 0, jnp.concatenate([mine, other], axis=0), jnp.concatenate([other, mine], axis=0)
    )

    packed = pl.pallas_call(
        pack_kernel,
        out_shape=jax.ShapeDtypeStruct((2, 2, 16, 512), BF),
        in_specs=[smem, vmem, vmem],
        out_specs=vmem,
        compiler_params=VMEM,
    )(yl[None], panel_low.T, panel_high.T)
    swapped = lax.all_to_all(packed, "yh", split_axis=0, concat_axis=0, tiled=True)
    swapped = swapped.reshape(2, 2, 2, 8, 512).transpose(1, 2, 0, 3, 4)
    stage = lax.all_gather(swapped.reshape(64, 512), "zh", axis=0, tiled=True)
    panel_a = lax.all_gather(stage[:128], "zl", axis=0, tiled=True).reshape(4, 2, 2, 2, 16, 512)
    panel_b = lax.all_gather(stage[128:], "zl", axis=0, tiled=True).reshape(4, 2, 2, 2, 16, 512)

    quarters = frames[0].reshape(256, 4, 512).transpose(1, 0, 2)
    frames_q = lax.all_to_all(quarters, ("yl", "yh"), split_axis=0, concat_axis=0, tiled=True)
    frames_q = frames_q.reshape(1024, 512)

    partial = pl.pallas_call(
        project_kernel,
        grid=(4,),
        out_shape=jax.ShapeDtypeStruct((1024, 1024), BF),
        in_specs=[
            pl.BlockSpec((4, 2, 2, 2, 16, 512), lambda i: (0, 0, 0, 0, 0, 0)),
            pl.BlockSpec((4, 2, 2, 2, 16, 512), lambda i: (0, 0, 0, 0, 0, 0)),
            pl.BlockSpec((256, 512), lambda i: (i, 0)),
        ],
        out_specs=pl.BlockSpec((1024, 256), lambda i: (0, i)),
        scratch_shapes=[pltpu.VMEM((1024, 512), BF)],
        compiler_params=VMEM,
    )(panel_a, panel_b, frames_q)

    pieces = lax.all_to_all(
        partial.reshape(32, 32, 1024), CHUNKS, split_axis=0, concat_axis=0, tiled=True
    )
    basis = jnp.sum(pieces.astype(F32), axis=0).astype(BF)

    head = jnp.concatenate([basis[:, 0:64], basis[:, 512:576]], axis=1)
    halo = lax.ppermute(head, Z, [(i + 1, i) for i in range(15)])
    left = lax.all_gather(basis, FE, axis=0, tiled=True)
    right = lax.all_gather(
        jnp.concatenate([basis, halo], axis=1), ("yh", "yl"), axis=0, tiled=True
    )

    terms = pl.pallas_call(
        cov_kernel,
        out_shape=jax.ShapeDtypeStruct((16, 56, 128), F32),
        in_specs=[smem, smem, vmem, vmem, vmem],
        out_specs=vmem,
        compiler_params=VMEM,
    )(both[:, 0], place, both[:, 1:], left, right)
    by_z = lax.all_to_all(terms, Z, split_axis=0, concat_axis=0, tiled=True)

    rows = pl.pallas_call(
        lambda *refs: rows_kernel(1.0 / 16384.0, *refs),
        out_shape=jax.ShapeDtypeStruct((8, 8, 128), F32),
        in_specs=[vmem, vmem],
        out_specs=vmem,
        compiler_params=VMEM,
    )(by_z, ridge[:, None])
    by_fe = lax.all_to_all(rows, FE, split_axis=0, concat_axis=0, tiled=True)

    return pl.pallas_call(
        final_kernel,
        out_shape=(
            jax.ShapeDtypeStruct((3, 2, 1024), F32),
            jax.ShapeDtypeStruct((2, 32), F32),
        ),
        in_specs=[smem, vmem, vmem],
        out_specs=(vmem, vmem),
        compiler_params=VMEM,
    )(place, by_fe, ridge[None, :])


def solution(mesh):
    fine = Mesh(
        np.asarray(mesh.devices).reshape(4, 4, 2, 4, 2, 2), ("zh", "zl", "yh", "x", "c", "yl")
    )
    tm = ("zh", "zl", "yh")
    in_specs = (P("yl", tm, FE), P(FE, tm), P(FE, tm), P("yl"), P("yl", None), P())
    rows = tm + FE + ("yl",)
    out_specs = (P(None, rows, None), P(rows, None))
    return jax.shard_map(local, mesh=fine, in_specs=in_specs, out_specs=out_specs, check_vma=False)
```

time: 558 us -> 189 us (0.34); the launches traced: 548 us -> 188 us
  waiting for transfers between devices: 401 us -> 43.7 us
  starting transfers between devices: 1.4 us -> 38.9 us
  blocking collectives: 114 us -> 90.4 us
  between operations: 15.2 us -> 1.42 us
  Pallas kernels: 0 us -> 7.87 us
  matrix products: 6.25 us -> 0 us
    all_gather x1 -> x0, waiting for transfers between devices: 163 us -> none  [local(): lax.all_gather(stacked, 'tm', axis=2, tiled=True)]
    unnamed x4 -> x0, waiting for transfers between devices: 156 us -> none
    psum x1 -> x0, blocking collectives: 114 us -> none  [local(): diag_lagged = lax.psum(local_var, ('tm', 'rep')) * inverse_count]
    psum x1 -> x0, waiting for transfers between devices: 76.6 us -> none  [local(): lax.psum(partial_rounded, 'feat').astype(jnp.float32).astype(jnp.bfloat16)]
    all_gather x0 -> x5, blocking collectives: none -> 75.2 us  [the longest x1 25.2 us: local(): stage = lax.all_gather(swapped.reshape(64, 512), 'zh', axis=0, tiled=True)]
    all_to_all x0 -> x4, starting transfers between devices: none -> 34.3 us  [the longest x1 18.1 us: local(): lax.all_to_all(partial.reshape(32, 32, 1024), CHUNKS, split_axis=0, conca...]
    all_to_all x0 -> x4, waiting for transfers between devices: none -> 30.7 us  [the longest x1 18.8 us: local(): by_z = lax.all_to_all(terms, Z, split_axis=0, concat_axis=0, tiled=True)]
    all_to_all x0 -> x1, blocking collectives: none -> 15.2 us  [local(): by_fe = lax.all_to_all(rows, FE, split_axis=0, concat_axis=0, tiled=True)]
  transfers between devices with their start and end apart: 4 -> 6, of which waited for: 4 -> 4; matrix products, arithmetic and copies ran while one was open for 1% -> 2% of each run, Pallas kernels for 0% -> 0%
where the time goes in v1:
time: 189 us; the launch traced here: 188 us
  blocking collectives  90.4 us (48%)
  waiting for transfers between devices  43.7 us (23%)
  starting transfers between devices  38.9 us (21%)
  Pallas kernels  7.87 us (4%)
  local copies, waits for them, and re-layouts  5 us (3%)
    all_gather x1, blocking collectives, local(): stage = lax.all_gather(swapped.reshape(64, 512), 'zh', axis=0, tiled=True)  25.2 us
    all_to_all x1, waiting for transfers between devices, local(): by_z = lax.all_to_all(terms, Z, split_axis=0, concat_axis=0, tiled=True)  18.8 us
    all_to_all x1, starting transfers between devices, local(): lax.all_to_all(partial.reshape(32, 32, 1024), CHUNKS, split_axis=0, conca...  18.1 us
    all_gather x1, blocking collectives, local(): left = lax.all_gather(basis, FE, axis=0, tiled=True)  15.3 us
    all_to_all x1, blocking collectives, local(): by_fe = lax.all_to_all(rows, FE, split_axis=0, concat_axis=0, tiled=True)  15.2 us
    all_gather x1, blocking collectives, local(): lax.all_gather(stage[:128], 'zl', axis=0, tiled=True)  13.2 us
    ppermute x1, waiting for transfers between devices, local(): other = lax.ppermute(mine, 'yl', [(0, 1), (1, 0)])  13 us
    all_gather x1, blocking collectives, local(): lax.all_gather(stage[128:], 'zl', axis=0, tiled=True)  12 us
  transfers between devices with their start and end apart: 6, of which 4 were waited for; matrix products, arithmetic and copies ran while one was open for 2% of the time, Pallas kernels for 0%

profile of v1, /device:TPU:1, one launch (start us, length us, event | category | flops | bytes accessed | tf_op | source)
XLA Modules:
  0.0 188.0 jit_solution(10412023904367868572)
XLA Ops:
  0.6 0.8 copy-done
  1.5 0.8 copy-done.1
  2.3 0.8 shard_map.77
  3.1 5.0 %all-to-all-start = ((bf16[2,2,16,512]{3,2,1,0:T(8,128)(2,1)}), bf16[2,2,16,512]{3,2,1,0:T(8,128)(2,1)S(1)}, u32[]{:S(2)}, u32[]{:S(2)}) async-start(bf16[2,2,16,512]{3,2,1,0:T(8,128)(2,1)} %shard_map.77), calls=%async_computation | async-start | bytes 131072 | tf_op jit(solution)/shard_map/all_to_all | solution.py:158
  8.1 1.8 reshape_squeeze.3
  10.0 1.2 copy.15
  11.1 1.5 all-to-all-done
  12.6 3.5 %all-to-all-start.1 = ((bf16[4,256,512]{2,1,0:T(8,128)(2,1)}), bf16[4,256,512]{2,1,0:T(8,128)(2,1)S(1)}, u32[]{:S(2)}, u32[]{:S(2)}) async-start(bf16[4,256,512]{2,1,0:T(8,128)(2,1)} %bitcast.18), calls=%async_computation.1 | async-start | bytes 2097152 | tf_op jit(solution)/shard_map/all_to_all | solution.py:165
  16.1 25.2 %all_gather.15 = bf16[256,512]{1,0:T(8,128)(2,1)S(1)} all-gather(bf16[64,512]{1,0:T(8,128)(2,1)S(1)} %bitcast.28), channel_id=1, replica_groups=mesh['zh'=4,'zl'=4,'yh'=2,'x'=4,'c'=2,'yl'=2] {'zh'}, dimensions={0}, use_global_device_ids=true | all-gather | bytes 327680 | tf_op jit(solution)/shard_map/all_gather | solution.py:160
  41.4 12.0 %all_gather.17 = bf16[512,512]{1,0:T(8,128)(2,1)S(1)} all-gather(bf16[128,512]{1,0:T(8,128)(2,1)S(1)} %get-tuple-element.2), channel_id=1, replica_groups=mesh['zh'=4,'zl'=4,'yh'=2,'x'=4,'c'=2,'yl'=2] {'zl'}, dimensions={0}, use_global_device_ids=true | all-gather | bytes 655360 | tf_op jit(solution)/shard_map/all_gather | solution.py:162
  53.3 13.2 %all_gather.16 = bf16[512,512]{1,0:T(8,128)(2,1)S(1)} all-gather(bf16[128,512]{1,0:T(8,128)(2,1)S(1)} %get-tuple-element.3), channel_id=1, replica_groups=mesh['zh'=4,'zl'=4,'yh'=2,'x'=4,'c'=2,'yl'=2] {'zl'}, dimensions={0}, use_global_device_ids=true | all-gather | bytes 655360 | tf_op jit(solution)/shard_map/all_gather | solution.py:161
  66.6 3.2 %shard_map.78 = bf16[1024,1024]{1,0:T(8,128)(2,1)} custom-call(bf16[4,2,2,2,16,512]{5,4,3,2,1,0:T(8,128)(2,1)S(1)} %bitcast.23, bf16[4,2,2,2,16,512]{5,4,3,2,1,0:T(8,128)(2,1)S(1)} %bitcast.22, bf16[1024,512]{1,0:T(8,128)(2,1)S(1)} %bitcast.21), custom_call_target="tpu_custom_call" | custom-call | tf_op jit(solution)/shard_map/pallas_call | solution.py:168
  69.8 18.1 %all-to-all-start.2 = ((bf16[32,32,1024]{2,1,0:T(8,128)(2,1)}), bf16[32,32,1024]{2,1,0:T(8,128)(2,1)S(1)}, u32[]{:S(2)}, u32[]{:S(2)}) async-start(bf16[32,32,1024]{2,1,0:T(8,128)(2,1)} %bitcast.13), calls=%async_computation.2 | async-start | bytes 4194304 | tf_op jit(solution)/shard_map/all_to_all | solution.py:182
  88.6 3.3 %collective-permute-start = (s32[1,65]{1,0:T(1,128)S(1)}, s32[1,65]{1,0:T(1,128)S(1)}, u32[]{:S(2)}, u32[]{:S(2)}) collective-permute-start(s32[1,65]{1,0:T(1,128)S(1)} %pad_add_fusion.1), channel_id=1, source_target_pairs={{0,1},{1,0},{2,3},{3,2},{4,5},{5,4},{6,7},{7,6},{8,9},{9,8},{10,11... | collective-permute-start | bytes 788 | tf_op jit(solution)/shard_map/ppermute | solution.py:146
  92.0 13.0 %collective-permute-done = s32[1,65]{1,0:T(1,128)S(1)} collective-permute-done((s32[1,65]{1,0:T(1,128)S(1)}, s32[1,65]{1,0:T(1,128)S(1)}, u32[]{:S(2)}, u32[]{:S(2)}) %collective-permute-start) | collective-permute-done | bytes 292 | tf_op jit(solution)/shard_map/ppermute | solution.py:146
  105.3 10.5 %all-to-all-done.2 = bf16[32,32,1024]{2,1,0:T(8,128)(2,1)S(1)} async-done(((bf16[32,32,1024]{2,1,0:T(8,128)(2,1)}), bf16[32,32,1024]{2,1,0:T(8,128)(2,1)S(1)}, u32[]{:S(2)}, u32[]{:S(2)}) %all-to-all-start.2) | async-done | bytes 2097184 | tf_op jit(solution)/shard_map/all_to_all | solution.py:182
  116.2 1.3 collective-permute-start.1
  117.5 15.3 %all_gather.18.left_ref = bf16[256,1024]{1,0:T(8,128)(2,1)S(1)} all-gather(bf16[32,1024]{1,0:T(8,128)(2,1)S(1)} %reduce_sum.12), channel_id=1, replica_groups=mesh['zh'=4,'zl'=4,'yh'=2,'x'=4,'c'=2,'yl'=2] {'x','c'}, dimensions={0}, use_global_device_ids=true | all-gather | bytes 589824 | tf_op jit(solution)/shard_map/all_gather | solution.py:189
  132.9 9.4 %all_gather.19.right_ref = bf16[128,1152]{1,0:T(8,128)(2,1)S(1)} all-gather(bf16[32,1152]{1,0:T(8,128)(2,1)S(1)} %pad_maximum_fusion), channel_id=1, replica_groups=mesh['zh'=4,'zl'=4,'yh'=2,'x'=4,'c'=2,'yl'=2] {'yh','yl'}, dimensions={0}, use_global_device_ids=true | all-gather | bytes 368640 | tf_op jit(solution)/shard_map/all_gather | solution.py:190
  142.3 2.5 %shard_map.79 = f32[16,56,128]{2,1,0:T(8,128)} custom-call(s32[2]{0:T(128)S(1)} %slice_reduce_fusion.lags_ref, s32[2]{0:T(128)S(1)} %pad_add_fusion.place_ref, s32[2,64]{1,0:T(2,128)S(1)} %slice.19.seg_ref, bf16[256,1024]{1,0:T(8,128)(2,1)S(1)} %all_gather.18.left_ref, bf16[128,1152]{1,0:T(8,128)(2,1)S(1)} %all_gather.19.right_ref), custom_call_target="tpu_custom_call" | custom-call | tf_op jit(solution)/shard_map/pallas_call | solution.py:194
  144.8 7.6 %all-to-all-start.3 = ((f32[16,56,128]{2,1,0:T(8,128)}), f32[16,56,128]{2,1,0:T(8,128)S(1)}, u32[]{:S(2)}, u32[]{:S(2)}) async-start(f32[16,56,128]{2,1,0:T(8,128)} %shard_map.79), calls=%async_computation.3 | async-start | bytes 917504 | tf_op jit(solution)/shard_map/all_to_all | solution.py:201
  152.6 18.8 %all-to-all-done.3.refs_0_ = f32[16,56,128]{2,1,0:T(8,128)S(1)} async-done(((f32[16,56,128]{2,1,0:T(8,128)}), f32[16,56,128]{2,1,0:T(8,128)S(1)}, u32[]{:S(2)}, u32[]{:S(2)}) %all-to-all-start.3) | async-done | bytes 458784 | tf_op jit(solution)/shard_map/all_to_all | solution.py:201
  171.6 15.2 %all_to_all.25.parts_ref = f32[8,8,128]{2,1,0:T(8,128)S(1)} all-to-all(f32[8,8,128]{2,1,0:T(8,128)S(1)} %shard_map.80), channel_id=1, replica_groups=mesh['zh'=4,'zl'=4,'yh'=2,'x'=4,'c'=2,'yl'=2] {'x','c'}, dimensions={0} | all-to-all | bytes 65536 | tf_op jit(solution)/shard_map/all_to_all | solution.py:210
  186.8 1.2 shard_map.81
  (21 shorter events, 1.2 us)
Async XLA Ops:
  0.6 0.8 copy-start
  1.5 0.8 copy-start.1
  3.1 9.5 %all-to-all-start = ((bf16[2,2,16,512]{3,2,1,0:T(8,128)(2,1)}), bf16[2,2,16,512]{3,2,1,0:T(8,128)(2,1)S(1)}, u32[]{:S(2)}, u32[]{:S(2)}) async-start(bf16[2,2,16,512]{3,2,1,0:T(8,128)(2,1)} %shard_map.77), calls=%async_computation | async-start | bytes 131072 | tf_op jit(solution)/shard_map/all_to_all | solution.py:158
  12.6 54.0 %all-to-all-start.1 = ((bf16[4,256,512]{2,1,0:T(8,128)(2,1)}), bf16[4,256,512]{2,1,0:T(8,128)(2,1)S(1)}, u32[]{:S(2)}, u32[]{:S(2)}) async-start(bf16[4,256,512]{2,1,0:T(8,128)(2,1)} %bitcast.18), calls=%async_computation.1 | async-start | bytes 2097152 | tf_op jit(solution)/shard_map/all_to_all | solution.py:165
  69.8 18.8 %copy-start.3 = (s32[1,64]{1,0:T(1,128)S(1)}, s32[1,64]{1,0:T(1,128)}, u32[]{:S(2)}) copy-start(s32[1,64]{1,0:T(1,128)} %param.10) | copy-start | bytes 772
  69.8 46.0 %all-to-all-start.2 = ((bf16[32,32,1024]{2,1,0:T(8,128)(2,1)}), bf16[32,32,1024]{2,1,0:T(8,128)(2,1)S(1)}, u32[]{:S(2)}, u32[]{:S(2)}) async-start(bf16[32,32,1024]{2,1,0:T(8,128)(2,1)} %bitcast.13), calls=%async_computation.2 | async-start | bytes 4194304 | tf_op jit(solution)/shard_map/all_to_all | solution.py:182
  88.6 16.4 %collective-permute-start = (s32[1,65]{1,0:T(1,128)S(1)}, s32[1,65]{1,0:T(1,128)S(1)}, u32[]{:S(2)}, u32[]{:S(2)}) collective-permute-start(s32[1,65]{1,0:T(1,128)S(1)} %pad_add_fusion.1), channel_id=1, source_target_pairs={{0,1},{1,0},{2,3},{3,2},{4,5},{5,4},{6,7},{7,6},{8,9},{9,8},{10,11... | collective-permute-start | bytes 788 | tf_op jit(solution)/shard_map/ppermute | solution.py:146
  116.1 36.4 %copy-start.2 = (f32[32]{0:T(128)S(1)}, f32[32]{0:T(128)}, u32[]{:S(2)}) copy-start(f32[32]{0:T(128)} %param.11) | copy-start | bytes 388
  116.2 16.6 %collective-permute-start.1 = (bf16[32,128]{1,0:T(8,128)(2,1)S(1)}, bf16[32,128]{1,0:T(8,128)(2,1)S(1)}, u32[]{:S(2)}, u32[]{:S(2)}) collective-permute-start(bf16[32,128]{1,0:T(8,128)(2,1)S(1)} %pad_maximum_fusion.1), channel_id=1, source_target_pairs={{32,0},{64,32},{96,64},{128,96},{160,128},{192,160},{224,192},{256... | collective-permute-start | bytes 24584 | tf_op jit(solution)/shard_map/ppermute | solution.py:188
  144.8 26.6 %all-to-all-start.3 = ((f32[16,56,128]{2,1,0:T(8,128)}), f32[16,56,128]{2,1,0:T(8,128)S(1)}, u32[]{:S(2)}, u32[]{:S(2)}) async-start(f32[16,56,128]{2,1,0:T(8,128)} %shard_map.79), calls=%async_computation.3 | async-start | bytes 917504 | tf_op jit(solution)/shard_map/all_to_all | solution.py:201

commit v2 on v1

v2 whole, which is shorter than its diff:
```python
import jax
import jax.numpy as jnp
import numpy as np
from jax import lax
from jax.experimental import pallas as pl
from jax.experimental.pallas import tpu as pltpu
from jax.sharding import Mesh, PartitionSpec as P

BF = jnp.bfloat16
F32 = jnp.float32
I32 = jnp.int32
HI = lax.Precision.HIGHEST
NT = (((1,), (1,)), ((), ()))
VMEM = pltpu.CompilerParams(vmem_limit_bytes=48 * 1024 * 1024)

Z = ("zh", "zl")
FE = ("x", "c")
MAIN = 896
CHUNKS = ("yh", "yl", "x", "c")


def one_hot(rows, cols, hit):
    r = lax.broadcasted_iota(I32, (rows, cols), 0)
    c = lax.broadcasted_iota(I32, (rows, cols), 1)
    return jnp.where(hit(r, c), 1.0, 0.0).astype(BF)


def pack_kernel(yl_ref, low_ref, high_ref, main_ref, rest_ref):
    off = pl.multiple_of(yl_ref[0] * 1024, 1024)
    src = one_hot(16, 16, lambda r, c: c == ((r >> 1) & 3) * 4 + (r >> 3) * 2 + (r & 1))
    for half, ref in enumerate((low_ref, high_ref)):
        rows = jnp.dot(src, ref[:, pl.ds(off, 1024)], preferred_element_type=F32).astype(BF)
        main_ref[half * 16 : half * 16 + 16, :] = rows[:, :MAIN]
        for z in range(16):
            rest_ref[z, half * 16 : half * 16 + 16, :] = rows[:, MAIN:]


def project_kernel(main_ref, rest_ref, frames_ref, out_ref):
    acc = lax.dot_general(main_ref[...], frames_ref[:, :MAIN], NT, preferred_element_type=F32)
    acc = acc + lax.dot_general(
        rest_ref[...], frames_ref[:, MAIN:], NT, preferred_element_type=F32
    )
    for yh in range(2):
        for yl in range(2):
            for half in range(2):
                for zh in range(4):
                    row = (zh * 4 + yh) * 32 + half * 16 + yl * 8
                    both = jnp.concatenate([acc[row : row + 8], acc[row + 64 : row + 72]], axis=0)
                    chunk = (yh * 2 + yl) * 8 + half * 4 + zh
                    out_ref[chunk * 16 : chunk * 16 + 16, :] = both.astype(BF)


def sum_kernel(parts_ref, basis_ref, head_ref):
    sums = []
    for yh in range(2):
        total = parts_ref[yh, 0, 0].astype(F32)
        for i in range(1, 16):
            total = total + parts_ref[yh, i // 8, i % 8].astype(F32)
        sums.append(total)
    basis = jnp.concatenate([sums[0][:8], sums[1][:8], sums[0][8:], sums[1][8:]], axis=0)
    basis_ref[...] = basis.astype(BF)
    lane = lax.broadcasted_iota(I32, (32, 128), 1)
    head = jnp.where(lane < 64, basis[:, :128], pltpu.roll(basis[:, 512:640], 64, 1))
    head_ref[...] = head.astype(BF)


def cov_kernel(lags_ref, place_ref, seg_ref, left_ref, right_ref, out_ref):
    z = place_ref[0]
    perm = one_hot(
        128,
        128,
        lambda r, c: c
        == ((r >> 5) & 1) * 64 + ((r >> 1) & 1) * 32 + (r >> 6) * 16 + ((r >> 2) & 7) * 2 + (r & 1),
    )
    right = jnp.dot(perm, right_ref[...], preferred_element_type=F32)
    halo = right[:, 1024:1152]
    tri = lax.broadcasted_iota(I32, (64, 64), 1) <= lax.broadcasted_iota(I32, (64, 64), 0)
    seg = seg_ref[...].astype(F32)
    keep, keep_end, lagged = [], [], []
    for rep in range(2):
        lag = lags_ref[rep]
        ends = jnp.sum(jnp.where(tri, seg[rep : rep + 1, :], 0.0), axis=1, keepdims=True)
        pos = lax.broadcasted_iota(I32, (1, 512), 1) + z * 512
        here = pos.astype(F32)
        ahead = (pos + lag).astype(F32)
        behind = (pos - lag).astype(F32)
        cut = jnp.where((ends > here) & (ends <= ahead), 1.0, 0.0)
        keep.append(1.0 - jnp.max(cut, axis=0, keepdims=True))
        cut_end = jnp.where((ends > behind) & (ends <= here), 1.0, 0.0)
        inside = jnp.where(behind >= 0.0, 1.0, 0.0)
        keep_end.append((1.0 - jnp.max(cut_end, axis=0, keepdims=True)) * inside)
        tail = halo if rep == 0 else pltpu.roll(halo, 64, 1)
        ext = jnp.concatenate([right[:, rep * 512 : (rep + 1) * 512], tail], axis=1)
        lagged.append(pltpu.roll(ext, 640 - lag, 1)[:, :512].astype(BF))
    keep = jnp.concatenate(keep, axis=1)
    keep_end = jnp.concatenate(keep_end, axis=1)
    lagged = jnp.concatenate(lagged, axis=1)
    now = right[:, :1024]
    now_bf = now.astype(BF)
    left = left_ref[...]
    left_start = left * keep.astype(BF)
    left_end = left * keep_end.astype(BF)
    for m, (lhs, rhs) in enumerate(
        ((left_start, now_bf), (left_start, lagged), (left_end, now_bf))
    ):
        block = lax.dot_general(lhs, rhs, NT, preferred_element_type=F32)
        for d in range(16):
            out_ref[d % 4, d // 4, m * 16 : (m + 1) * 16, :] = block[d * 16 : (d + 1) * 16, :]
    var = lax.dot_general(
        jnp.ones((8, 1024), F32), now * now * keep_end, NT, precision=HI, preferred_element_type=F32
    )
    for d in range(16):
        out_ref[d % 4, d // 4, 48:56, :] = var


def rows_kernel(parts_ref, out_ref):
    for zh in range(4):
        total = (parts_ref[0, zh] + parts_ref[1, zh]) + (parts_ref[2, zh] + parts_ref[3, zh])
        for f in range(8):
            for m in range(3):
                src = m * 16 + f * 2
                out_ref[zh, f, m * 2 : m * 2 + 2, :] = total[src : src + 2, :]
            out_ref[zh, f, 6:8, :] = total[48:50, :]


def final_kernel(scale, place_ref, parts_ref, ridge_ref, row_ref, cov_ref, score_ref):
    first = place_ref[1]
    ridge = ridge_ref[...]
    lane = lax.broadcasted_iota(I32, (2, 128), 1)
    row = lax.broadcasted_iota(I32, (2, 128), 0)
    diag = jnp.zeros((2, 1), F32)
    weighted = [jnp.zeros((32, 128), F32) for _ in range(2)]
    for f in range(8):
        total = (parts_ref[0, f] + parts_ref[1, f]) + (parts_ref[2, f] + parts_ref[3, f])
        total = total * scale
        for m in range(3):
            cov_ref[m, :, f * 128 : (f + 1) * 128] = total[m * 2 : m * 2 + 2, :]
        own = lane + f * 128 == first + row
        diag = diag + jnp.sum(jnp.where(own, total[0:2, :], 0.0), axis=1, keepdims=True)
        inverse = 1.0 / (total[6:7, :] + ridge)
        for e in range(2):
            cross = total[2 + e : 3 + e, :]
            weighted[e] = weighted[e] + (cross * cross) * inverse
    ones = jnp.ones((8, 128), F32)
    pad = jnp.zeros((96, 128), F32)
    score = [
        lax.dot_general(
            ones,
            jnp.concatenate([w, pad], axis=0),
            NT,
            precision=HI,
            preferred_element_type=F32,
        )[0:1, :32]
        for w in weighted
    ]
    for e in range(2):
        score_ref[e : e + 1, :] = score[e] / (diag[e : e + 1, :] + row_ref[...])


def local(frames, panel_low, panel_high, lags, seg_lengths, ridge):
    z = lax.axis_index(Z).astype(I32)
    yl = lax.axis_index("yl").astype(I32)
    own_first = ((z * 2 + lax.axis_index("yh")) * 8 + lax.axis_index(FE)) * 4 + yl * 2
    place = jnp.stack([z, own_first.astype(I32)])
    smem = pl.BlockSpec(memory_space=pltpu.SMEM)
    vmem = pl.BlockSpec(memory_space=pltpu.VMEM)

    mine = jnp.concatenate([lags.reshape(1, 1), seg_lengths], axis=1)
    other = lax.ppermute(mine, "yl", [(0, 1), (1, 0)])
    both = jnp.where(
        yl == 0, jnp.concatenate([mine, other], axis=0), jnp.concatenate([other, mine], axis=0)
    )

    low, high = frames[:, :, :1024], frames[:, :, 1024:]
    halves = jnp.concatenate([low, low, high, high], axis=0)
    frames_h = lax.all_to_all(halves, ("yl", "yh"), split_axis=0, concat_axis=0, tiled=True)

    main, rest = pl.pallas_call(
        pack_kernel,
        out_shape=(
            jax.ShapeDtypeStruct((32, MAIN), BF),
            jax.ShapeDtypeStruct((16, 32, 1024 - MAIN), BF),
        ),
        in_specs=[smem, vmem, vmem],
        out_specs=(vmem, vmem),
        compiler_params=VMEM,
    )(yl[None], panel_low.T, panel_high.T)
    main, rest, both = lax.optimization_barrier((main, rest, both))
    panel_rest = lax.all_to_all(rest, Z, split_axis=0, concat_axis=0, tiled=True)
    panel_main = lax.all_gather(main, Z, axis=0, tiled=True)

    partial = pl.pallas_call(
        project_kernel,
        grid=(4,),
        out_shape=jax.ShapeDtypeStruct((512, 1024), BF),
        in_specs=[
            pl.BlockSpec((512, MAIN), lambda i: (0, 0)),
            pl.BlockSpec((512, 1024 - MAIN), lambda i: (0, 0)),
            pl.BlockSpec((256, 1024), lambda i: (i, 0)),
        ],
        out_specs=pl.BlockSpec((512, 256), lambda i: (0, i)),
        compiler_params=VMEM,
    )(panel_main, panel_rest.reshape(512, 1024 - MAIN), frames_h.reshape(1024, 1024))

    parts = lax.all_to_all(
        partial.reshape(32, 16, 1024), CHUNKS, split_axis=0, concat_axis=0, tiled=True
    )
    basis, head = pl.pallas_call(
        sum_kernel,
        out_shape=(
            jax.ShapeDtypeStruct((32, 1024), BF),
            jax.ShapeDtypeStruct((32, 128), BF),
        ),
        in_specs=[vmem],
        out_specs=(vmem, vmem),
        compiler_params=VMEM,
    )(parts.reshape(2, 2, 8, 16, 1024))

    halo = lax.ppermute(head, Z, [(i + 1, i) for i in range(15)])
    left = lax.all_gather(basis, FE, axis=0, tiled=True)
    right = lax.all_gather(
        jnp.concatenate([basis, halo], axis=1), ("yh", "yl"), axis=0, tiled=True
    )

    terms = pl.pallas_call(
        cov_kernel,
        out_shape=jax.ShapeDtypeStruct((4, 4, 56, 128), F32),
        in_specs=[smem, smem, vmem, vmem, vmem],
        out_specs=vmem,
        compiler_params=VMEM,
    )(both[:, 0], place, both[:, 1:], left, right)
    by_zl = lax.all_to_all(terms, "zl", split_axis=0, concat_axis=0, tiled=True)
    rows = pl.pallas_call(
        rows_kernel,
        out_shape=jax.ShapeDtypeStruct((4, 8, 8, 128), F32),
        in_specs=[vmem],
        out_specs=vmem,
        compiler_params=VMEM,
    )(by_zl)
    by_row = lax.all_to_all(
        rows.reshape(32, 8, 128), ("zh", "x", "c"), split_axis=0, concat_axis=0, tiled=True
    )
    return pl.pallas_call(
        lambda *refs: final_kernel(1.0 / 16384.0, *refs),
        out_shape=(
            jax.ShapeDtypeStruct((3, 2, 1024), F32),
            jax.ShapeDtypeStruct((2, 32), F32),
        ),
        in_specs=[smem, vmem, vmem, vmem],
        out_specs=(vmem, vmem),
        compiler_params=VMEM,
    )(place, by_row.reshape(4, 8, 8, 128), ridge[:, None], ridge[None, :])


def solution(mesh):
    fine = Mesh(
        np.asarray(mesh.devices).reshape(4, 4, 2, 4, 2, 2), ("zh", "zl", "yh", "x", "c", "yl")
    )
    tm = ("zh", "zl", "yh")
    in_specs = (P("yl", tm, FE), P(FE, tm), P(FE, tm), P("yl"), P("yl", None), P())
    rows = tm + FE + ("yl",)
    out_specs = (P(None, rows, None), P(rows, None))
    return jax.shard_map(local, mesh=fine, in_specs=in_specs, out_specs=out_specs, check_vma=False)
```

time: 189 us -> 174 us (0.921)
  blocking collectives: 90.4 us -> 64.5 us
  starting transfers between devices: 38.9 us -> 51.2 us
  other arithmetic: 0.7 us -> 3.22 us
    all_gather x3 -> x1, blocking collectives: 50.5 us -> 28.1 us  [local(): panel_main = lax.all_gather(main, Z, axis=0, tiled=True)]
    ppermute x1, waiting for transfers between devices: 13 us -> 0.01 us  [local(): other = lax.ppermute(mine, 'yl', [(0, 1), (1, 0)])]
    all_to_all x4, starting transfers between devices: 34.3 us -> 45.9 us  [the longest x1 16.9 us: local(): lax.all_to_all(partial.reshape(32, 16, 1024), CHUNKS, split_axis=0, conca...]
    all_to_all x4, waiting for transfers between devices: 30.7 us -> 42.2 us  [the longest x1 16.9 us: local(): lax.all_to_all(partial.reshape(32, 16, 1024), CHUNKS, split_axis=0, conca...]
    another operation x2 -> x0, local copies, waits for them, and re-layouts: 3.01 us -> none  [local(): quarters = frames[0].reshape(256, 4, 512).transpose(1, 0, 2)]
    all_gather x1, blocking collectives: 15.3 us -> 13.3 us  [local(): left = lax.all_gather(basis, FE, axis=0, tiled=True)]
    pallas_call x4 -> x5, Pallas kernels: 4.71 us -> 4.75 us  [the longest x1 1.75 us: local(): pl.pallas_call(cov_kernel, out_shape=jax.ShapeDtypeStruct((4, 4, 56, 128)...]
  transfers between devices with their start and end apart: 6 -> 6, of which waited for: 4 -> 3; matrix products, arithmetic and copies ran while one was open for 2% -> 2% of each run, Pallas kernels for 0% -> 0%
where the time goes in v2:
time: 174 us
  blocking collectives  64.5 us (37%)
  starting transfers between devices  51.2 us (29%)
  waiting for transfers between devices  42.2 us (24%)
  Pallas kernels  7.75 us (4%)
  other arithmetic  3.22 us (2%)
  local copies, waits for them, and re-layouts  3.22 us (2%)
    all_gather x1, blocking collectives, local(): panel_main = lax.all_gather(main, Z, axis=0, tiled=True)  28.1 us
    all_to_all x1, starting transfers between devices, local(): lax.all_to_all(partial.reshape(32, 16, 1024), CHUNKS, split_axis=0, conca...  16.9 us
    all_to_all x1, waiting for transfers between devices, local(): lax.all_to_all(partial.reshape(32, 16, 1024), CHUNKS, split_axis=0, conca...  16.9 us
    all_to_all x1, waiting for transfers between devices, local(): lax.all_to_all(rows.reshape(32, 8, 128), ('zh', 'x', 'c'), split_axis=0,...  16.2 us
    all_to_all x1, starting transfers between devices, local(): lax.all_to_all(rest, Z, split_axis=0, concat_axis=0, tiled=True)  14.9 us
    all_to_all x1, blocking collectives, local(): by_zl = lax.all_to_all(terms, 'zl', split_axis=0, concat_axis=0, tiled=True)  13.7 us
    all_gather x1, blocking collectives, local(): left = lax.all_gather(basis, FE, axis=0, tiled=True)  13.3 us
    all_to_all x1, starting transfers between devices, local(): lax.all_to_all(rows.reshape(32, 8, 128), ('zh', 'x', 'c'), split_axis=0,...  10.2 us
  transfers between devices with their start and end apart: 6, of which 3 were waited for; matrix products, arithmetic and copies ran while one was open for 2% of the time, Pallas kernels for 0%

profile of v2, /device:TPU:1, one launch (start us, length us, event | category | flops | bytes accessed | tf_op | source)
XLA Modules:
  0.0 173.5 jit_solution(11879267064499367036)
XLA Ops:
  1.3 0.7 pad_add_fusion.1
  2.0 4.0 %collective-permute-start = (s32[1,65]{1,0:T(1,128)S(1)}, s32[1,65]{1,0:T(1,128)S(1)}, u32[]{:S(2)}, u32[]{:S(2)}) collective-permute-start(s32[1,65]{1,0:T(1,128)S(1)} %pad_add_fusion.1), channel_id=1, source_target_pairs={{0,1},{1,0},{2,3},{3,2},{4,5},{5,4},{6,7},{7,6},{8,9},{9,8},{10,11... | collective-permute-start | bytes 788 | tf_op jit(solution)/shard_map/ppermute | solution.py:169
  6.1 0.8 copy-done
  6.9 0.8 copy-done.1
  7.7 0.8 shard_map.77
  8.5 0.8 add_select_fusion
  9.3 14.9 %all-to-all-start = ((bf16[16,32,128]{2,1,0:T(8,128)(2,1)}), bf16[16,32,128]{2,1,0:T(8,128)(2,1)S(1)}, u32[]{:S(2)}, u32[]{:S(2)}) async-start(bf16[16,32,128]{2,1,0:T(8,128)(2,1)} %get-tuple-element.13), calls=%async_computation | async-start | bytes 262144 | tf_op jit(solution)/shard_map/all_to_all | solution.py:189
  24.3 1.3 fusion
  25.5 1.6 pad_maximum_fusion
  27.1 9.1 %all-to-all-done = bf16[16,32,128]{2,1,0:T(8,128)(2,1)S(1)} async-done(((bf16[16,32,128]{2,1,0:T(8,128)(2,1)}), bf16[16,32,128]{2,1,0:T(8,128)(2,1)S(1)}, u32[]{:S(2)}, u32[]{:S(2)}) %all-to-all-start) | async-done | bytes 131104 | tf_op jit(solution)/shard_map/all_to_all | solution.py:189
  36.2 3.9 %all-to-all-start.1 = ((bf16[4,256,1024]{2,1,0:T(8,128)(2,1)}), bf16[4,256,1024]{2,1,0:T(8,128)(2,1)S(1)}, u32[]{:S(2)}, u32[]{:S(2)}) async-start(bf16[4,256,1024]{2,1,0:T(8,128)(2,1)} %pad_maximum_fusion), calls=%async_computation.1 | async-start | bytes 4194304 | tf_op jit(solution)/shard_map/all_to_all | solution.py:176
  40.1 28.1 %all_gather.9.main_ref = bf16[512,896]{1,0:T(8,128)(2,1)S(1)} all-gather(bf16[32,896]{1,0:T(8,128)(2,1)S(1)} %get-tuple-element.12), channel_id=1, replica_groups=mesh['zh'=4,'zl'=4,'yh'=2,'x'=4,'c'=2,'yl'=2] {'zh','zl'}, dimensions={0}, use_global_device_ids=true | all-gather | bytes 974848 | tf_op jit(solution)/shard_map/all_gather | solution.py:190
  68.2 3.0 %shard_map.78 = bf16[512,1024]{1,0:T(8,128)(2,1)} custom-call(bf16[512,896]{1,0:T(8,128)(2,1)S(1)} %all_gather.9.main_ref, bf16[512,128]{1,0:T(8,128)(2,1)S(1)} %bitcast.18, bf16[1024,1024]{1,0:T(8,128)(2,1)S(1)} %bitcast.16), custom_call_target="tpu_custom_call" | custom-call | tf_op jit(solution)/shard_map/pallas_call | solution.py:192
  71.2 16.9 %all-to-all-start.2 = ((bf16[32,16,1024]{2,1,0:T(8,128)(2,1)}), bf16[32,16,1024]{2,1,0:T(8,128)(2,1)S(1)}, u32[]{:S(2)}, u32[]{:S(2)}) async-start(bf16[32,16,1024]{2,1,0:T(8,128)(2,1)} %bitcast.8), calls=%async_computation.2 | async-start | bytes 2097152 | tf_op jit(solution)/shard_map/all_to_all | solution.py:205
  88.4 16.9 %all-to-all-done.2 = bf16[32,16,1024]{2,1,0:T(8,128)(2,1)S(1)} async-done(((bf16[32,16,1024]{2,1,0:T(8,128)(2,1)}), bf16[32,16,1024]{2,1,0:T(8,128)(2,1)S(1)}, u32[]{:S(2)}, u32[]{:S(2)}) %all-to-all-start.2) | async-done | bytes 1048608 | tf_op jit(solution)/shard_map/all_to_all | solution.py:205
  105.5 1.3 collective-permute-start.1
  106.8 13.3 %all_gather.10.left_ref = bf16[256,1024]{1,0:T(8,128)(2,1)S(1)} all-gather(bf16[32,1024]{1,0:T(8,128)(2,1)S(1)} %get-tuple-element.14), channel_id=1, replica_groups=mesh['zh'=4,'zl'=4,'yh'=2,'x'=4,'c'=2,'yl'=2] {'x','c'}, dimensions={0}, use_global_device_ids=true | all-gather | bytes 589824 | tf_op jit(solution)/shard_map/all_gather | solution.py:220
  120.2 9.4 %all_gather.11.right_ref = bf16[128,1152]{1,0:T(8,128)(2,1)S(1)} all-gather(bf16[32,1152]{1,0:T(8,128)(2,1)S(1)} %pad_maximum_fusion.1), channel_id=1, replica_groups=mesh['zh'=4,'zl'=4,'yh'=2,'x'=4,'c'=2,'yl'=2] {'yh','yl'}, dimensions={0}, use_global_device_ids=true | all-gather | bytes 368640 | tf_op jit(solution)/shard_map/all_gather | solution.py:221
  129.6 1.7 %shard_map.80 = f32[4,4,56,128]{3,2,1,0:T(8,128)S(1)} custom-call(s32[2]{0:T(128)S(1)} %slice_reduce_fusion.lags_ref, s32[2]{0:T(128)S(1)} %pad_add_fusion.place_ref.refs_0_, s32[2,64]{1,0:T(2,128)S(1)} %slice.13.seg_ref, bf16[256,1024]{1,0:T(8,128)(2,1)S(1)} %all_gather.10.left_ref, bf16[128,1152]{1,0:T(8,128)(2,1)S(1)} %all_gather.11.right_ref), custom_call_target="tpu_custom_call" | custom-call | tf_op jit(solution)/shard_map/pallas_call | solution.py:225
  131.4 13.7 %all_to_all.25.parts_ref = f32[4,4,56,128]{3,2,1,0:T(8,128)S(1)} all-to-all(f32[4,4,56,128]{3,2,1,0:T(8,128)S(1)} %shard_map.80), channel_id=1, replica_groups=mesh['zh'=4,'zl'=4,'yh'=2,'x'=4,'c'=2,'yl'=2] {'zl'}, dimensions={0} | all-to-all | bytes 917504 | tf_op jit(solution)/shard_map/all_to_all | solution.py:232
  145.0 0.7 shard_map.81
  145.7 10.2 %all-to-all-start.4 = ((f32[32,8,128]{2,1,0:T(8,128)}), f32[32,8,128]{2,1,0:T(8,128)S(1)}, u32[]{:S(2)}, u32[]{:S(2)}) async-start(f32[32,8,128]{2,1,0:T(8,128)} %bitcast.10), calls=%async_computation.4 | async-start | bytes 262144 | tf_op jit(solution)/shard_map/all_to_all | solution.py:240
  156.0 16.2 %all-to-all-done.4 = f32[32,8,128]{2,1,0:T(8,128)S(1)} async-done(((f32[32,8,128]{2,1,0:T(8,128)}), f32[32,8,128]{2,1,0:T(8,128)S(1)}, u32[]{:S(2)}, u32[]{:S(2)}) %all-to-all-start.4) | async-done | bytes 131104 | tf_op jit(solution)/shard_map/all_to_all | solution.py:240
  172.1 1.4 shard_map.82
  (13 shorter events, 0.5 us)
Async XLA Ops:
  2.0 6.5 %collective-permute-start = (s32[1,65]{1,0:T(1,128)S(1)}, s32[1,65]{1,0:T(1,128)S(1)}, u32[]{:S(2)}, u32[]{:S(2)}) collective-permute-start(s32[1,65]{1,0:T(1,128)S(1)} %pad_add_fusion.1), channel_id=1, source_target_pairs={{0,1},{1,0},{2,3},{3,2},{4,5},{5,4},{6,7},{7,6},{8,9},{9,8},{10,11... | collective-permute-start | bytes 788 | tf_op jit(solution)/shard_map/ppermute | solution.py:169
  6.0 0.8 copy-start
  6.9 0.8 copy-start.1
  9.3 26.9 %all-to-all-start = ((bf16[16,32,128]{2,1,0:T(8,128)(2,1)}), bf16[16,32,128]{2,1,0:T(8,128)(2,1)S(1)}, u32[]{:S(2)}, u32[]{:S(2)}) async-start(bf16[16,32,128]{2,1,0:T(8,128)(2,1)} %get-tuple-element.13), calls=%async_computation | async-start | bytes 262144 | tf_op jit(solution)/shard_map/all_to_all | solution.py:189
  36.2 31.9 %all-to-all-start.1 = ((bf16[4,256,1024]{2,1,0:T(8,128)(2,1)}), bf16[4,256,1024]{2,1,0:T(8,128)(2,1)S(1)}, u32[]{:S(2)}, u32[]{:S(2)}) async-start(bf16[4,256,1024]{2,1,0:T(8,128)(2,1)} %pad_maximum_fusion), calls=%async_computation.1 | async-start | bytes 4194304 | tf_op jit(solution)/shard_map/all_to_all | solution.py:176
  71.2 34.1 %all-to-all-start.2 = ((bf16[32,16,1024]{2,1,0:T(8,128)(2,1)}), bf16[32,16,1024]{2,1,0:T(8,128)(2,1)S(1)}, u32[]{:S(2)}, u32[]{:S(2)}) async-start(bf16[32,16,1024]{2,1,0:T(8,128)(2,1)} %bitcast.8), calls=%async_computation.2 | async-start | bytes 2097152 | tf_op jit(solution)/shard_map/all_to_all | solution.py:205
  105.5 50.4 %copy-start.2 = (f32[32]{0:T(128)S(1)}, f32[32]{0:T(128)}, u32[]{:S(2)}) copy-start(f32[32]{0:T(128)} %param.11) | copy-start | bytes 388
  105.5 14.6 %collective-permute-start.1 = (bf16[32,128]{1,0:T(8,128)(2,1)S(1)}, bf16[32,128]{1,0:T(8,128)(2,1)S(1)}, u32[]{:S(2)}, u32[]{:S(2)}) collective-permute-start(bf16[32,128]{1,0:T(8,128)(2,1)S(1)} %get-tuple-element.15), channel_id=1, source_target_pairs={{32,0},{64,32},{96,64},{128,96},{160,128},{192,160},{224,192},{256... | collective-permute-start | bytes 24584 | tf_op jit(solution)/shard_map/ppermute | solution.py:219
  145.7 26.4 %all-to-all-start.4 = ((f32[32,8,128]{2,1,0:T(8,128)}), f32[32,8,128]{2,1,0:T(8,128)S(1)}, u32[]{:S(2)}, u32[]{:S(2)}) async-start(f32[32,8,128]{2,1,0:T(8,128)} %bitcast.10), calls=%async_computation.4 | async-start | bytes 262144 | tf_op jit(solution)/shard_map/all_to_all | solution.py:240

commit v3 on v2

v3 whole, which is shorter than its diff:
```python
import jax
import jax.numpy as jnp
import numpy as np
from jax import lax
from jax.experimental import pallas as pl
from jax.experimental.pallas import tpu as pltpu
from jax.sharding import Mesh, PartitionSpec as P

BF = jnp.bfloat16
F32 = jnp.float32
I32 = jnp.int32
HI = lax.Precision.HIGHEST
NT = (((1,), (1,)), ((), ()))
VMEM = pltpu.CompilerParams(vmem_limit_bytes=48 * 1024 * 1024)

Z = ("z3", "z2", "z1", "z0")
Z8 = ("z3", "z2", "z1")
FE = ("x", "c")


def one_hot(rows, cols, hit):
    r = lax.broadcasted_iota(I32, (rows, cols), 0)
    c = lax.broadcasted_iota(I32, (rows, cols), 1)
    return jnp.where(hit(r, c), 1.0, 0.0).astype(BF)


def pack_kernel(yl_ref, low_ref, high_ref, out_ref):
    off = pl.multiple_of(yl_ref[0] * 1024, 1024)
    src = one_hot(16, 16, lambda r, c: c == ((r >> 1) & 3) * 4 + (r >> 3) * 2 + (r & 1))
    for half, ref in enumerate((low_ref, high_ref)):
        rows = jnp.dot(src, ref[:, pl.ds(off, 1024)], preferred_element_type=F32)
        out_ref[half * 16 : half * 16 + 16, :] = rows.astype(BF)


def halves_kernel(frames_ref, out_ref):
    for half in range(2):
        rows = frames_ref[0, :, half * 1024 : (half + 1) * 1024]
        out_ref[half * 2] = rows
        out_ref[half * 2 + 1] = rows


def project_kernel(place_ref, own_ref, other_ref, frames_ref, keep_ref, send_ref):
    z0 = place_ref[0] & 1
    c = place_ref[2]
    frames = frames_ref[...]
    own = lax.dot_general(own_ref[...], frames, NT, preferred_element_type=F32)
    other = lax.dot_general(other_ref[...], frames, NT, preferred_element_type=F32)

    def store(even, odd, keep_ref, send_ref, own_c):
        for yh, acc in enumerate((even, odd)):
            for yl in range(2):
                for half in range(2):
                    for zh in range(4):
                        row = zh * 64 + half * 16 + yl * 8
                        both = jnp.concatenate(
                            [acc[row : row + 8], acc[row + 32 : row + 40]], axis=0
                        )
                        chunk = (yh * 2 + yl) * 4 + half * 2 + (zh >> 1)
                        ref = keep_ref if (zh & 1) == own_c else send_ref
                        ref[chunk * 16 : chunk * 16 + 16, :] = both.astype(BF)

    for own_z0 in range(2):
        for own_c in range(2):

            @pl.when((z0 == own_z0) & (c == own_c))
            def _(own_z0=own_z0, own_c=own_c):
                pair = (own, other) if own_z0 == 0 else (other, own)
                store(*pair, keep_ref, send_ref, own_c)


def sum_kernel(parts_ref, basis_ref, tail_ref):
    sums = []
    for yh in range(2):
        total = parts_ref[yh, 0, 0].astype(F32)
        for i in range(1, 8):
            total = total + parts_ref[yh, i // 4, i % 4].astype(F32)
        sums.append(total)
    basis = jnp.concatenate([sums[0][:8], sums[1][:8], sums[0][8:], sums[1][8:]], axis=0)
    basis_ref[...] = basis.astype(BF)
    lane = lax.broadcasted_iota(I32, (32, 128), 1)
    tail = jnp.where(lane < 64, pltpu.roll(basis[:, 384:512], 64, 1), basis[:, 896:])
    tail_ref[...] = tail.astype(BF)


def cov_kernel(lags_ref, place_ref, seg_ref, left_ref, right_ref, out_ref):
    z = place_ref[0]
    perm = one_hot(
        128,
        128,
        lambda r, c: c
        == ((r >> 5) & 1) * 64 + ((r >> 1) & 1) * 32 + (r >> 6) * 16 + ((r >> 2) & 7) * 2 + (r & 1),
    )
    now = jnp.dot(perm, right_ref[...], preferred_element_type=F32)
    now_bf = now.astype(BF)
    tri = lax.broadcasted_iota(I32, (64, 64), 1) <= lax.broadcasted_iota(I32, (64, 64), 0)
    seg = seg_ref[...].astype(F32)
    tails = left_ref[:, 1024:].astype(F32)
    keep, keep_end, lagged = [], [], []
    for rep in range(2):
        lag = lags_ref[rep]
        ends = jnp.sum(jnp.where(tri, seg[rep : rep + 1, :], 0.0), axis=1, keepdims=True)
        pos = lax.broadcasted_iota(I32, (1, 512), 1) + z * 512
        here = pos.astype(F32)
        ahead = (pos + lag).astype(F32)
        behind = (pos - lag).astype(F32)
        cut = jnp.where((ends > here) & (ends <= ahead), 1.0, 0.0)
        keep.append(1.0 - jnp.max(cut, axis=0, keepdims=True))
        cut_end = jnp.where((ends > behind) & (ends <= here), 1.0, 0.0)
        inside = jnp.where(behind >= 0.0, 1.0, 0.0)
        keep_end.append((1.0 - jnp.max(cut_end, axis=0, keepdims=True)) * inside)
        tail = tails if rep == 1 else pltpu.roll(tails, 64, 1)
        block = left_ref[:, rep * 512 : (rep + 1) * 512].astype(F32)
        ext = jnp.concatenate([tail, block], axis=1)
        lagged.append(pltpu.roll(ext, lag + 512, 1)[:, :512].astype(BF))
    keep = jnp.concatenate(keep, axis=1)
    keep_end = jnp.concatenate(keep_end, axis=1)
    lagged = jnp.concatenate(lagged, axis=1)
    left = left_ref[:, :1024]
    start_bf, end_bf = keep.astype(BF), keep_end.astype(BF)
    for m, lhs in enumerate((left * start_bf, lagged * end_bf, left * end_bf)):
        block = lax.dot_general(lhs, now_bf, NT, preferred_element_type=F32)
        for d in range(16):
            out_ref[d % 2, d // 2, m * 16 : (m + 1) * 16, :] = block[d * 16 : (d + 1) * 16, :]
    var = lax.dot_general(
        jnp.ones((8, 1024), F32), now * now * keep_end, NT, precision=HI, preferred_element_type=F32
    )
    for d in range(16):
        out_ref[d % 2, d // 2, 48:56, :] = var


def pair_kernel(parts_ref, out_ref):
    out_ref[...] = parts_ref[0] + parts_ref[1]


def rows_kernel(parts_ref, out_ref):
    total = parts_ref[0]
    for d in range(1, 8):
        total = total + parts_ref[d]
    for f in range(8):
        for m in range(3):
            src = m * 16 + f * 2
            out_ref[f, m * 2 : m * 2 + 2, :] = total[src : src + 2, :]
        out_ref[f, 6:8, :] = total[48:50, :]


def final_kernel(scale, place_ref, parts_ref, ridge_ref, row_ref, cov_ref, score_ref):
    first = place_ref[1]
    ridge = ridge_ref[...]
    lane = lax.broadcasted_iota(I32, (2, 128), 1)
    row = lax.broadcasted_iota(I32, (2, 128), 0)
    diag = jnp.zeros((2, 1), F32)
    weighted = [jnp.zeros((32, 128), F32) for _ in range(2)]
    for f in range(8):
        total = parts_ref[f] * scale
        for m in range(3):
            cov_ref[m, :, f * 128 : (f + 1) * 128] = total[m * 2 : m * 2 + 2, :]
        own = lane + f * 128 == first + row
        diag = diag + jnp.sum(jnp.where(own, total[0:2, :], 0.0), axis=1, keepdims=True)
        inverse = 1.0 / (total[6:7, :] + ridge)
        for e in range(2):
            cross = total[2 + e : 3 + e, :]
            weighted[e] = weighted[e] + (cross * cross) * inverse
    ones = jnp.ones((8, 128), F32)
    pad = jnp.zeros((96, 128), F32)
    score = [
        lax.dot_general(
            ones,
            jnp.concatenate([w, pad], axis=0),
            NT,
            precision=HI,
            preferred_element_type=F32,
        )[0:1, :32]
        for w in weighted
    ]
    for e in range(2):
        score_ref[e : e + 1, :] = score[e] / (diag[e : e + 1, :] + row_ref[...])


def call(kernel, out, *args, smem=0, **kw):
    specs = [pl.BlockSpec(memory_space=pltpu.SMEM)] * smem
    specs += [pl.BlockSpec(memory_space=pltpu.VMEM)] * (len(args) - smem)
    shapes = [jax.ShapeDtypeStruct(*o) for o in out]
    outs = [pl.BlockSpec(memory_space=pltpu.VMEM)] * len(out)
    got = pl.pallas_call(
        kernel, out_shape=shapes, in_specs=specs, out_specs=outs, compiler_params=VMEM
    )(*args)
    return got[0] if len(out) == 1 else got


def all_to_all(x, axes):
    return lax.all_to_all(x, axes, split_axis=0, concat_axis=0, tiled=True)


def local(frames, panel_low, panel_high, lags, seg_lengths, ridge):
    z = lax.axis_index(Z).astype(I32)
    yl = lax.axis_index("yl").astype(I32)
    c = lax.axis_index("c").astype(I32)
    own_first = ((z * 2 + lax.axis_index("yh")) * 8 + lax.axis_index(FE)) * 4 + yl * 2
    place = jnp.stack([z, own_first.astype(I32), c])

    mine = jnp.concatenate([lags.reshape(1, 1), seg_lengths], axis=1)
    other = lax.ppermute(mine, "yl", [(0, 1), (1, 0)])

    halves = pl.pallas_call(
        halves_kernel,
        grid=(4,),
        out_shape=jax.ShapeDtypeStruct((4, 256, 1024), BF),
        in_specs=[pl.BlockSpec((1, 64, 2048), lambda i: (0, i, 0))],
        out_specs=pl.BlockSpec((4, 64, 1024), lambda i: (0, i, 0)),
        compiler_params=VMEM,
    )(frames)
    frames_h = all_to_all(halves, ("yl", "yh")).reshape(1024, 1024)

    packed = call(
        pack_kernel, [((32, 1024), BF)], yl[None], panel_low.T, panel_high.T, smem=1
    )
    panel_own = lax.all_gather(packed, Z8, axis=0, tiled=True)
    panel_other = lax.ppermute(panel_own, "z0", [(0, 1), (1, 0)])
    panel_other, other = lax.optimization_barrier((panel_other, other))
    both = jnp.where(
        yl == 0, jnp.concatenate([mine, other], axis=0), jnp.concatenate([other, mine], axis=0)
    )

    whole = pl.BlockSpec((256, 1024), lambda i: (0, 0))
    column = pl.BlockSpec((256, 256), lambda i: (0, i))
    keep, send = pl.pallas_call(
        project_kernel,
        grid=(4,),
        out_shape=[jax.ShapeDtypeStruct((256, 1024), BF)] * 2,
        in_specs=[
            pl.BlockSpec(memory_space=pltpu.SMEM),
            whole,
            whole,
            pl.BlockSpec((256, 1024), lambda i: (i, 0)),
        ],
        out_specs=[column, column],
        compiler_params=VMEM,
    )(place, panel_own, panel_other, frames_h)
    got = lax.ppermute(send, "c", [(0, 1), (1, 0)])
    pairs = (keep.astype(F32) + got.astype(F32)).astype(BF)
    parts = all_to_all(pairs.reshape(16, 16, 1024), ("yh", "yl", "x"))
    basis, tail = call(
        sum_kernel, [((32, 1024), BF), ((32, 128), BF)], parts.reshape(2, 2, 4, 16, 1024)
    )

    before = lax.ppermute(tail, Z, [(i, i + 1) for i in range(15)])
    right = all_to_all(jnp.broadcast_to(basis[None], (4, 32, 1024)), ("yh", "yl"))
    left = lax.all_gather(jnp.concatenate([basis, before], axis=1), FE, axis=0, tiled=True)

    terms = call(
        cov_kernel,
        [((2, 8, 56, 128), F32)],
        both[:, 0],
        place,
        both[:, 1:],
        left,
        right.reshape(128, 1024),
        smem=2,
    )
    pair = call(pair_kernel, [((8, 56, 128), F32)], all_to_all(terms, "z0"))
    rows = call(rows_kernel, [((8, 8, 128), F32)], all_to_all(pair, Z8))
    by_row = all_to_all(rows, FE)
    return call(
        lambda *refs: final_kernel(1.0 / 16384.0, *refs),
        [((3, 2, 1024), F32), ((2, 32), F32)],
        place,
        by_row,
        ridge[:, None],
        ridge[None, :],
        smem=1,
    )


def solution(mesh):
    fine = Mesh(
        np.asarray(mesh.devices).reshape(2, 2, 2, 2, 2, 4, 2, 2),
        ("z3", "z2", "z1", "z0", "yh", "x", "c", "yl"),
    )
    tm = Z + ("yh",)
    in_specs = (P("yl", tm, FE), P(FE, tm), P(FE, tm), P("yl"), P("yl", None), P())
    rows = tm + FE + ("yl",)
    out_specs = (P(None, rows, None), P(rows, None))
    return jax.shard_map(local, mesh=fine, in_specs=in_specs, out_specs=out_specs, check_vma=False)
```

time: 174 us -> 155 us (0.89)
  waiting for transfers between devices: 42.2 us -> 20.1 us
  blocking collectives: 64.5 us -> 79 us
  starting transfers between devices: 51.2 us -> 42.1 us
  other arithmetic: 3.22 us -> 1.22 us
    all_to_all x4, waiting for transfers between devices: 42.2 us -> 15.3 us  [all_to_all(): return lax.all_to_all(x, axes, split_axis=0, concat_axis=0, tiled=True)]
    all_to_all x4, starting transfers between devices: 45.9 us -> 24.4 us  [all_to_all(): return lax.all_to_all(x, axes, split_axis=0, concat_axis=0, tiled=True)]
    all_to_all x1 -> x2, blocking collectives: 13.7 us -> 31.8 us  [all_to_all(): return lax.all_to_all(x, axes, split_axis=0, concat_axis=0, tiled=True)]
    ppermute x1 -> x3, starting transfers between devices: 1.29 us -> 14.9 us  [the longest x1 8.63 us: local(): got = lax.ppermute(send, 'c', [(0, 1), (1, 0)])]
    all_gather x3 -> x2, blocking collectives: 50.8 us -> 47.2 us  [the longest x1 32.1 us: local(): panel_own = lax.all_gather(packed, Z8, axis=0, tiled=True)]
    ppermute x1 -> x3, waiting for transfers between devices: 0.01 us -> 3.48 us  [the longest x1 1.96 us: local(): panel_other = lax.ppermute(panel_own, 'z0', [(0, 1), (1, 0)])]
    pallas_call x6 -> x8, Pallas kernels: 7.75 us -> 7.19 us  [the longest x6 4.11 us: call(): pl.pallas_call(kernel, out_shape=shapes, in_specs=specs, out_specs=outs,...]
  transfers between devices with their start and end apart: 6 -> 8, of which waited for: 3 -> 5; matrix products, arithmetic and copies ran while one was open for 2% -> 1% of each run, Pallas kernels for 0% -> 0%
where the time goes in v3:
time: 155 us
  blocking collectives  79 us (51%)
  starting transfers between devices  42.1 us (27%)
  waiting for transfers between devices  20.1 us (13%)
  Pallas kernels  7.19 us (5%)
  local copies, waits for them, and re-layouts  3.56 us (2%)
    all_gather x1, blocking collectives, local(): panel_own = lax.all_gather(packed, Z8, axis=0, tiled=True)  32.1 us
    all_to_all x2, blocking collectives, all_to_all(): return lax.all_to_all(x, axes, split_axis=0, concat_axis=0, tiled=True)  31.8 us
    all_to_all x4, starting transfers between devices, all_to_all(): return lax.all_to_all(x, axes, split_axis=0, concat_axis=0, tiled=True)  24.4 us
    all_to_all x4, waiting for transfers between devices, all_to_all(): return lax.all_to_all(x, axes, split_axis=0, concat_axis=0, tiled=True)  15.3 us
    all_gather x1, blocking collectives, local(): lax.all_gather(jnp.concatenate([basis, before], axis=1), FE, axis=0, tile...  15.1 us
    ppermute x1, starting transfers between devices, local(): got = lax.ppermute(send, 'c', [(0, 1), (1, 0)])  8.63 us
    pallas_call x6, Pallas kernels, call(): pl.pallas_call(kernel, out_shape=shapes, in_specs=specs, out_specs=outs,...  4.11 us
    ppermute x1, starting transfers between devices, local(): panel_other = lax.ppermute(panel_own, 'z0', [(0, 1), (1, 0)])  3.45 us
  transfers between devices with their start and end apart: 8, of which 5 were waited for; matrix products, arithmetic and copies ran while one was open for 1% of the time, Pallas kernels for 0%

profile of v3, /device:TPU:1, one launch (start us, length us, event | category | flops | bytes accessed | tf_op | source)
XLA Modules:
  0.0 154.6 jit_solution(2366524896901730965)
XLA Ops:
  0.6 1.2 copy-done.1
  2.2 1.3 copy-done
  3.5 5.1 %all-to-all-start = ((bf16[4,256,1024]{2,1,0:T(8,128)(2,1)}), bf16[4,256,1024]{2,1,0:T(8,128)(2,1)S(1)}, u32[]{:S(2)}, u32[]{:S(2)}) async-start(bf16[4,256,1024]{2,1,0:T(8,128)(2,1)} %copy-done), calls=%async_computation | async-start | bytes 4194304 | tf_op jit(solution)/shard_map/all_to_all | solution.py:191
  8.8 32.1 %all_gather.6.own_ref = bf16[256,1024]{1,0:T(8,128)(2,1)S(1)} all-gather(bf16[32,1024]{1,0:T(8,128)(2,1)S(1)} %shard_map.77), channel_id=1, replica_groups=mesh['z3'=2,'z2'=2,'z1'=2,'z0'=2,'yh'=2,'x'=4,'c'=2,'yl'=2] {'z3','z2','..., dimensions={0}, use_global_device_ids=true | all-gather | bytes 589824 | tf_op jit(solution)/shard_map/all_gather | solution.py:217
  41.0 3.5 %collective-permute-start = (bf16[256,1024]{1,0:T(8,128)(2,1)S(1)}, bf16[256,1024]{1,0:T(8,128)(2,1)S(1)}, u32[]{:S(2)}, u32[]{:S(2)}) collective-permute-start(bf16[256,1024]{1,0:T(8,128)(2,1)S(1)} %all_gather.6.own_ref), channel_id=1, source_target_pairs={{0,32},{32,0},{1,33},{33,1},{2,34},{34,2},{3,35},{35,3},{4,36},{36... | collective-permute-start | bytes 1572872 | tf_op jit(solution)/shard_map/ppermute | solution.py:218
  45.1 2.8 %collective-permute-start.1 = (s32[1,65]{1,0:T(1,128)S(1)}, s32[1,65]{1,0:T(1,128)S(1)}, u32[]{:S(2)}, u32[]{:S(2)}) collective-permute-start(s32[1,65]{1,0:T(1,128)S(1)} %pad_add_fusion.1), channel_id=1, source_target_pairs={{0,1},{1,0},{2,3},{3,2},{4,5},{5,4},{6,7},{7,6},{8,9},{9,8},{10,11... | collective-permute-start | bytes 788 | tf_op jit(solution)/shard_map/ppermute | solution.py:202
  48.1 1.4 collective-permute-done.1
  49.4 2.0 %collective-permute-done.other_ref = bf16[256,1024]{1,0:T(8,128)(2,1)S(1)} collective-permute-done((bf16[256,1024]{1,0:T(8,128)(2,1)S(1)}, bf16[256,1024]{1,0:T(8,128)(2,1)S(1)}, u32[]{:S(2)}, u32[]{:S(2)}) %collective-permute-start) | collective-permute-done | bytes 524320 | tf_op jit(solution)/shard_map/ppermute | solution.py:218
  51.4 2.8 %shard_map.79 = (bf16[256,1024]{1,0:T(8,128)(2,1)S(1)}, bf16[256,1024]{1,0:T(8,128)(2,1)S(1)}) custom-call(s32[3]{0:T(128)S(1)} %pad_add_fusion.place_ref.refs_0_, bf16[256,1024]{1,0:T(8,128)(2,1)S(1)} %all_gather.6.own_ref, bf16[256,1024]{1,0:T(8,128)(2,1)S(1)} %collective-permute-done.other_ref, bf16[1024,1024]{1,0:T(8,128)(2,1)S(1)} %bitcast.15), custom_call_target="tpu_custom_call" | custom-call | tf_op jit(solution)/shard_map/pallas_call | solution.py:226
  54.1 8.6 %collective-permute-start.2 = (bf16[256,1024]{1,0:T(8,128)(2,1)S(1)}, bf16[256,1024]{1,0:T(8,128)(2,1)S(1)}, u32[]{:S(2)}, u32[]{:S(2)}) collective-permute-start(bf16[256,1024]{1,0:T(8,128)(2,1)S(1)} %get-tuple-element.11), channel_id=1, source_target_pairs={{0,2},{2,0},{1,3},{3,1},{4,6},{6,4},{5,7},{7,5},{8,10},{10,8},{9,1... | collective-permute-start | bytes 1572872 | tf_op jit(solution)/shard_map/ppermute | solution.py:239
  62.8 1.5 collective-permute-done.2
  64.3 1.0 add_convert_fusion
  65.3 7.3 %all-to-all-start.1 = ((bf16[16,16,1024]{2,1,0:T(8,128)(2,1)}), bf16[16,16,1024]{2,1,0:T(8,128)(2,1)S(1)}, u32[]{:S(2)}, u32[]{:S(2)}) async-start(bf16[16,16,1024]{2,1,0:T(8,128)(2,1)} %bitcast.8), calls=%async_computation.1 | async-start | bytes 1048576 | tf_op jit(solution)/shard_map/all_to_all | solution.py:191
  72.7 10.6 %all-to-all-done.1 = bf16[16,16,1024]{2,1,0:T(8,128)(2,1)S(1)} async-done(((bf16[16,16,1024]{2,1,0:T(8,128)(2,1)}), bf16[16,16,1024]{2,1,0:T(8,128)(2,1)S(1)}, u32[]{:S(2)}, u32[]{:S(2)}) %all-to-all-start.1) | async-done | bytes 524320 | tf_op jit(solution)/shard_map/all_to_all | solution.py:191
  83.4 2.8 %collective-permute-start.3 = (bf16[32,128]{1,0:T(8,128)(2,1)S(1)}, bf16[32,128]{1,0:T(8,128)(2,1)S(1)}, u32[]{:S(2)}, u32[]{:S(2)}) collective-permute-start(bf16[32,128]{1,0:T(8,128)(2,1)S(1)} %get-tuple-element.13), channel_id=1, source_target_pairs={{0,32},{32,64},{64,96},{96,128},{128,160},{160,192},{192,224},{224... | collective-permute-start | bytes 24584 | tf_op jit(solution)/shard_map/ppermute | solution.py:246
  86.4 0.7 broadcast_in_dim.16
  87.2 3.4 %all-to-all-start.2 = ((bf16[4,32,1024]{2,1,0:T(8,128)(2,1)}), bf16[4,32,1024]{2,1,0:T(8,128)(2,1)S(1)}, u32[]{:S(2)}, u32[]{:S(2)}) async-start(bf16[4,32,1024]{2,1,0:T(8,128)(2,1)} %broadcast_in_dim.16), calls=%async_computation.2 | async-start | bytes 524288 | tf_op jit(solution)/shard_map/all_to_all | solution.py:191
  90.6 15.1 %all_gather.7.left_ref = bf16[256,1152]{1,0:T(8,128)(2,1)S(1)} all-gather(bf16[32,1152]{1,0:T(8,128)(2,1)S(1)} %pad_maximum_fusion), channel_id=1, replica_groups=mesh['z3'=2,'z2'=2,'z1'=2,'z0'=2,'yh'=2,'x'=4,'c'=2,'yl'=2] {'x','c'}, dimensions={0}, use_global_device_ids=true | all-gather | bytes 663552 | tf_op jit(solution)/shard_map/all_gather | solution.py:248
  105.7 1.9 %shard_map.81 = f32[2,8,56,128]{3,2,1,0:T(8,128)S(1)} custom-call(s32[2]{0:T(128)S(1)} %slice_reduce_fusion.lags_ref, s32[3]{0:T(128)S(1)} %pad_add_fusion.place_ref.refs_0_, s32[2,64]{1,0:T(2,128)S(1)} %slice.7.seg_ref, bf16[256,1152]{1,0:T(8,128)(2,1)S(1)} %all_gather.7.left_ref, bf16[128,1024]{1,0:T(8,128)(2,1)S(1)} %bitcast.17), custom_call_target="tpu_custom_call" | custom-call | tf_op jit(solution)/shard_map/pallas_call | solution.py:184
  107.6 9.7 %all_to_all.30.parts_ref = f32[2,8,56,128]{3,2,1,0:T(8,128)S(1)} all-to-all(f32[2,8,56,128]{3,2,1,0:T(8,128)S(1)} %shard_map.81), channel_id=1, replica_groups=mesh['z3'=2,'z2'=2,'z1'=2,'z0'=2,'yh'=2,'x'=4,'c'=2,'yl'=2] {'z0'}, dimensions={0} | all-to-all | bytes 917504 | tf_op jit(solution)/shard_map/all_to_all | solution.py:191
  117.3 22.1 %all_to_all.31.parts_ref = f32[8,56,128]{2,1,0:T(8,128)S(1)} all-to-all(f32[8,56,128]{2,1,0:T(8,128)S(1)} %shard_map.82), channel_id=1, replica_groups=mesh['z3'=2,'z2'=2,'z1'=2,'z0'=2,'yh'=2,'x'=4,'c'=2,'yl'=2] {'z3','z2','..., dimensions={0} | all-to-all | bytes 458752 | tf_op jit(solution)/shard_map/all_to_all | solution.py:191
  140.0 8.5 %all-to-all-start.5 = ((f32[8,8,128]{2,1,0:T(8,128)}), f32[8,8,128]{2,1,0:T(8,128)S(1)}, u32[]{:S(2)}, u32[]{:S(2)}) async-start(f32[8,8,128]{2,1,0:T(8,128)} %shard_map.83), calls=%async_computation.5 | async-start | bytes 65536 | tf_op jit(solution)/shard_map/all_to_all | solution.py:191
  148.6 4.6 %all-to-all-done.5.refs_1_ = f32[8,8,128]{2,1,0:T(8,128)S(1)} async-done(((f32[8,8,128]{2,1,0:T(8,128)}), f32[8,8,128]{2,1,0:T(8,128)S(1)}, u32[]{:S(2)}, u32[]{:S(2)}) %all-to-all-start.5) | async-done | bytes 32800 | tf_op jit(solution)/shard_map/all_to_all | solution.py:191
  153.2 1.4 shard_map.84
  (25 shorter events, 1.7 us)
Async XLA Ops:
  0.6 1.2 copy-start.1
  2.2 1.3 copy-start
  3.5 5.2 %copy-start.2 = (bf16[2048,16]{0,1:T(8,128)(2,1)S(1)}, bf16[2048,16]{0,1:T(8,128)(2,1)}, u32[]{:S(2)}) copy-start(bf16[2048,16]{0,1:T(8,128)(2,1)} %param.7) | copy-start | bytes 196612
  3.5 5.2 %copy-start.3 = (bf16[2048,16]{0,1:T(8,128)(2,1)S(1)}, bf16[2048,16]{0,1:T(8,128)(2,1)}, u32[]{:S(2)}) copy-start(bf16[2048,16]{0,1:T(8,128)(2,1)} %param.8) | copy-start | bytes 196612
  3.5 41.5 %copy-start.5 = (s32[1,64]{1,0:T(1,128)S(1)}, s32[1,64]{1,0:T(1,128)}, u32[]{:S(2)}) copy-start(s32[1,64]{1,0:T(1,128)} %param.10) | copy-start | bytes 772
  3.5 47.8 %all-to-all-start = ((bf16[4,256,1024]{2,1,0:T(8,128)(2,1)}), bf16[4,256,1024]{2,1,0:T(8,128)(2,1)S(1)}, u32[]{:S(2)}, u32[]{:S(2)}) async-start(bf16[4,256,1024]{2,1,0:T(8,128)(2,1)} %copy-done), calls=%async_computation | async-start | bytes 4194304 | tf_op jit(solution)/shard_map/all_to_all | solution.py:191
  41.0 10.4 %collective-permute-start = (bf16[256,1024]{1,0:T(8,128)(2,1)S(1)}, bf16[256,1024]{1,0:T(8,128)(2,1)S(1)}, u32[]{:S(2)}, u32[]{:S(2)}) collective-permute-start(bf16[256,1024]{1,0:T(8,128)(2,1)S(1)} %all_gather.6.own_ref), channel_id=1, source_target_pairs={{0,32},{32,0},{1,33},{33,1},{2,34},{34,2},{3,35},{35,3},{4,36},{36... | collective-permute-start | bytes 1572872 | tf_op jit(solution)/shard_map/ppermute | solution.py:218
  45.1 4.3 %collective-permute-start.1 = (s32[1,65]{1,0:T(1,128)S(1)}, s32[1,65]{1,0:T(1,128)S(1)}, u32[]{:S(2)}, u32[]{:S(2)}) collective-permute-start(s32[1,65]{1,0:T(1,128)S(1)} %pad_add_fusion.1), channel_id=1, source_target_pairs={{0,1},{1,0},{2,3},{3,2},{4,5},{5,4},{6,7},{7,6},{8,9},{9,8},{10,11... | collective-permute-start | bytes 788 | tf_op jit(solution)/shard_map/ppermute | solution.py:202
  54.1 10.2 %collective-permute-start.2 = (bf16[256,1024]{1,0:T(8,128)(2,1)S(1)}, bf16[256,1024]{1,0:T(8,128)(2,1)S(1)}, u32[]{:S(2)}, u32[]{:S(2)}) collective-permute-start(bf16[256,1024]{1,0:T(8,128)(2,1)S(1)} %get-tuple-element.11), channel_id=1, source_target_pairs={{0,2},{2,0},{1,3},{3,1},{4,6},{6,4},{5,7},{7,5},{8,10},{10,8},{9,1... | collective-permute-start | bytes 1572872 | tf_op jit(solution)/shard_map/ppermute | solution.py:239
  65.3 18.1 %all-to-all-start.1 = ((bf16[16,16,1024]{2,1,0:T(8,128)(2,1)}), bf16[16,16,1024]{2,1,0:T(8,128)(2,1)S(1)}, u32[]{:S(2)}, u32[]{:S(2)}) async-start(bf16[16,16,1024]{2,1,0:T(8,128)(2,1)} %bitcast.8), calls=%async_computation.1 | async-start | bytes 1048576 | tf_op jit(solution)/shard_map/all_to_all | solution.py:191
  83.4 7.1 %collective-permute-start.3 = (bf16[32,128]{1,0:T(8,128)(2,1)S(1)}, bf16[32,128]{1,0:T(8,128)(2,1)S(1)}, u32[]{:S(2)}, u32[]{:S(2)}) collective-permute-start(bf16[32,128]{1,0:T(8,128)(2,1)S(1)} %get-tuple-element.13), channel_id=1, source_target_pairs={{0,32},{32,64},{64,96},{96,128},{128,160},{160,192},{192,224},{224... | collective-permute-start | bytes 24584 | tf_op jit(solution)/shard_map/ppermute | solution.py:246
  87.2 18.5 %all-to-all-start.2 = ((bf16[4,32,1024]{2,1,0:T(8,128)(2,1)}), bf16[4,32,1024]{2,1,0:T(8,128)(2,1)S(1)}, u32[]{:S(2)}, u32[]{:S(2)}) async-start(bf16[4,32,1024]{2,1,0:T(8,128)(2,1)} %broadcast_in_dim.16), calls=%async_computation.2 | async-start | bytes 524288 | tf_op jit(solution)/shard_map/all_to_all | solution.py:191
  90.6 57.9 %copy-start.4 = (f32[32]{0:T(128)S(1)}, f32[32]{0:T(128)}, u32[]{:S(2)}) copy-start(f32[32]{0:T(128)} %param.11) | copy-start | bytes 388
  140.0 13.2 %all-to-all-start.5 = ((f32[8,8,128]{2,1,0:T(8,128)}), f32[8,8,128]{2,1,0:T(8,128)S(1)}, u32[]{:S(2)}, u32[]{:S(2)}) async-start(f32[8,8,128]{2,1,0:T(8,128)} %shard_map.83), calls=%async_computation.5 | async-start | bytes 65536 | tf_op jit(solution)/shard_map/all_to_all | solution.py:191

commit v4 on v3

--- a/solution.py
+++ b/solution.py
@@ -48,16 +48,17 @@
 
     def store(even, odd, keep_ref, send_ref, own_c):
         for yh, acc in enumerate((even, odd)):
-            for yl in range(2):
-                for half in range(2):
-                    for zh in range(4):
-                        row = zh * 64 + half * 16 + yl * 8
-                        both = jnp.concatenate(
-                            [acc[row : row + 8], acc[row + 32 : row + 40]], axis=0
-                        )
-                        chunk = (yh * 2 + yl) * 4 + half * 2 + (zh >> 1)
-                        ref = keep_ref if (zh & 1) == own_c else send_ref
-                        ref[chunk * 16 : chunk * 16 + 16, :] = both.astype(BF)
+            for z1 in range(2):
+                for yl in range(2):
+                    for half in range(2):
+                        for z2 in range(2):
+                            row = (z2 * 2 + z1) * 32 + half * 16 + yl * 8
+                            both = jnp.concatenate(
+                                [acc[row : row + 8], acc[row + 128 : row + 136]], axis=0
+                            )
+                            chunk = ((z1 * 2 + yh) * 2 + yl) * 4 + half * 2
+                            ref = keep_ref if z2 == own_c else send_ref
+                            ref[chunk * 8 : chunk * 8 + 16, :] = both.astype(BF)
 
     for own_z0 in range(2):
         for own_c in range(2):
@@ -69,37 +70,41 @@
 
 
 def sum_kernel(parts_ref, basis_ref, tail_ref):
-    sums = []
-    for yh in range(2):
-        total = parts_ref[yh, 0, 0].astype(F32)
-        for i in range(1, 8):
-            total = total + parts_ref[yh, i // 4, i % 4].astype(F32)
-        sums.append(total)
-    basis = jnp.concatenate([sums[0][:8], sums[1][:8], sums[0][8:], sums[1][8:]], axis=0)
-    basis_ref[...] = basis.astype(BF)
-    lane = lax.broadcasted_iota(I32, (32, 128), 1)
-    tail = jnp.where(lane < 64, pltpu.roll(basis[:, 384:512], 64, 1), basis[:, 896:])
-    tail_ref[...] = tail.astype(BF)
+    for z0 in range(2):
+        sums = []
+        for yh in range(2):
+            total = parts_ref[z0, yh, 0, 0].astype(F32)
+            for i in range(1, 8):
+                total = total + parts_ref[z0, yh, i // 4, i % 4].astype(F32)
+            sums.append(total)
+        basis = jnp.concatenate(sums, axis=0)
+        for rep in range(2):
+            at = rep * 1024 + z0 * 512
+            basis_ref[:, at : at + 512] = basis[:, rep * 512 : (rep + 1) * 512].astype(BF)
+        if z0 == 1:
+            lane = lax.broadcasted_iota(I32, (16, 128), 1)
+            tail = jnp.where(lane < 64, pltpu.roll(basis[:, 384:512], 64, 1), basis[:, 896:])
+            tail_ref[...] = tail.astype(BF)
 
 
 def cov_kernel(lags_ref, place_ref, seg_ref, left_ref, right_ref, out_ref):
-    z = place_ref[0]
+    first = (place_ref[0] >> 1) * 1024
     perm = one_hot(
         128,
         128,
         lambda r, c: c
-        == ((r >> 5) & 1) * 64 + ((r >> 1) & 1) * 32 + (r >> 6) * 16 + ((r >> 2) & 7) * 2 + (r & 1),
+        == (r >> 5) * 32 + ((r >> 1) & 1) * 16 + ((r >> 2) & 7) * 2 + (r & 1),
     )
     now = jnp.dot(perm, right_ref[...], preferred_element_type=F32)
     now_bf = now.astype(BF)
     tri = lax.broadcasted_iota(I32, (64, 64), 1) <= lax.broadcasted_iota(I32, (64, 64), 0)
     seg = seg_ref[...].astype(F32)
-    tails = left_ref[:, 1024:].astype(F32)
+    tails = left_ref[:, 2048:].astype(F32)
     keep, keep_end, lagged = [], [], []
     for rep in range(2):
         lag = lags_ref[rep]
         ends = jnp.sum(jnp.where(tri, seg[rep : rep + 1, :], 0.0), axis=1, keepdims=True)
-        pos = lax.broadcasted_iota(I32, (1, 512), 1) + z * 512
+        pos = lax.broadcasted_iota(I32, (1, 1024), 1) + first
         here = pos.astype(F32)
         ahead = (pos + lag).astype(F32)
         behind = (pos - lag).astype(F32)
@@ -109,27 +114,23 @@
         inside = jnp.where(behind >= 0.0, 1.0, 0.0)
         keep_end.append((1.0 - jnp.max(cut_end, axis=0, keepdims=True)) * inside)
         tail = tails if rep == 1 else pltpu.roll(tails, 64, 1)
-        block = left_ref[:, rep * 512 : (rep + 1) * 512].astype(F32)
+        block = left_ref[:, rep * 1024 : (rep + 1) * 1024].astype(F32)
         ext = jnp.concatenate([tail, block], axis=1)
-        lagged.append(pltpu.roll(ext, lag + 512, 1)[:, :512].astype(BF))
+        lagged.append(pltpu.roll(ext, lag + 1024, 1)[:, :1024].astype(BF))
     keep = jnp.concatenate(keep, axis=1)
     keep_end = jnp.concatenate(keep_end, axis=1)
     lagged = jnp.concatenate(lagged, axis=1)
-    left = left_ref[:, :1024]
+    left = left_ref[:, :2048]
     start_bf, end_bf = keep.astype(BF), keep_end.astype(BF)
     for m, lhs in enumerate((left * start_bf, lagged * end_bf, left * end_bf)):
         block = lax.dot_general(lhs, now_bf, NT, preferred_element_type=F32)
-        for d in range(16):
-            out_ref[d % 2, d // 2, m * 16 : (m + 1) * 16, :] = block[d * 16 : (d + 1) * 16, :]
+        for d in range(8):
+            out_ref[d, m * 16 : (m + 1) * 16, :] = block[d * 16 : (d + 1) * 16, :]
     var = lax.dot_general(
-        jnp.ones((8, 1024), F32), now * now * keep_end, NT, precision=HI, preferred_element_type=F32
-    )
-    for d in range(16):
-        out_ref[d % 2, d // 2, 48:56, :] = var
-
-
-def pair_kernel(parts_ref, out_ref):
-    out_ref[...] = parts_ref[0] + parts_ref[1]
+        jnp.ones((8, 2048), F32), now * now * keep_end, NT, precision=HI, preferred_element_type=F32
+    )
+    for d in range(8):
+        out_ref[d, 48:56, :] = var
 
 
 def rows_kernel(parts_ref, out_ref):
@@ -238,27 +239,26 @@
     )(place, panel_own, panel_other, frames_h)
     got = lax.ppermute(send, "c", [(0, 1), (1, 0)])
     pairs = (keep.astype(F32) + got.astype(F32)).astype(BF)
-    parts = all_to_all(pairs.reshape(16, 16, 1024), ("yh", "yl", "x"))
+    parts = all_to_all(pairs.reshape(32, 8, 1024), ("z0", "yh", "yl", "x"))
     basis, tail = call(
-        sum_kernel, [((32, 1024), BF), ((32, 128), BF)], parts.reshape(2, 2, 4, 16, 1024)
-    )
-
-    before = lax.ppermute(tail, Z, [(i, i + 1) for i in range(15)])
-    right = all_to_all(jnp.broadcast_to(basis[None], (4, 32, 1024)), ("yh", "yl"))
+        sum_kernel, [((16, 2048), BF), ((16, 128), BF)], parts.reshape(2, 2, 2, 4, 8, 1024)
+    )
+
+    before = lax.ppermute(tail, Z8, [(i, i + 1) for i in range(7)])
+    right = all_to_all(jnp.broadcast_to(basis[None], (8, 16, 2048)), ("z0", "yh", "yl"))
     left = lax.all_gather(jnp.concatenate([basis, before], axis=1), FE, axis=0, tiled=True)
 
     terms = call(
         cov_kernel,
-        [((2, 8, 56, 128), F32)],
+        [((8, 56, 128), F32)],
         both[:, 0],
         place,
         both[:, 1:],
         left,
-        right.reshape(128, 1024),
+        right.reshape(128, 2048),
         smem=2,
     )
-    pair = call(pair_kernel, [((8, 56, 128), F32)], all_to_all(terms, "z0"))
-    rows = call(rows_kernel, [((8, 8, 128), F32)], all_to_all(pair, Z8))
+    rows = call(rows_kernel, [((8, 8, 128), F32)], all_to_all(terms, Z8))
     by_row = all_to_all(rows, FE)
     return call(
         lambda *refs: final_kernel(1.0 / 16384.0, *refs),

time: 155 us -> 149 us (0.961)
  blocking collectives: 79 us -> 93.7 us
  starting transfers between devices: 42.1 us -> 31.1 us
  waiting for transfers between devices: 20.1 us -> 10.6 us
    all_to_all x2, blocking collectives: 31.8 us -> 45.9 us  [all_to_all(): return lax.all_to_all(x, axes, split_axis=0, concat_axis=0, tiled=True)]
    all_to_all x4 -> x3, starting transfers between devices: 24.4 us -> 13.4 us  [all_to_all(): return lax.all_to_all(x, axes, split_axis=0, concat_axis=0, tiled=True)]
    all_to_all x4 -> x3, waiting for transfers between devices: 15.3 us -> 4.65 us  [all_to_all(): return lax.all_to_all(x, axes, split_axis=0, concat_axis=0, tiled=True)]
    pallas_call x6 -> x5, Pallas kernels: 4.11 us -> 4.74 us  [call(): pl.pallas_call(kernel, out_shape=shapes, in_specs=specs, out_specs=outs,...]
  transfers between devices with their start and end apart: 8 -> 7, of which waited for: 5 -> 5; matrix products, arithmetic and copies ran while one was open for 1% -> 0% of each run, Pallas kernels for 0% -> 0%
where the time goes in v4:
time: 149 us
  blocking collectives  93.7 us (63%)
  starting transfers between devices  31.1 us (21%)
  waiting for transfers between devices  10.6 us (7%)
  Pallas kernels  7.81 us (5%)
  local copies, waits for them, and re-layouts  3.67 us (2%)
    all_to_all x2, blocking collectives, all_to_all(): return lax.all_to_all(x, axes, split_axis=0, concat_axis=0, tiled=True)  45.9 us
    all_gather x1, blocking collectives, local(): panel_own = lax.all_gather(packed, Z8, axis=0, tiled=True)  32.1 us
    all_gather x1, blocking collectives, local(): lax.all_gather(jnp.concatenate([basis, before], axis=1), FE, axis=0, tile...  15.7 us
    all_to_all x3, starting transfers between devices, all_to_all(): return lax.all_to_all(x, axes, split_axis=0, concat_axis=0, tiled=True)  13.4 us
    ppermute x1, starting transfers between devices, local(): got = lax.ppermute(send, 'c', [(0, 1), (1, 0)])  8.61 us
    pallas_call x5, Pallas kernels, call(): pl.pallas_call(kernel, out_shape=shapes, in_specs=specs, out_specs=outs,...  4.74 us
    all_to_all x3, waiting for transfers between devices, all_to_all(): return lax.all_to_all(x, axes, split_axis=0, concat_axis=0, tiled=True)  4.65 us
    ppermute x1, starting transfers between devices, local(): panel_other = lax.ppermute(panel_own, 'z0', [(0, 1), (1, 0)])  3.45 us
  transfers between devices with their start and end apart: 7, of which 5 were waited for; matrix products, arithmetic and copies ran while one was open for 0% of the time, Pallas kernels for 0%

profile of v4, /device:TPU:1, one launch (start us, length us, event | category | flops | bytes accessed | tf_op | source)
XLA Modules:
  0.0 148.7 jit_solution(6946561208134888601)
XLA Ops:
  0.6 1.2 copy-done.1
  1.9 0.3 shard_map.78
  2.2 1.3 copy-done
  3.5 5.1 %all-to-all-start = ((bf16[4,256,1024]{2,1,0:T(8,128)(2,1)}), bf16[4,256,1024]{2,1,0:T(8,128)(2,1)S(1)}, u32[]{:S(2)}, u32[]{:S(2)}) async-start(bf16[4,256,1024]{2,1,0:T(8,128)(2,1)} %copy-done), calls=%async_computation | async-start | bytes 4194304 | tf_op jit(solution)/shard_map/all_to_all | solution.py:192
  8.8 32.1 %all_gather.6.own_ref = bf16[256,1024]{1,0:T(8,128)(2,1)S(1)} all-gather(bf16[32,1024]{1,0:T(8,128)(2,1)S(1)} %shard_map.77), channel_id=1, replica_groups=mesh['z3'=2,'z2'=2,'z1'=2,'z0'=2,'yh'=2,'x'=4,'c'=2,'yl'=2] {'z3','z2','..., dimensions={0}, use_global_device_ids=true | all-gather | bytes 589824 | tf_op jit(solution)/shard_map/all_gather | solution.py:218
  40.9 3.5 %collective-permute-start = (bf16[256,1024]{1,0:T(8,128)(2,1)S(1)}, bf16[256,1024]{1,0:T(8,128)(2,1)S(1)}, u32[]{:S(2)}, u32[]{:S(2)}) collective-permute-start(bf16[256,1024]{1,0:T(8,128)(2,1)S(1)} %all_gather.6.own_ref), channel_id=1, source_target_pairs={{0,32},{32,0},{1,33},{33,1},{2,34},{34,2},{3,35},{35,3},{4,36},{36... | collective-permute-start | bytes 1572872 | tf_op jit(solution)/shard_map/ppermute | solution.py:219
  45.1 2.8 %collective-permute-start.1 = (s32[1,65]{1,0:T(1,128)S(1)}, s32[1,65]{1,0:T(1,128)S(1)}, u32[]{:S(2)}, u32[]{:S(2)}) collective-permute-start(s32[1,65]{1,0:T(1,128)S(1)} %pad_add_fusion.1), channel_id=1, source_target_pairs={{0,1},{1,0},{2,3},{3,2},{4,5},{5,4},{6,7},{7,6},{8,9},{9,8},{10,11... | collective-permute-start | bytes 788 | tf_op jit(solution)/shard_map/ppermute | solution.py:203
  48.1 1.4 collective-permute-done.1
  49.4 2.0 %collective-permute-done.other_ref = bf16[256,1024]{1,0:T(8,128)(2,1)S(1)} collective-permute-done((bf16[256,1024]{1,0:T(8,128)(2,1)S(1)}, bf16[256,1024]{1,0:T(8,128)(2,1)S(1)}, u32[]{:S(2)}, u32[]{:S(2)}) %collective-permute-start) | collective-permute-done | bytes 524320 | tf_op jit(solution)/shard_map/ppermute | solution.py:219
  51.4 2.8 %shard_map.79 = (bf16[256,1024]{1,0:T(8,128)(2,1)S(1)}, bf16[256,1024]{1,0:T(8,128)(2,1)S(1)}) custom-call(s32[3]{0:T(128)S(1)} %pad_add_fusion.place_ref.refs_0_, bf16[256,1024]{1,0:T(8,128)(2,1)S(1)} %all_gather.6.own_ref, bf16[256,1024]{1,0:T(8,128)(2,1)S(1)} %collective-permute-done.other_ref, bf16[1024,1024]{1,0:T(8,128)(2,1)S(1)} %bitcast.16), custom_call_target="tpu_custom_call" | custom-call | tf_op jit(solution)/shard_map/pallas_call | solution.py:227
  54.1 8.6 %collective-permute-start.2 = (bf16[256,1024]{1,0:T(8,128)(2,1)S(1)}, bf16[256,1024]{1,0:T(8,128)(2,1)S(1)}, u32[]{:S(2)}, u32[]{:S(2)}) collective-permute-start(bf16[256,1024]{1,0:T(8,128)(2,1)S(1)} %get-tuple-element.11), channel_id=1, source_target_pairs={{0,2},{2,0},{1,3},{3,1},{4,6},{6,4},{5,7},{7,5},{8,10},{10,8},{9,1... | collective-permute-start | bytes 1572872 | tf_op jit(solution)/shard_map/ppermute | solution.py:240
  62.8 1.5 %collective-permute-done.2 = bf16[256,1024]{1,0:T(8,128)(2,1)S(1)} collective-permute-done((bf16[256,1024]{1,0:T(8,128)(2,1)S(1)}, bf16[256,1024]{1,0:T(8,128)(2,1)S(1)}, u32[]{:S(2)}, u32[]{:S(2)}) %collective-permute-start.2) | collective-permute-done | bytes 524320 | tf_op jit(solution)/shard_map/ppermute | solution.py:240
  64.5 18.4 %all_to_all.25 = bf16[32,8,1024]{2,1,0:T(8,128)(2,1)S(1)} all-to-all(bf16[32,8,1024]{2,1,0:T(8,128)(2,1)S(1)} %fusion), channel_id=1, replica_groups=mesh['z3'=2,'z2'=2,'z1'=2,'z0'=2,'yh'=2,'x'=4,'c'=2,'yl'=2] {'z0','yh','..., dimensions={0} | all-to-all | bytes 1048576 | tf_op jit(solution)/shard_map/all_to_all | solution.py:192
  82.9 0.8 broadcast_in_dim.16
  83.7 3.8 %all-to-all-start.2 = ((bf16[8,16,2048]{2,1,0:T(8,128)(2,1)}), bf16[8,16,2048]{2,1,0:T(8,128)(2,1)S(1)}, u32[]{:S(2)}, u32[]{:S(2)}) async-start(bf16[8,16,2048]{2,1,0:T(8,128)(2,1)} %broadcast_in_dim.16), calls=%async_computation.2 | async-start | bytes 1048576 | tf_op jit(solution)/shard_map/all_to_all | solution.py:192
  87.6 2.8 %collective-permute-start.3 = (bf16[16,128]{1,0:T(8,128)(2,1)S(1)}, bf16[16,128]{1,0:T(8,128)(2,1)S(1)}, u32[]{:S(2)}, u32[]{:S(2)}) collective-permute-start(bf16[16,128]{1,0:T(8,128)(2,1)S(1)} %get-tuple-element.13), channel_id=1, source_target_pairs={{0,64},{64,128},{128,192},{192,256},{256,320},{320,384},{384,448},... | collective-permute-start | bytes 12296 | tf_op jit(solution)/shard_map/ppermute | solution.py:247
  90.6 1.2 collective-permute-done.3
  91.8 15.7 %all_gather.7.left_ref = bf16[128,2176]{1,0:T(8,128)(2,1)S(1)} all-gather(bf16[16,2176]{1,0:T(8,128)(2,1)S(1)} %pad_maximum_fusion), channel_id=1, replica_groups=mesh['z3'=2,'z2'=2,'z1'=2,'z0'=2,'yh'=2,'x'=4,'c'=2,'yl'=2] {'x','c'}, dimensions={0}, use_global_device_ids=true | all-gather | bytes 626688 | tf_op jit(solution)/shard_map/all_gather | solution.py:249
  107.5 2.5 %shard_map.81 = f32[8,56,128]{2,1,0:T(8,128)S(1)} custom-call(s32[2]{0:T(128)S(1)} %slice_reduce_fusion.lags_ref, s32[3]{0:T(128)S(1)} %pad_add_fusion.place_ref.refs_0_, s32[2,64]{1,0:T(2,128)S(1)} %slice.7.seg_ref, bf16[128,2176]{1,0:T(8,128)(2,1)S(1)} %all_gather.7.left_ref, bf16[128,2048]{1,0:T(8,128)(2,1)S(1)} %bitcast.17), custom_call_target="tpu_custom_call" | custom-call | tf_op jit(solution)/shard_map/pallas_call | solution.py:185
  110.0 27.5 %all_to_all.26.parts_ref = f32[8,56,128]{2,1,0:T(8,128)S(1)} all-to-all(f32[8,56,128]{2,1,0:T(8,128)S(1)} %shard_map.81), channel_id=1, replica_groups=mesh['z3'=2,'z2'=2,'z1'=2,'z0'=2,'yh'=2,'x'=4,'c'=2,'yl'=2] {'z3','z2','..., dimensions={0} | all-to-all | bytes 458752 | tf_op jit(solution)/shard_map/all_to_all | solution.py:192
  137.5 0.6 shard_map.82
  138.2 4.5 %all-to-all-start.4 = ((f32[8,8,128]{2,1,0:T(8,128)}), f32[8,8,128]{2,1,0:T(8,128)S(1)}, u32[]{:S(2)}, u32[]{:S(2)}) async-start(f32[8,8,128]{2,1,0:T(8,128)} %shard_map.82), calls=%async_computation.4 | async-start | bytes 65536 | tf_op jit(solution)/shard_map/all_to_all | solution.py:192
  142.7 4.6 %all-to-all-done.4.refs_1_ = f32[8,8,128]{2,1,0:T(8,128)S(1)} async-done(((f32[8,8,128]{2,1,0:T(8,128)}), f32[8,8,128]{2,1,0:T(8,128)S(1)}, u32[]{:S(2)}, u32[]{:S(2)}) %all-to-all-start.4) | async-done | bytes 32800 | tf_op jit(solution)/shard_map/all_to_all | solution.py:192
  147.4 1.4 shard_map.83
  (22 shorter events, 0.9 us)
Async XLA Ops:
  0.6 1.2 copy-start.1
  2.2 1.3 copy-start
  3.5 5.2 %copy-start.2 = (bf16[2048,16]{0,1:T(8,128)(2,1)S(1)}, bf16[2048,16]{0,1:T(8,128)(2,1)}, u32[]{:S(2)}) copy-start(bf16[2048,16]{0,1:T(8,128)(2,1)} %param.7) | copy-start | bytes 196612
  3.5 5.2 %copy-start.3 = (bf16[2048,16]{0,1:T(8,128)(2,1)S(1)}, bf16[2048,16]{0,1:T(8,128)(2,1)}, u32[]{:S(2)}) copy-start(bf16[2048,16]{0,1:T(8,128)(2,1)} %param.8) | copy-start | bytes 196612
  3.5 41.5 %copy-start.5 = (s32[1,64]{1,0:T(1,128)S(1)}, s32[1,64]{1,0:T(1,128)}, u32[]{:S(2)}) copy-start(s32[1,64]{1,0:T(1,128)} %param.10) | copy-start | bytes 772
  3.5 47.8 %all-to-all-start = ((bf16[4,256,1024]{2,1,0:T(8,128)(2,1)}), bf16[4,256,1024]{2,1,0:T(8,128)(2,1)S(1)}, u32[]{:S(2)}, u32[]{:S(2)}) async-start(bf16[4,256,1024]{2,1,0:T(8,128)(2,1)} %copy-done), calls=%async_computation | async-start | bytes 4194304 | tf_op jit(solution)/shard_map/all_to_all | solution.py:192
  40.9 10.4 %collective-permute-start = (bf16[256,1024]{1,0:T(8,128)(2,1)S(1)}, bf16[256,1024]{1,0:T(8,128)(2,1)S(1)}, u32[]{:S(2)}, u32[]{:S(2)}) collective-permute-start(bf16[256,1024]{1,0:T(8,128)(2,1)S(1)} %all_gather.6.own_ref), channel_id=1, source_target_pairs={{0,32},{32,0},{1,33},{33,1},{2,34},{34,2},{3,35},{35,3},{4,36},{36... | collective-permute-start | bytes 1572872 | tf_op jit(solution)/shard_map/ppermute | solution.py:219
  45.1 4.3 %collective-permute-start.1 = (s32[1,65]{1,0:T(1,128)S(1)}, s32[1,65]{1,0:T(1,128)S(1)}, u32[]{:S(2)}, u32[]{:S(2)}) collective-permute-start(s32[1,65]{1,0:T(1,128)S(1)} %pad_add_fusion.1), channel_id=1, source_target_pairs={{0,1},{1,0},{2,3},{3,2},{4,5},{5,4},{6,7},{7,6},{8,9},{9,8},{10,11... | collective-permute-start | bytes 788 | tf_op jit(solution)/shard_map/ppermute | solution.py:203
  54.1 10.1 %collective-permute-start.2 = (bf16[256,1024]{1,0:T(8,128)(2,1)S(1)}, bf16[256,1024]{1,0:T(8,128)(2,1)S(1)}, u32[]{:S(2)}, u32[]{:S(2)}) collective-permute-start(bf16[256,1024]{1,0:T(8,128)(2,1)S(1)} %get-tuple-element.11), channel_id=1, source_target_pairs={{0,2},{2,0},{1,3},{3,1},{4,6},{6,4},{5,7},{7,5},{8,10},{10,8},{9,1... | collective-permute-start | bytes 1572872 | tf_op jit(solution)/shard_map/ppermute | solution.py:240
  83.7 58.9 %copy-start.4 = (f32[32]{0:T(128)S(1)}, f32[32]{0:T(128)}, u32[]{:S(2)}) copy-start(f32[32]{0:T(128)} %param.11) | copy-start | bytes 388
  83.7 23.7 %all-to-all-start.2 = ((bf16[8,16,2048]{2,1,0:T(8,128)(2,1)}), bf16[8,16,2048]{2,1,0:T(8,128)(2,1)S(1)}, u32[]{:S(2)}, u32[]{:S(2)}) async-start(bf16[8,16,2048]{2,1,0:T(8,128)(2,1)} %broadcast_in_dim.16), calls=%async_computation.2 | async-start | bytes 1048576 | tf_op jit(solution)/shard_map/all_to_all | solution.py:192
  87.6 4.2 %collective-permute-start.3 = (bf16[16,128]{1,0:T(8,128)(2,1)S(1)}, bf16[16,128]{1,0:T(8,128)(2,1)S(1)}, u32[]{:S(2)}, u32[]{:S(2)}) collective-permute-start(bf16[16,128]{1,0:T(8,128)(2,1)S(1)} %get-tuple-element.13), channel_id=1, source_target_pairs={{0,64},{64,128},{128,192},{192,256},{256,320},{320,384},{384,448},... | collective-permute-start | bytes 12296 | tf_op jit(solution)/shard_map/ppermute | solution.py:247
  138.2 9.2 %all-to-all-start.4 = ((f32[8,8,128]{2,1,0:T(8,128)}), f32[8,8,128]{2,1,0:T(8,128)S(1)}, u32[]{:S(2)}, u32[]{:S(2)}) async-start(f32[8,8,128]{2,1,0:T(8,128)} %shard_map.82), calls=%async_computation.4 | async-start | bytes 65536 | tf_op jit(solution)/shard_map/all_to_all | solution.py:192

commit v5 on v4

--- a/solution.py
+++ b/solution.py
@@ -39,37 +39,35 @@
         out_ref[half * 2 + 1] = rows
 
 
-def project_kernel(place_ref, own_ref, other_ref, frames_ref, keep_ref, send_ref):
-    z0 = place_ref[0] & 1
-    c = place_ref[2]
-    frames = frames_ref[...]
-    own = lax.dot_general(own_ref[...], frames, NT, preferred_element_type=F32)
-    other = lax.dot_general(other_ref[...], frames, NT, preferred_element_type=F32)
-
-    def store(even, odd, keep_ref, send_ref, own_c):
-        for yh, acc in enumerate((even, odd)):
-            for z1 in range(2):
-                for yl in range(2):
-                    for half in range(2):
-                        for z2 in range(2):
-                            row = (z2 * 2 + z1) * 32 + half * 16 + yl * 8
-                            both = jnp.concatenate(
-                                [acc[row : row + 8], acc[row + 128 : row + 136]], axis=0
-                            )
-                            chunk = ((z1 * 2 + yh) * 2 + yl) * 4 + half * 2
-                            ref = keep_ref if z2 == own_c else send_ref
-                            ref[chunk * 8 : chunk * 8 + 16, :] = both.astype(BF)
-
-    for own_z0 in range(2):
-        for own_c in range(2):
-
-            @pl.when((z0 == own_z0) & (c == own_c))
-            def _(own_z0=own_z0, own_c=own_c):
-                pair = (own, other) if own_z0 == 0 else (other, own)
-                store(*pair, keep_ref, send_ref, own_c)
-
-
-def sum_kernel(parts_ref, basis_ref, tail_ref):
+def project_kernel(place_ref, panel_ref, frames_ref, keep_ref, send_ref):
+    acc = lax.dot_general(panel_ref[...], frames_ref[...], NT, preferred_element_type=F32)
+
+    def store(refs):
+        for z1 in range(2):
+            for yl in range(2):
+                for half in range(2):
+                    for z2 in range(2):
+                        row = (z2 * 2 + z1) * 32 + half * 16 + yl * 8
+                        both = jnp.concatenate(
+                            [acc[row : row + 8], acc[row + 128 : row + 136]], axis=0
+                        )
+                        at = ((z1 * 2 + yl) * 4 + half * 2) * 8
+                        refs[z2][at : at + 16, :] = both.astype(BF)
+
+    pl.when(place_ref[2] == 0)(lambda: store((keep_ref, send_ref)))
+    pl.when(place_ref[2] == 1)(lambda: store((send_ref, keep_ref)))
+
+
+def join_kernel(place_ref, keep_a, got_a, keep_b, got_b, out_ref):
+    own = place_ref[0] & 1
+    for yh, keep, got in ((own, keep_a, got_a), (1 - own, keep_b, got_b)):
+        for z0 in range(2):
+            rows = slice(z0 * 64, z0 * 64 + 64)
+            pair = keep[rows, :].astype(F32) + got[rows, :].astype(F32)
+            out_ref[z0 * 2 + yh] = pair.astype(BF)
+
+
+def sum_kernel(parts_ref, basis_ref, tail_ref, tiled_ref):
     for z0 in range(2):
         sums = []
         for yh in range(2):
@@ -80,27 +78,20 @@
         basis = jnp.concatenate(sums, axis=0)
         for rep in range(2):
             at = rep * 1024 + z0 * 512
-            basis_ref[:, at : at + 512] = basis[:, rep * 512 : (rep + 1) * 512].astype(BF)
+            block = basis[:, rep * 512 : (rep + 1) * 512].astype(BF)
+            basis_ref[:, at : at + 512] = block
+            for d in range(8):
+                tiled_ref[d, :, at : at + 512] = block
         if z0 == 1:
             lane = lax.broadcasted_iota(I32, (16, 128), 1)
             tail = jnp.where(lane < 64, pltpu.roll(basis[:, 384:512], 64, 1), basis[:, 896:])
             tail_ref[...] = tail.astype(BF)
 
 
-def cov_kernel(lags_ref, place_ref, seg_ref, left_ref, right_ref, out_ref):
+def mask_kernel(lags_ref, place_ref, seg_ref, out_ref):
     first = (place_ref[0] >> 1) * 1024
-    perm = one_hot(
-        128,
-        128,
-        lambda r, c: c
-        == (r >> 5) * 32 + ((r >> 1) & 1) * 16 + ((r >> 2) & 7) * 2 + (r & 1),
-    )
-    now = jnp.dot(perm, right_ref[...], preferred_element_type=F32)
-    now_bf = now.astype(BF)
     tri = lax.broadcasted_iota(I32, (64, 64), 1) <= lax.broadcasted_iota(I32, (64, 64), 0)
     seg = seg_ref[...].astype(F32)
-    tails = left_ref[:, 2048:].astype(F32)
-    keep, keep_end, lagged = [], [], []
     for rep in range(2):
         lag = lags_ref[rep]
         ends = jnp.sum(jnp.where(tri, seg[rep : rep + 1, :], 0.0), axis=1, keepdims=True)
@@ -109,17 +100,31 @@
         ahead = (pos + lag).astype(F32)
         behind = (pos - lag).astype(F32)
         cut = jnp.where((ends > here) & (ends <= ahead), 1.0, 0.0)
-        keep.append(1.0 - jnp.max(cut, axis=0, keepdims=True))
         cut_end = jnp.where((ends > behind) & (ends <= here), 1.0, 0.0)
         inside = jnp.where(behind >= 0.0, 1.0, 0.0)
-        keep_end.append((1.0 - jnp.max(cut_end, axis=0, keepdims=True)) * inside)
+        at = slice(rep * 1024, (rep + 1) * 1024)
+        out_ref[0:1, at] = 1.0 - jnp.max(cut, axis=0, keepdims=True)
+        out_ref[1:2, at] = (1.0 - jnp.max(cut_end, axis=0, keepdims=True)) * inside
+
+
+def cov_kernel(lags_ref, mask_ref, left_ref, right_ref, out_ref):
+    perm = one_hot(
+        128,
+        128,
+        lambda r, c: c
+        == (r >> 5) * 32 + ((r >> 1) & 1) * 16 + ((r >> 2) & 7) * 2 + (r & 1),
+    )
+    now = jnp.dot(perm, right_ref[...], preferred_element_type=F32)
+    now_bf = now.astype(BF)
+    tails = left_ref[:, 2048:].astype(F32)
+    lagged = []
+    for rep in range(2):
         tail = tails if rep == 1 else pltpu.roll(tails, 64, 1)
         block = left_ref[:, rep * 1024 : (rep + 1) * 1024].astype(F32)
         ext = jnp.concatenate([tail, block], axis=1)
-        lagged.append(pltpu.roll(ext, lag + 1024, 1)[:, :1024].astype(BF))
-    keep = jnp.concatenate(keep, axis=1)
-    keep_end = jnp.concatenate(keep_end, axis=1)
+        lagged.append(pltpu.roll(ext, lags_ref[rep] + 1024, 1)[:, :1024].astype(BF))
     lagged = jnp.concatenate(lagged, axis=1)
+    keep, keep_end = mask_ref[0:1, :], mask_ref[1:2, :]
     left = left_ref[:, :2048]
     start_bf, end_bf = keep.astype(BF), keep_end.astype(BF)
     for m, lhs in enumerate((left * start_bf, lagged * end_bf, left * end_bf)):
@@ -205,11 +210,11 @@
     halves = pl.pallas_call(
         halves_kernel,
         grid=(4,),
-        out_shape=jax.ShapeDtypeStruct((4, 256, 1024), BF),
+        out_shape=pltpu.HBM((4, 256, 1024), BF),
         in_specs=[pl.BlockSpec((1, 64, 2048), lambda i: (0, i, 0))],
         out_specs=pl.BlockSpec((4, 64, 1024), lambda i: (0, i, 0)),
         compiler_params=VMEM,
-    )(frames)
+    )(pltpu.with_memory_space_constraint(frames, pltpu.HBM))
     frames_h = all_to_all(halves, ("yl", "yh")).reshape(1024, 1024)
 
     packed = call(
@@ -217,46 +222,53 @@
     )
     panel_own = lax.all_gather(packed, Z8, axis=0, tiled=True)
     panel_other = lax.ppermute(panel_own, "z0", [(0, 1), (1, 0)])
-    panel_other, other = lax.optimization_barrier((panel_other, other))
     both = jnp.where(
         yl == 0, jnp.concatenate([mine, other], axis=0), jnp.concatenate([other, mine], axis=0)
     )
-
-    whole = pl.BlockSpec((256, 1024), lambda i: (0, 0))
-    column = pl.BlockSpec((256, 256), lambda i: (0, i))
-    keep, send = pl.pallas_call(
-        project_kernel,
-        grid=(4,),
-        out_shape=[jax.ShapeDtypeStruct((256, 1024), BF)] * 2,
-        in_specs=[
-            pl.BlockSpec(memory_space=pltpu.SMEM),
-            whole,
-            whole,
-            pl.BlockSpec((256, 1024), lambda i: (i, 0)),
-        ],
-        out_specs=[column, column],
-        compiler_params=VMEM,
-    )(place, panel_own, panel_other, frames_h)
-    got = lax.ppermute(send, "c", [(0, 1), (1, 0)])
-    pairs = (keep.astype(F32) + got.astype(F32)).astype(BF)
+    run_lags = both[:, 0]
+    masks = call(mask_kernel, [((8, 2048), F32)], run_lags, place, both[:, 1:], smem=2)
+
+    def project(panel):
+        column = pl.BlockSpec((128, 256), lambda i: (0, i))
+        keep, send = pl.pallas_call(
+            project_kernel,
+            grid=(4,),
+            out_shape=[jax.ShapeDtypeStruct((128, 1024), BF)] * 2,
+            in_specs=[
+                pl.BlockSpec(memory_space=pltpu.SMEM),
+                pl.BlockSpec((256, 1024), lambda i: (0, 0)),
+                pl.BlockSpec((256, 1024), lambda i: (i, 0)),
+            ],
+            out_specs=[column, column],
+            compiler_params=VMEM,
+        )(place, panel, frames_h)
+        return keep, lax.ppermute(send, "c", [(0, 1), (1, 0)])
+
+    first = project(panel_own)
+    panel_other, masks, run_lags, first = lax.optimization_barrier(
+        (panel_other, masks, run_lags, first)
+    )
+    second = project(panel_other)
+    pairs = call(join_kernel, [((4, 64, 1024), BF)], place, *first, *second, smem=1)
     parts = all_to_all(pairs.reshape(32, 8, 1024), ("z0", "yh", "yl", "x"))
-    basis, tail = call(
-        sum_kernel, [((16, 2048), BF), ((16, 128), BF)], parts.reshape(2, 2, 2, 4, 8, 1024)
+    basis, tail, tiled = call(
+        sum_kernel,
+        [((16, 2048), BF), ((16, 128), BF), ((8, 16, 2048), BF)],
+        parts.reshape(2, 2, 2, 4, 8, 1024),
     )
 
     before = lax.ppermute(tail, Z8, [(i, i + 1) for i in range(7)])
-    right = all_to_all(jnp.broadcast_to(basis[None], (8, 16, 2048)), ("z0", "yh", "yl"))
+    right = all_to_all(tiled, ("z0", "yh", "yl"))
     left = lax.all_gather(jnp.concatenate([basis, before], axis=1), FE, axis=0, tiled=True)
 
     terms = call(
         cov_kernel,
         [((8, 56, 128), F32)],
-        both[:, 0],
-        place,
-        both[:, 1:],
+        run_lags,
+        masks,
         left,
         right.reshape(128, 2048),
-        smem=2,
+        smem=1,
     )
     rows = call(rows_kernel, [((8, 8, 128), F32)], all_to_all(terms, Z8))
     by_row = all_to_all(rows, FE)

time: 149 us -> 154 us (1.034)
  Pallas kernels: 7.81 us -> 15.7 us
  local copies, waits for them, and re-layouts: 3.67 us -> 0.29 us
  waiting for transfers between devices: 10.6 us -> 7.93 us
  starting transfers between devices: 31.1 us -> 33.5 us
    pallas_call x2 -> x3, Pallas kernels: 3.08 us -> 8.58 us  [the longest x2 5.01 us: project(): pl.pallas_call(project_kernel, grid=(4,), out_shape=[jax.ShapeDtypeStruct...]
    unnamed x12 -> x8, local copies, waits for them, and re-layouts: 2.56 us -> 0.01 us
    pallas_call x5 -> x7, Pallas kernels: 4.74 us -> 7.15 us  [call(): pl.pallas_call(kernel, out_shape=shapes, in_specs=specs, out_specs=outs,...]
    ppermute x1, waiting for transfers between devices: 1.96 us -> 0.01 us  [local(): panel_other = lax.ppermute(panel_own, 'z0', [(0, 1), (1, 0)])]
    ppermute x1 -> x2, starting transfers between devices: 8.61 us -> 10.2 us  [project(): return (keep, lax.ppermute(send, 'c', [(0, 1), (1, 0)]))]
  transfers between devices with their start and end apart: 7 -> 8, of which waited for: 5 -> 4; matrix products, arithmetic and copies ran while one was open for 0% -> 0% of each run, Pallas kernels for 0% -> 3%
where the time goes in v5:
time: 154 us; the launch traced here: 153 us
  blocking collectives  93.9 us (61%)
  starting transfers between devices  33.5 us (22%)
  Pallas kernels  15.7 us (10%)
  waiting for transfers between devices  7.93 us (5%)
    all_to_all x2, blocking collectives, all_to_all(): return lax.all_to_all(x, axes, split_axis=0, concat_axis=0, tiled=True)  45.2 us
    all_gather x1, blocking collectives, local(): panel_own = lax.all_gather(packed, Z8, axis=0, tiled=True)  33 us
    all_gather x1, blocking collectives, local(): lax.all_gather(jnp.concatenate([basis, before], axis=1), FE, axis=0, tile...  15.7 us
    all_to_all x3, starting transfers between devices, all_to_all(): return lax.all_to_all(x, axes, split_axis=0, concat_axis=0, tiled=True)  13.5 us
    ppermute x2, starting transfers between devices, project(): return (keep, lax.ppermute(send, 'c', [(0, 1), (1, 0)]))  10.2 us
    pallas_call x7, Pallas kernels, call(): pl.pallas_call(kernel, out_shape=shapes, in_specs=specs, out_specs=outs,...  7.15 us
    pallas_call x2, Pallas kernels, project(): pl.pallas_call(project_kernel, grid=(4,), out_shape=[jax.ShapeDtypeStruct...  5.01 us
    all_to_all x3, waiting for transfers between devices, all_to_all(): return lax.all_to_all(x, axes, split_axis=0, concat_axis=0, tiled=True)  4.65 us
  transfers between devices with their start and end apart: 8, of which 4 were waited for; matrix products, arithmetic and copies ran while one was open for 0% of the time, Pallas kernels for 3%

profile of v5, /device:TPU:1, one launch (start us, length us, event | category | flops | bytes accessed | tf_op | source)
XLA Modules:
  0.0 152.9 jit_solution(13479924438291832929)
XLA Ops:
  0.6 3.6 %shard_map.79 = bf16[4,256,1024]{2,1,0:T(8,128)(2,1)} custom-call(bf16[1,256,2048]{2,1,0:T(8,128)(2,1)} %frames_ref.1), custom_call_target="tpu_custom_call" | custom-call | tf_op jit(solution)/shard_map/pallas_call | solution.py:210
  4.2 5.1 %all-to-all-start = ((bf16[4,256,1024]{2,1,0:T(8,128)(2,1)}), bf16[4,256,1024]{2,1,0:T(8,128)(2,1)S(1)}, u32[]{:S(2)}, u32[]{:S(2)}) async-start(bf16[4,256,1024]{2,1,0:T(8,128)(2,1)} %shard_map.79), calls=%async_computation | async-start | bytes 4194304 | tf_op jit(solution)/shard_map/all_to_all | solution.py:197
  9.5 33.0 %all_gather.6.panel_ref = bf16[256,1024]{1,0:T(8,128)(2,1)S(1)} all-gather(bf16[32,1024]{1,0:T(8,128)(2,1)S(1)} %shard_map.77), channel_id=1, replica_groups=mesh['z3'=2,'z2'=2,'z1'=2,'z0'=2,'yh'=2,'x'=4,'c'=2,'yl'=2] {'z3','z2','..., dimensions={0}, use_global_device_ids=true | all-gather | bytes 589824 | tf_op jit(solution)/shard_map/all_gather | solution.py:223
  42.5 2.6 %collective-permute-start = (bf16[256,1024]{1,0:T(8,128)(2,1)S(1)}, bf16[256,1024]{1,0:T(8,128)(2,1)S(1)}, u32[]{:S(2)}, u32[]{:S(2)}) collective-permute-start(bf16[256,1024]{1,0:T(8,128)(2,1)S(1)} %all_gather.6.panel_ref), channel_id=1, source_target_pairs={{0,32},{32,0},{1,33},{33,1},{2,34},{34,2},{3,35},{35,3},{4,36},{36... | collective-permute-start | bytes 1572872 | tf_op jit(solution)/shard_map/ppermute | solution.py:224
  45.9 2.9 %shard_map.80 = (bf16[128,1024]{1,0:T(8,128)(2,1)S(1)}, bf16[128,1024]{1,0:T(8,128)(2,1)}) custom-call(s32[3]{0:T(128)S(1)} %pad_add_fusion.place_ref.refs_0_, bf16[256,1024]{1,0:T(8,128)(2,1)S(1)} %all_gather.6.panel_ref, bf16[1024,1024]{1,0:T(8,128)(2,1)S(1)} %bitcast.15), custom_call_target="tpu_custom_call" | custom-call | tf_op jit(solution)/shard_map/pallas_call | solution.py:233
  48.8 7.5 %collective-permute-start.2 = (bf16[128,1024]{1,0:T(8,128)(2,1)}, bf16[128,1024]{1,0:T(8,128)(2,1)}, u32[]{:S(2)}, u32[]{:S(2)}) collective-permute-start(bf16[128,1024]{1,0:T(8,128)(2,1)} %get-tuple-element.15), channel_id=1, source_target_pairs={{0,2},{2,0},{1,3},{3,1},{4,6},{6,4},{5,7},{7,5},{8,10},{10,8},{9,1... | collective-permute-start | bytes 786440 | tf_op jit(solution)/shard_map/ppermute | solution.py:245
  56.4 4.1 %collective-permute-start.1 = (s32[1,65]{1,0:T(1,128)S(1)}, s32[1,65]{1,0:T(1,128)S(1)}, u32[]{:S(2)}, u32[]{:S(2)}) collective-permute-start(s32[1,65]{1,0:T(1,128)S(1)} %pad_add_fusion.1), channel_id=1, source_target_pairs={{0,1},{1,0},{2,3},{3,2},{4,5},{5,4},{6,7},{7,6},{8,9},{9,8},{10,11... | collective-permute-start | bytes 788 | tf_op jit(solution)/shard_map/ppermute | solution.py:208
  60.5 0.9 collective-permute-done.1
  61.6 0.8 shard_map.78.mask_ref
  62.5 2.1 %shard_map.81 = (bf16[128,1024]{1,0:T(8,128)(2,1)S(1)}, bf16[128,1024]{1,0:T(8,128)(2,1)S(1)}) custom-call(s32[3]{0:T(128)S(1)} %pad_add_fusion.place_ref.refs_0_, bf16[256,1024]{1,0:T(8,128)(2,1)S(1)} %collective-permute-done.panel_ref, bf16[1024,1024]{1,0:T(8,128)(2,1)S(1)} %bitcast.16), custom_call_target="tpu_custom_call" | custom-call | tf_op jit(solution)/shard_map/pallas_call | solution.py:233
  64.6 2.8 %collective-permute-start.3 = (bf16[128,1024]{1,0:T(8,128)(2,1)S(1)}, bf16[128,1024]{1,0:T(8,128)(2,1)S(1)}, u32[]{:S(2)}, u32[]{:S(2)}) collective-permute-start(bf16[128,1024]{1,0:T(8,128)(2,1)S(1)} %get-tuple-element.22), channel_id=1, source_target_pairs={{0,2},{2,0},{1,3},{3,1},{4,6},{6,4},{5,7},{7,5},{8,10},{10,8},{9,1... | collective-permute-start | bytes 786440 | tf_op jit(solution)/shard_map/ppermute | solution.py:245
  67.4 1.1 collective-permute-done.3.got_b
  68.5 1.1 shard_map.82
  69.6 17.6 %all_to_all.25 = bf16[32,8,1024]{2,1,0:T(8,128)(2,1)S(1)} all-to-all(bf16[32,8,1024]{2,1,0:T(8,128)(2,1)S(1)} %bitcast.18), channel_id=1, replica_groups=mesh['z3'=2,'z2'=2,'z1'=2,'z0'=2,'yh'=2,'x'=4,'c'=2,'yl'=2] {'z0','yh','..., dimensions={0} | all-to-all | bytes 1048576 | tf_op jit(solution)/shard_map/all_to_all | solution.py:197
  87.2 0.9 shard_map.83
  88.1 3.8 %all-to-all-start.2 = ((bf16[8,16,2048]{2,1,0:T(8,128)(2,1)}), bf16[8,16,2048]{2,1,0:T(8,128)(2,1)S(1)}, u32[]{:S(2)}, u32[]{:S(2)}) async-start(bf16[8,16,2048]{2,1,0:T(8,128)(2,1)} %get-tuple-element.25), calls=%async_computation.2 | async-start | bytes 1048576 | tf_op jit(solution)/shard_map/all_to_all | solution.py:197
  91.9 3.0 %collective-permute-start.4 = (bf16[16,128]{1,0:T(8,128)(2,1)S(1)}, bf16[16,128]{1,0:T(8,128)(2,1)S(1)}, u32[]{:S(2)}, u32[]{:S(2)}) collective-permute-start(bf16[16,128]{1,0:T(8,128)(2,1)S(1)} %get-tuple-element.24), channel_id=1, source_target_pairs={{0,64},{64,128},{128,192},{192,256},{256,320},{320,384},{384,448},... | collective-permute-start | bytes 12296 | tf_op jit(solution)/shard_map/ppermute | solution.py:260
  94.9 1.2 collective-permute-done.4
  96.2 15.7 %all_gather.7.left_ref = bf16[128,2176]{1,0:T(8,128)(2,1)S(1)} all-gather(bf16[16,2176]{1,0:T(8,128)(2,1)S(1)} %pad_maximum_fusion), channel_id=1, replica_groups=mesh['z3'=2,'z2'=2,'z1'=2,'z0'=2,'yh'=2,'x'=4,'c'=2,'yl'=2] {'x','c'}, dimensions={0}, use_global_device_ids=true | all-gather | bytes 626688 | tf_op jit(solution)/shard_map/all_gather | solution.py:262
  111.8 2.2 %shard_map.84 = f32[8,56,128]{2,1,0:T(8,128)S(1)} custom-call(s32[2]{0:T(128)S(1)} %slice_reduce_fusion.lags_ref, f32[8,2048]{1,0:T(8,128)S(1)} %shard_map.78.mask_ref, bf16[128,2176]{1,0:T(8,128)(2,1)S(1)} %all_gather.7.left_ref, bf16[128,2048]{1,0:T(8,128)(2,1)S(1)} %bitcast.17), custom_call_target="tpu_custom_call" | custom-call | tf_op jit(solution)/shard_map/pallas_call | solution.py:190
  114.1 27.6 %all_to_all.26.parts_ref = f32[8,56,128]{2,1,0:T(8,128)S(1)} all-to-all(f32[8,56,128]{2,1,0:T(8,128)S(1)} %shard_map.84), channel_id=1, replica_groups=mesh['z3'=2,'z2'=2,'z1'=2,'z0'=2,'yh'=2,'x'=4,'c'=2,'yl'=2] {'z3','z2','..., dimensions={0} | all-to-all | bytes 458752 | tf_op jit(solution)/shard_map/all_to_all | solution.py:197
  142.3 4.5 %all-to-all-start.4 = ((f32[8,8,128]{2,1,0:T(8,128)}), f32[8,8,128]{2,1,0:T(8,128)S(1)}, u32[]{:S(2)}, u32[]{:S(2)}) async-start(f32[8,8,128]{2,1,0:T(8,128)} %shard_map.85), calls=%async_computation.4 | async-start | bytes 65536 | tf_op jit(solution)/shard_map/all_to_all | solution.py:197
  146.9 4.6 %all-to-all-done.4.refs_1_ = f32[8,8,128]{2,1,0:T(8,128)S(1)} async-done(((f32[8,8,128]{2,1,0:T(8,128)}), f32[8,8,128]{2,1,0:T(8,128)S(1)}, u32[]{:S(2)}, u32[]{:S(2)}) %all-to-all-start.4) | async-done | bytes 32800 | tf_op jit(solution)/shard_map/all_to_all | solution.py:197
  151.6 1.4 shard_map.86
  (21 shorter events, 1.3 us)
Async XLA Ops:
  4.2 5.2 %copy-start = (bf16[2048,16]{0,1:T(8,128)(2,1)S(1)}, bf16[2048,16]{0,1:T(8,128)(2,1)}, u32[]{:S(2)}) copy-start(bf16[2048,16]{0,1:T(8,128)(2,1)} %param.7) | copy-start | bytes 196612
  4.2 5.2 %copy-start.1 = (bf16[2048,16]{0,1:T(8,128)(2,1)S(1)}, bf16[2048,16]{0,1:T(8,128)(2,1)}, u32[]{:S(2)}) copy-start(bf16[2048,16]{0,1:T(8,128)(2,1)} %param.8) | copy-start | bytes 196612
  4.2 41.7 %all-to-all-start = ((bf16[4,256,1024]{2,1,0:T(8,128)(2,1)}), bf16[4,256,1024]{2,1,0:T(8,128)(2,1)S(1)}, u32[]{:S(2)}, u32[]{:S(2)}) async-start(bf16[4,256,1024]{2,1,0:T(8,128)(2,1)} %shard_map.79), calls=%async_computation | async-start | bytes 4194304 | tf_op jit(solution)/shard_map/all_to_all | solution.py:197
  9.3 46.9 %copy-start.3 = (s32[1,64]{1,0:T(1,128)S(1)}, s32[1,64]{1,0:T(1,128)}, u32[]{:S(2)}) copy-start(s32[1,64]{1,0:T(1,128)} %param.10) | copy-start | bytes 772
  42.5 20.0 %collective-permute-start = (bf16[256,1024]{1,0:T(8,128)(2,1)S(1)}, bf16[256,1024]{1,0:T(8,128)(2,1)S(1)}, u32[]{:S(2)}, u32[]{:S(2)}) collective-permute-start(bf16[256,1024]{1,0:T(8,128)(2,1)S(1)} %all_gather.6.panel_ref), channel_id=1, source_target_pairs={{0,32},{32,0},{1,33},{33,1},{2,34},{34,2},{3,35},{35,3},{4,36},{36... | collective-permute-start | bytes 1572872 | tf_op jit(solution)/shard_map/ppermute | solution.py:224
  48.8 13.7 %collective-permute-start.2 = (bf16[128,1024]{1,0:T(8,128)(2,1)}, bf16[128,1024]{1,0:T(8,128)(2,1)}, u32[]{:S(2)}, u32[]{:S(2)}) collective-permute-start(bf16[128,1024]{1,0:T(8,128)(2,1)} %get-tuple-element.15), channel_id=1, source_target_pairs={{0,2},{2,0},{1,3},{3,1},{4,6},{6,4},{5,7},{7,5},{8,10},{10,8},{9,1... | collective-permute-start | bytes 786440 | tf_op jit(solution)/shard_map/ppermute | solution.py:245
  56.4 5.0 %collective-permute-start.1 = (s32[1,65]{1,0:T(1,128)S(1)}, s32[1,65]{1,0:T(1,128)S(1)}, u32[]{:S(2)}, u32[]{:S(2)}) collective-permute-start(s32[1,65]{1,0:T(1,128)S(1)} %pad_add_fusion.1), channel_id=1, source_target_pairs={{0,1},{1,0},{2,3},{3,2},{4,5},{5,4},{6,7},{7,6},{8,9},{9,8},{10,11... | collective-permute-start | bytes 788 | tf_op jit(solution)/shard_map/ppermute | solution.py:208
  64.6 3.9 %collective-permute-start.3 = (bf16[128,1024]{1,0:T(8,128)(2,1)S(1)}, bf16[128,1024]{1,0:T(8,128)(2,1)S(1)}, u32[]{:S(2)}, u32[]{:S(2)}) collective-permute-start(bf16[128,1024]{1,0:T(8,128)(2,1)S(1)} %get-tuple-element.22), channel_id=1, source_target_pairs={{0,2},{2,0},{1,3},{3,1},{4,6},{6,4},{5,7},{7,5},{8,10},{10,8},{9,1... | collective-permute-start | bytes 786440 | tf_op jit(solution)/shard_map/ppermute | solution.py:245
  88.1 58.7 %copy-start.2 = (f32[32]{0:T(128)S(1)}, f32[32]{0:T(128)}, u32[]{:S(2)}) copy-start(f32[32]{0:T(128)} %param.11) | copy-start | bytes 388
  88.1 23.7 %all-to-all-start.2 = ((bf16[8,16,2048]{2,1,0:T(8,128)(2,1)}), bf16[8,16,2048]{2,1,0:T(8,128)(2,1)S(1)}, u32[]{:S(2)}, u32[]{:S(2)}) async-start(bf16[8,16,2048]{2,1,0:T(8,128)(2,1)} %get-tuple-element.25), calls=%async_computation.2 | async-start | bytes 1048576 | tf_op jit(solution)/shard_map/all_to_all | solution.py:197
  91.9 4.3 %collective-permute-start.4 = (bf16[16,128]{1,0:T(8,128)(2,1)S(1)}, bf16[16,128]{1,0:T(8,128)(2,1)S(1)}, u32[]{:S(2)}, u32[]{:S(2)}) collective-permute-start(bf16[16,128]{1,0:T(8,128)(2,1)S(1)} %get-tuple-element.24), channel_id=1, source_target_pairs={{0,64},{64,128},{128,192},{192,256},{256,320},{320,384},{384,448},... | collective-permute-start | bytes 12296 | tf_op jit(solution)/shard_map/ppermute | solution.py:260
  142.3 9.3 %all-to-all-start.4 = ((f32[8,8,128]{2,1,0:T(8,128)}), f32[8,8,128]{2,1,0:T(8,128)S(1)}, u32[]{:S(2)}, u32[]{:S(2)}) async-start(f32[8,8,128]{2,1,0:T(8,128)} %shard_map.85), calls=%async_computation.4 | async-start | bytes 65536 | tf_op jit(solution)/shard_map/all_to_all | solution.py:197

commit v6 on v5

v6 whole, which is shorter than its diff:
```python
import jax
import jax.numpy as jnp
import numpy as np
from jax import lax
from jax.experimental import pallas as pl
from jax.experimental.pallas import tpu as pltpu
from jax.sharding import Mesh, PartitionSpec as P

BF = jnp.bfloat16
F32 = jnp.float32
I32 = jnp.int32
HI = lax.Precision.HIGHEST
NT = (((1,), (1,)), ((), ()))
VMEM = pltpu.CompilerParams(vmem_limit_bytes=48 * 1024 * 1024)

Z = ("z3", "z2", "z1", "z0")
Z8 = ("z3", "z2", "z1")
FE = ("x", "c")


def one_hot(rows, cols, hit):
    r = lax.broadcasted_iota(I32, (rows, cols), 0)
    c = lax.broadcasted_iota(I32, (rows, cols), 1)
    return jnp.where(hit(r, c), 1.0, 0.0).astype(BF)


def pack_kernel(yl_ref, low_ref, high_ref, out_ref):
    off = pl.multiple_of(yl_ref[0] * 1024, 1024)
    src = one_hot(16, 16, lambda r, c: c == ((r >> 1) & 3) * 4 + (r >> 3) * 2 + (r & 1))
    for half, ref in enumerate((low_ref, high_ref)):
        rows = jnp.dot(src, ref[:, pl.ds(off, 1024)], preferred_element_type=F32)
        out_ref[half * 16 : half * 16 + 16, :] = rows.astype(BF)


def halves_kernel(lag_ref, seg_ref, frames_ref, out_ref, info_ref, sems):
    copies = []
    for i in range(4):
        half = frames_ref.at[0, :, pl.ds((i // 2) * 1024, 1024)]
        copies.append(pltpu.make_async_copy(half, out_ref.at[i, pl.ds(0, 256)], sems.at[i]))
    for copy in copies:
        copy.start()
    seg = jnp.concatenate([seg_ref[...], jnp.zeros((1, 64), I32)], axis=1)
    row = lax.broadcasted_iota(I32, (16, 128), 0)
    info = jnp.where(row == 0, seg >> 8, jnp.where(row == 1, seg & 255, lag_ref[0]))
    info_ref[:, :128] = info.astype(F32).astype(BF)
    info_ref[:, 128:] = jnp.zeros((16, 896), BF)
    for i in range(4):
        copy = pltpu.make_async_copy(info_ref, out_ref.at[i, pl.ds(256, 16)], sems.at[4 + i])
        copy.start()
        copies.append(copy)
    for copy in copies:
        copy.wait()


def project_kernel(place_ref, own_ref, other_ref, frames_ref, tails_ref, keep_ref, send_ref):
    own_yh = place_ref[0] & 1
    for t in range(5):
        frames = frames_ref[t, :256] if t < 4 else tails_ref[...]
        lanes = slice(t * 256, t * 256 + 256) if t < 4 else slice(1024, 1152)
        for yh, panel_ref in ((own_yh, own_ref), (1 - own_yh, other_ref)):
            acc = lax.dot_general(panel_ref[...], frames, NT, preferred_element_type=F32)

            def store(refs, acc=acc, yh=yh, lanes=lanes):
                for z1 in range(2):
                    for yl in range(2):
                        for half in range(2):
                            for z2 in range(2):
                                row = (z2 * 2 + z1) * 32 + half * 16 + yl * 8
                                both = jnp.concatenate(
                                    [acc[row : row + 8], acc[row + 128 : row + 136]], axis=0
                                )
                                at = (yl * 4 + half * 2) * 8
                                refs[z2][z1 * 2 + yh, at : at + 16, lanes] = both.astype(BF)

            pl.when(place_ref[2] == 0)(lambda store=store: store((keep_ref, send_ref)))
            pl.when(place_ref[2] == 1)(lambda store=store: store((send_ref, keep_ref)))


def sum_kernel(parts_ref, basis_ref, tiled_ref):
    for z0 in range(2):
        sums = []
        for yh in range(2):
            total = parts_ref[z0, yh, 0, 0].astype(F32)
            for i in range(1, 8):
                total = total + parts_ref[z0, yh, i // 4, i % 4].astype(F32)
            sums.append(total)
        basis = jnp.concatenate(sums, axis=0).astype(BF)
        for rep in range(2):
            at = rep * 1024 + z0 * 512
            block = basis[:, rep * 512 : (rep + 1) * 512]
            basis_ref[:, at : at + 512] = block
            for d in range(8):
                tiled_ref[d, :, at : at + 512] = block
        if z0 == 0:
            basis_ref[:, 2048:] = basis[:, 1024:]


def mask_kernel(place_ref, info_ref, out_ref):
    first = (place_ref[0] >> 1) * 1024
    tri = lax.broadcasted_iota(I32, (64, 64), 1) <= lax.broadcasted_iota(I32, (64, 64), 0)
    for rep in range(2):
        info = info_ref[rep].astype(F32)
        seg = info[0:1, :64] * 256.0 + info[1:2, :64]
        lag = info[2:3, 0:1]
        ends = jnp.sum(jnp.where(tri, seg, 0.0), axis=1, keepdims=True)
        here = (lax.broadcasted_iota(I32, (1, 1024), 1) + first).astype(F32)
        ahead = here + lag
        behind = here - lag
        cut = jnp.where((ends > here) & (ends <= ahead), 1.0, 0.0)
        cut_end = jnp.where((ends > behind) & (ends <= here), 1.0, 0.0)
        inside = jnp.where(behind >= 0.0, 1.0, 0.0)
        at = slice(rep * 1024, (rep + 1) * 1024)
        out_ref[0:1, at] = 1.0 - jnp.max(cut, axis=0, keepdims=True)
        out_ref[1:2, at] = (1.0 - jnp.max(cut_end, axis=0, keepdims=True)) * inside
        out_ref[2 + rep : 3 + rep, :] = jnp.broadcast_to(lag, (1, 2048))


def cov_kernel(mask_ref, left_ref, right_ref, out_ref):
    perm = one_hot(
        128,
        128,
        lambda r, c: c
        == (r >> 5) * 32 + ((r >> 1) & 1) * 16 + ((r >> 2) & 7) * 2 + (r & 1),
    )
    now = jnp.dot(perm, right_ref[...], preferred_element_type=F32)
    now_bf = now.astype(BF)
    lane = lax.broadcasted_iota(I32, (128, 128), 1)
    lagged = []
    for rep in range(2):
        lag = jnp.max(mask_ref[2 + rep : 3 + rep, :128]).astype(I32)
        tails = left_ref[:, 2048:].astype(F32)
        before = pltpu.roll(tails, lag if rep == 1 else lag + 64, 1)
        for j in range(8):
            at = rep * 1024 + j * 128
            block = pltpu.roll(left_ref[:, at : at + 128].astype(F32), lag, 1)
            lagged.append(jnp.where(lane < lag, before, block).astype(BF))
            before = block
    lagged = jnp.concatenate(lagged, axis=1)
    keep, keep_end = mask_ref[0:1, :], mask_ref[1:2, :]
    left = left_ref[:, :2048]
    start_bf, end_bf = keep.astype(BF), keep_end.astype(BF)
    for m, lhs in enumerate((left * start_bf, lagged * end_bf, left * end_bf)):
        block = lax.dot_general(lhs, now_bf, NT, preferred_element_type=F32)
        for d in range(8):
            out_ref[d, m * 16 : (m + 1) * 16, :] = block[d * 16 : (d + 1) * 16, :]
    var = lax.dot_general(
        jnp.ones((8, 2048), F32), now * now * keep_end, NT, precision=HI, preferred_element_type=F32
    )
    for d in range(8):
        out_ref[d, 48:56, :] = var


def rows_kernel(parts_ref, out_ref):
    total = parts_ref[0]
    for d in range(1, 8):
        total = total + parts_ref[d]
    for f in range(8):
        for m in range(3):
            src = m * 16 + f * 2
            out_ref[f, m * 2 : m * 2 + 2, :] = total[src : src + 2, :]
        out_ref[f, 6:8, :] = total[48:50, :]


def final_kernel(scale, place_ref, parts_ref, ridge_ref, row_ref, cov_ref, score_ref):
    first = place_ref[1]
    ridge = ridge_ref[...]
    lane = lax.broadcasted_iota(I32, (2, 128), 1)
    row = lax.broadcasted_iota(I32, (2, 128), 0)
    diag = jnp.zeros((2, 1), F32)
    weighted = [jnp.zeros((32, 128), F32) for _ in range(2)]
    for f in range(8):
        total = parts_ref[f] * scale
        for m in range(3):
            cov_ref[m, :, f * 128 : (f + 1) * 128] = total[m * 2 : m * 2 + 2, :]
        own = lane + f * 128 == first + row
        diag = diag + jnp.sum(jnp.where(own, total[0:2, :], 0.0), axis=1, keepdims=True)
        inverse = 1.0 / (total[6:7, :] + ridge)
        for e in range(2):
            cross = total[2 + e : 3 + e, :]
            weighted[e] = weighted[e] + (cross * cross) * inverse
    ones = jnp.ones((8, 128), F32)
    pad = jnp.zeros((96, 128), F32)
    score = [
        lax.dot_general(
            ones,
            jnp.concatenate([w, pad], axis=0),
            NT,
            precision=HI,
            preferred_element_type=F32,
        )[0:1, :32]
        for w in weighted
    ]
    for e in range(2):
        score_ref[e : e + 1, :] = score[e] / (diag[e : e + 1, :] + row_ref[...])


def call(kernel, out, *args, smem=0, **kw):
    specs = [pl.BlockSpec(memory_space=pltpu.SMEM)] * smem
    specs += [pl.BlockSpec(memory_space=pltpu.VMEM)] * (len(args) - smem)
    shapes = [jax.ShapeDtypeStruct(*o) for o in out]
    outs = [pl.BlockSpec(memory_space=pltpu.VMEM)] * len(out)
    got = pl.pallas_call(
        kernel, out_shape=shapes, in_specs=specs, out_specs=outs, compiler_params=VMEM
    )(*args)
    return got[0] if len(out) == 1 else got


def all_to_all(x, axes):
    return lax.all_to_all(x, axes, split_axis=0, concat_axis=0, tiled=True)


def local(frames, panel_low, panel_high, lags, seg_lengths, ridge):
    z = lax.axis_index(Z).astype(I32)
    yl = lax.axis_index("yl").astype(I32)
    c = lax.axis_index("c").astype(I32)
    own_first = ((z * 2 + lax.axis_index("yh")) * 8 + lax.axis_index(FE)) * 4 + yl * 2
    place = jnp.stack([z, own_first.astype(I32), c])

    halves = pl.pallas_call(
        halves_kernel,
        out_shape=pltpu.HBM((4, 272, 1024), BF),
        in_specs=[
            pl.BlockSpec(memory_space=pltpu.SMEM),
            pl.BlockSpec(memory_space=pltpu.VMEM),
            pl.BlockSpec(memory_space=pltpu.HBM),
        ],
        out_specs=pl.BlockSpec(memory_space=pltpu.HBM),
        scratch_shapes=[pltpu.VMEM((16, 1024), BF), pltpu.SemaphoreType.DMA((8,))],
        compiler_params=VMEM,
    )(lags, seg_lengths, pltpu.with_memory_space_constraint(frames, pltpu.HBM))
    frames_h = all_to_all(halves, ("yl", "yh"))

    packed = call(
        pack_kernel, [((32, 1024), BF)], yl[None], panel_low.T, panel_high.T, smem=1
    )
    panel_own = lax.all_gather(packed, Z8, axis=0, tiled=True)
    panel_other = lax.ppermute(panel_own, "z0", [(0, 1), (1, 0)])

    by_run = frames_h.reshape(2, 2, 272, 1024)
    tails = lax.ppermute(
        by_run[:, 1, 192:256].reshape(128, 1024), Z, [(i, i + 1) for i in range(1, 15, 2)]
    )
    masks = call(mask_kernel, [((8, 2048), F32)], place, by_run[:, 0, 256:, :128], smem=1)
    panel_other, masks = lax.optimization_barrier((panel_other, masks))

    keep, send = call(
        project_kernel,
        [((4, 64, 1152), BF)] * 2,
        place,
        panel_own,
        panel_other,
        frames_h,
        tails,
        smem=1,
    )
    got = lax.ppermute(send, "c", [(0, 1), (1, 0)])
    pairs = (keep.astype(F32) + got.astype(F32)).astype(BF)
    parts = all_to_all(pairs.reshape(32, 8, 1152), ("z0", "yh", "yl", "x"))
    basis, tiled = call(
        sum_kernel,
        [((16, 2176), BF), ((8, 16, 2048), BF)],
        parts.reshape(2, 2, 2, 4, 8, 1152),
    )

    right = all_to_all(tiled, ("z0", "yh", "yl"))
    left = lax.all_gather(basis, FE, axis=0, tiled=True)

    terms = call(
        cov_kernel, [((8, 56, 128), F32)], masks, left, right.reshape(128, 2048)
    )
    rows = call(rows_kernel, [((8, 8, 128), F32)], all_to_all(terms, Z8))
    by_row = all_to_all(rows, FE)
    return call(
        lambda *refs: final_kernel(1.0 / 16384.0, *refs),
        [((3, 2, 1024), F32), ((2, 32), F32)],
        place,
        by_row,
        ridge[:, None],
        ridge[None, :],
        smem=1,
    )


def solution(mesh):
    fine = Mesh(
        np.asarray(mesh.devices).reshape(2, 2, 2, 2, 2, 4, 2, 2),
        ("z3", "z2", "z1", "z0", "yh", "x", "c", "yl"),
    )
    tm = Z + ("yh",)
    in_specs = (P("yl", tm, FE), P(FE, tm), P(FE, tm), P("yl"), P("yl", None), P())
    rows = tm + FE + ("yl",)
    out_specs = (P(None, rows, None), P(rows, None))
    return jax.shard_map(local, mesh=fine, in_specs=in_specs, out_specs=out_specs, check_vma=False)
```

time: 154 us -> 208 us (1.35)
  Pallas kernels: 15.7 us -> 75.3 us
  starting transfers between devices: 33.5 us -> 25.3 us
  waiting for transfers between devices: 7.93 us -> 11.8 us
    pallas_call x3 -> x1, Pallas kernels: 8.58 us -> 64.7 us  [local(): pl.pallas_call(halves_kernel, out_shape=pltpu.HBM((4, 272, 1024), BF), in...]
    ppermute x4 -> x2, starting transfers between devices: 17.4 us -> 8.91 us  [the longest x1 8.23 us: local(): got = lax.ppermute(send, 'c', [(0, 1), (1, 0)])]
    ppermute x1, waiting for transfers between devices: 0.01 us -> 5.56 us  [local(): panel_other = lax.ppermute(panel_own, 'z0', [(0, 1), (1, 0)])]
    pallas_call x7, Pallas kernels: 7.15 us -> 10.6 us  [call(): pl.pallas_call(kernel, out_shape=shapes, in_specs=specs, out_specs=outs,...]
  transfers between devices with their start and end apart: 8 -> 6, of which waited for: 4 -> 3; matrix products, arithmetic and copies ran while one was open for 0% -> 0% of each run, Pallas kernels for 3% -> 0%
where the time goes in v6:
time: 208 us; the launch traced here: 207 us
  blocking collectives  92.3 us (44%)
  Pallas kernels  75.3 us (36%)
  starting transfers between devices  25.3 us (12%)
  waiting for transfers between devices  11.8 us (6%)
    pallas_call x1, Pallas kernels, local(): pl.pallas_call(halves_kernel, out_shape=pltpu.HBM((4, 272, 1024), BF), in...  64.7 us
    all_to_all x2, blocking collectives, all_to_all(): return lax.all_to_all(x, axes, split_axis=0, concat_axis=0, tiled=True)  44.5 us
    all_gather x1, blocking collectives, local(): panel_own = lax.all_gather(packed, Z8, axis=0, tiled=True)  32.7 us
    all_gather x1, blocking collectives, local(): left = lax.all_gather(basis, FE, axis=0, tiled=True)  15.1 us
    all_to_all x3, starting transfers between devices, all_to_all(): return lax.all_to_all(x, axes, split_axis=0, concat_axis=0, tiled=True)  13.6 us
    pallas_call x7, Pallas kernels, call(): pl.pallas_call(kernel, out_shape=shapes, in_specs=specs, out_specs=outs,...  10.6 us
    ppermute x1, starting transfers between devices, local(): got = lax.ppermute(send, 'c', [(0, 1), (1, 0)])  8.23 us
    ppermute x1, waiting for transfers between devices, local(): panel_other = lax.ppermute(panel_own, 'z0', [(0, 1), (1, 0)])  5.56 us
  transfers between devices with their start and end apart: 6, of which 3 were waited for; matrix products, arithmetic and copies ran while one was open for 0% of the time, Pallas kernels for 0%

profile of v6, /device:TPU:1, one launch (start us, length us, event | category | flops | bytes accessed | tf_op | source)
XLA Modules:
  0.0 207.1 jit_solution(13525297183553191400)
XLA Ops:
  1.3 0.6 copy-done.3
  1.9 64.7 %shard_map.78 = bf16[4,272,1024]{2,1,0:T(8,128)(2,1)} custom-call(s32[1]{0:T(128)S(6)} %copy.13.lag_ref, s32[1,64]{1,0:T(1,128)S(1)} %copy-done.3, bf16[1,256,2048]{2,1,0:T(8,128)(2,1)} %frames_ref.1), custom_call_target="tpu_custom_call" | custom-call | tf_op jit(solution)/shard_map/pallas_call | solution.py:219
  66.7 5.2 %all-to-all-start = ((bf16[4,272,1024]{2,1,0:T(8,128)(2,1)}), bf16[4,272,1024]{2,1,0:T(8,128)(2,1)S(1)}, u32[]{:S(2)}, u32[]{:S(2)}) async-start(bf16[4,272,1024]{2,1,0:T(8,128)(2,1)} %shard_map.78), calls=%async_computation | async-start | bytes 4456448 | tf_op jit(solution)/shard_map/all_to_all | solution.py:209
  71.8 0.1 shard_map.77
  72.0 32.7 %all_gather.6.own_ref = bf16[256,1024]{1,0:T(8,128)(2,1)S(1)} all-gather(bf16[32,1024]{1,0:T(8,128)(2,1)S(1)} %shard_map.77), channel_id=1, replica_groups=mesh['z3'=2,'z2'=2,'z1'=2,'z0'=2,'yh'=2,'x'=4,'c'=2,'yl'=2] {'z3','z2','..., dimensions={0}, use_global_device_ids=true | all-gather | bytes 589824 | tf_op jit(solution)/shard_map/all_gather | solution.py:236
  104.7 2.8 %collective-permute-start = (bf16[256,1024]{1,0:T(8,128)(2,1)S(1)}, bf16[256,1024]{1,0:T(8,128)(2,1)S(1)}, u32[]{:S(2)}, u32[]{:S(2)}) collective-permute-start(bf16[256,1024]{1,0:T(8,128)(2,1)S(1)} %all_gather.6.own_ref), channel_id=1, source_target_pairs={{0,32},{32,0},{1,33},{33,1},{2,34},{34,2},{3,35},{35,3},{4,36},{36... | collective-permute-start | bytes 1572872 | tf_op jit(solution)/shard_map/ppermute | solution.py:237
  107.5 0.7 collective-permute-start.1
  108.3 0.9 shard_map.79.mask_ref
  109.2 5.6 %collective-permute-done.other_ref = bf16[256,1024]{1,0:T(8,128)(2,1)S(1)} collective-permute-done((bf16[256,1024]{1,0:T(8,128)(2,1)S(1)}, bf16[256,1024]{1,0:T(8,128)(2,1)S(1)}, u32[]{:S(2)}, u32[]{:S(2)}) %collective-permute-start) | collective-permute-done | bytes 524320 | tf_op jit(solution)/shard_map/ppermute | solution.py:237
  114.8 5.1 %shard_map.80 = (bf16[4,64,1152]{2,1,0:T(8,128)(2,1)S(1)}, bf16[4,64,1152]{2,1,0:T(8,128)(2,1)S(1)}) custom-call(s32[3]{0:T(128)S(1)} %pad_add_fusion.place_ref.refs_0_, bf16[256,1024]{1,0:T(8,128)(2,1)S(1)} %all_gather.6.own_ref, bf16[256,1024]{1,0:T(8,128)(2,1)S(1)} %collective-permute-done.other_ref, bf16[4,272,1024]{2,1,0:T(8,128)(2,1)S(1)} %all-to-all-done.frames_ref, ...), custom_call_target="tpu_custom_call" | custom-call | tf_op jit(solution)/shard_map/pallas_call | solution.py:202
  119.9 8.2 %collective-permute-start.2 = (bf16[4,64,1152]{2,1,0:T(8,128)(2,1)S(1)}, bf16[4,64,1152]{2,1,0:T(8,128)(2,1)S(1)}, u32[]{:S(2)}, u32[]{:S(2)}) collective-permute-start(bf16[4,64,1152]{2,1,0:T(8,128)(2,1)S(1)} %get-tuple-element.11), channel_id=1, source_target_pairs={{0,2},{2,0},{1,3},{3,1},{4,6},{6,4},{5,7},{7,5},{8,10},{10,8},{9,1... | collective-permute-start | bytes 1769480 | tf_op jit(solution)/shard_map/ppermute | solution.py:256
  128.1 1.6 collective-permute-done.2
  129.7 0.2 add_convert_fusion
  129.9 19.0 %all_to_all.25 = bf16[32,8,1152]{2,1,0:T(8,128)(2,1)S(1)} all-to-all(bf16[32,8,1152]{2,1,0:T(8,128)(2,1)S(1)} %bitcast.27), channel_id=1, replica_groups=mesh['z3'=2,'z2'=2,'z1'=2,'z0'=2,'yh'=2,'x'=4,'c'=2,'yl'=2] {'z0','yh','..., dimensions={0} | all-to-all | bytes 1179648 | tf_op jit(solution)/shard_map/all_to_all | solution.py:209
  148.9 0.9 shard_map.81
  149.8 3.8 %all-to-all-start.2 = ((bf16[8,16,2048]{2,1,0:T(8,128)(2,1)}), bf16[8,16,2048]{2,1,0:T(8,128)(2,1)S(1)}, u32[]{:S(2)}, u32[]{:S(2)}) async-start(bf16[8,16,2048]{2,1,0:T(8,128)(2,1)} %get-tuple-element.13), calls=%async_computation.2 | async-start | bytes 1048576 | tf_op jit(solution)/shard_map/all_to_all | solution.py:209
  153.6 15.1 %all_gather.7.left_ref = bf16[128,2176]{1,0:T(8,128)(2,1)S(1)} all-gather(bf16[16,2176]{1,0:T(8,128)(2,1)S(1)} %get-tuple-element.12), channel_id=1, replica_groups=mesh['z3'=2,'z2'=2,'z1'=2,'z0'=2,'yh'=2,'x'=4,'c'=2,'yl'=2] {'x','c'}, dimensions={0}, use_global_device_ids=true | all-gather | bytes 626688 | tf_op jit(solution)/shard_map/all_gather | solution.py:266
  168.7 1.7 shard_map.82
  170.3 25.5 %all_to_all.26.parts_ref = f32[8,56,128]{2,1,0:T(8,128)S(1)} all-to-all(f32[8,56,128]{2,1,0:T(8,128)S(1)} %shard_map.82), channel_id=1, replica_groups=mesh['z3'=2,'z2'=2,'z1'=2,'z0'=2,'yh'=2,'x'=4,'c'=2,'yl'=2] {'z3','z2','..., dimensions={0} | all-to-all | bytes 458752 | tf_op jit(solution)/shard_map/all_to_all | solution.py:209
  195.8 0.6 shard_map.83
  196.4 4.6 %all-to-all-start.4 = ((f32[8,8,128]{2,1,0:T(8,128)}), f32[8,8,128]{2,1,0:T(8,128)S(1)}, u32[]{:S(2)}, u32[]{:S(2)}) async-start(f32[8,8,128]{2,1,0:T(8,128)} %shard_map.83), calls=%async_computation.4 | async-start | bytes 65536 | tf_op jit(solution)/shard_map/all_to_all | solution.py:209
  201.0 0.1 copy.10.refs_2_
  201.1 4.6 %all-to-all-done.4.refs_1_ = f32[8,8,128]{2,1,0:T(8,128)S(1)} async-done(((f32[8,8,128]{2,1,0:T(8,128)}), f32[8,8,128]{2,1,0:T(8,128)S(1)}, u32[]{:S(2)}, u32[]{:S(2)}) %all-to-all-start.4) | async-done | bytes 32800 | tf_op jit(solution)/shard_map/all_to_all | solution.py:209
  205.8 1.4 shard_map.84
  (13 shorter events, 0.1 us)
Async XLA Ops:
  1.3 0.7 copy-start.3
  66.6 5.2 %copy-start = (bf16[2048,16]{0,1:T(8,128)(2,1)S(1)}, bf16[2048,16]{0,1:T(8,128)(2,1)}, u32[]{:S(2)}) copy-start(bf16[2048,16]{0,1:T(8,128)(2,1)} %param.7) | copy-start | bytes 196612
  66.7 5.2 %copy-start.1 = (bf16[2048,16]{0,1:T(8,128)(2,1)S(1)}, bf16[2048,16]{0,1:T(8,128)(2,1)}, u32[]{:S(2)}) copy-start(bf16[2048,16]{0,1:T(8,128)(2,1)} %param.8) | copy-start | bytes 196612
  66.7 40.8 %all-to-all-start = ((bf16[4,272,1024]{2,1,0:T(8,128)(2,1)}), bf16[4,272,1024]{2,1,0:T(8,128)(2,1)S(1)}, u32[]{:S(2)}, u32[]{:S(2)}) async-start(bf16[4,272,1024]{2,1,0:T(8,128)(2,1)} %shard_map.78), calls=%async_computation | async-start | bytes 4456448 | tf_op jit(solution)/shard_map/all_to_all | solution.py:209
  104.7 10.1 %collective-permute-start = (bf16[256,1024]{1,0:T(8,128)(2,1)S(1)}, bf16[256,1024]{1,0:T(8,128)(2,1)S(1)}, u32[]{:S(2)}, u32[]{:S(2)}) collective-permute-start(bf16[256,1024]{1,0:T(8,128)(2,1)S(1)} %all_gather.6.own_ref), channel_id=1, source_target_pairs={{0,32},{32,0},{1,33},{33,1},{2,34},{34,2},{3,35},{35,3},{4,36},{36... | collective-permute-start | bytes 1572872 | tf_op jit(solution)/shard_map/ppermute | solution.py:237
  107.5 7.2 %collective-permute-start.1 = (bf16[128,1024]{1,0:T(8,128)(2,1)S(1)}, bf16[128,1024]{1,0:T(8,128)(2,1)S(1)}, u32[]{:S(2)}, u32[]{:S(2)}) collective-permute-start(bf16[128,1024]{1,0:T(8,128)(2,1)S(1)} %bitcast.28), channel_id=1, source_target_pairs={{32,64},{96,128},{160,192},{224,256},{288,320},{352,384},{416,448}... | collective-permute-start | bytes 786440 | tf_op jit(solution)/shard_map/ppermute | solution.py:240
  119.9 9.8 %collective-permute-start.2 = (bf16[4,64,1152]{2,1,0:T(8,128)(2,1)S(1)}, bf16[4,64,1152]{2,1,0:T(8,128)(2,1)S(1)}, u32[]{:S(2)}, u32[]{:S(2)}) collective-permute-start(bf16[4,64,1152]{2,1,0:T(8,128)(2,1)S(1)} %get-tuple-element.11), channel_id=1, source_target_pairs={{0,2},{2,0},{1,3},{3,1},{4,6},{6,4},{5,7},{7,5},{8,10},{10,8},{9,1... | collective-permute-start | bytes 1769480 | tf_op jit(solution)/shard_map/ppermute | solution.py:256
  148.9 52.1 %copy-start.2 = (f32[32]{0:T(128)S(1)}, f32[32]{0:T(128)}, u32[]{:S(2)}) copy-start(f32[32]{0:T(128)} %param.11) | copy-start | bytes 388
  149.8 18.9 %all-to-all-start.2 = ((bf16[8,16,2048]{2,1,0:T(8,128)(2,1)}), bf16[8,16,2048]{2,1,0:T(8,128)(2,1)S(1)}, u32[]{:S(2)}, u32[]{:S(2)}) async-start(bf16[8,16,2048]{2,1,0:T(8,128)(2,1)} %get-tuple-element.13), calls=%async_computation.2 | async-start | bytes 1048576 | tf_op jit(solution)/shard_map/all_to_all | solution.py:209
  196.4 9.3 %all-to-all-start.4 = ((f32[8,8,128]{2,1,0:T(8,128)}), f32[8,8,128]{2,1,0:T(8,128)S(1)}, u32[]{:S(2)}, u32[]{:S(2)}) async-start(f32[8,8,128]{2,1,0:T(8,128)} %shard_map.83), calls=%async_computation.4 | async-start | bytes 65536 | tf_op jit(solution)/shard_map/all_to_all | solution.py:209

commit v7 on v6

--- a/solution.py
+++ b/solution.py
@@ -32,48 +32,57 @@
         out_ref[half * 16 : half * 16 + 16, :] = rows.astype(BF)
 
 
-def halves_kernel(lag_ref, seg_ref, frames_ref, out_ref, info_ref, sems):
-    copies = []
-    for i in range(4):
-        half = frames_ref.at[0, :, pl.ds((i // 2) * 1024, 1024)]
-        copies.append(pltpu.make_async_copy(half, out_ref.at[i, pl.ds(0, 256)], sems.at[i]))
-    for copy in copies:
-        copy.start()
+def halves_kernel(lag_ref, seg_ref, frames_ref, out_ref, rows_ref, sems):
+    loads = []
+    for half in range(2):
+        part = frames_ref.at[0, :, pl.ds(half * 1024, 1024)]
+        load = pltpu.make_async_copy(part, rows_ref.at[half, pl.ds(0, 256)], sems.at[half])
+        load.start()
+        loads.append(load)
     seg = jnp.concatenate([seg_ref[...], jnp.zeros((1, 64), I32)], axis=1)
     row = lax.broadcasted_iota(I32, (16, 128), 0)
     info = jnp.where(row == 0, seg >> 8, jnp.where(row == 1, seg & 255, lag_ref[0]))
-    info_ref[:, :128] = info.astype(F32).astype(BF)
-    info_ref[:, 128:] = jnp.zeros((16, 896), BF)
-    for i in range(4):
-        copy = pltpu.make_async_copy(info_ref, out_ref.at[i, pl.ds(256, 16)], sems.at[4 + i])
-        copy.start()
-        copies.append(copy)
-    for copy in copies:
-        copy.wait()
-
-
-def project_kernel(place_ref, own_ref, other_ref, frames_ref, tails_ref, keep_ref, send_ref):
+    stores = []
+    for half in range(2):
+        rows_ref[half, 256:, :128] = info.astype(F32).astype(BF)
+        rows_ref[half, 256:, 128:] = jnp.zeros((16, 896), BF)
+        loads[half].wait()
+        for i in (half * 2, half * 2 + 1):
+            store = pltpu.make_async_copy(rows_ref.at[half], out_ref.at[i], sems.at[2 + i])
+            store.start()
+            stores.append(store)
+    for store in stores:
+        store.wait()
+
+
+def project_kernel(
+    place_ref, own_ref, other_ref, frames_ref, tails_ref, keep_ref, send_ref, panel_ref
+):
     own_yh = place_ref[0] & 1
+    c = place_ref[2]
+    for kind in range(2):
+        z2 = c if kind == 0 else 1 - c
+        for yh, ref in ((own_yh, own_ref), (1 - own_yh, other_ref)):
+            for z3 in range(2):
+                src = pl.multiple_of(z3 * 128 + z2 * 64, 64)
+                dst = pl.multiple_of(kind * 256 + yh * 128 + z3 * 64, 64)
+                panel_ref[pl.ds(dst, 64), :] = ref[pl.ds(src, 64), :]
+    panel = panel_ref[...]
     for t in range(5):
         frames = frames_ref[t, :256] if t < 4 else tails_ref[...]
         lanes = slice(t * 256, t * 256 + 256) if t < 4 else slice(1024, 1152)
-        for yh, panel_ref in ((own_yh, own_ref), (1 - own_yh, other_ref)):
-            acc = lax.dot_general(panel_ref[...], frames, NT, preferred_element_type=F32)
-
-            def store(refs, acc=acc, yh=yh, lanes=lanes):
+        acc = lax.dot_general(panel, frames, NT, preferred_element_type=F32)
+        for kind, ref in enumerate((keep_ref, send_ref)):
+            for yh in range(2):
                 for z1 in range(2):
-                    for yl in range(2):
-                        for half in range(2):
-                            for z2 in range(2):
-                                row = (z2 * 2 + z1) * 32 + half * 16 + yl * 8
-                                both = jnp.concatenate(
-                                    [acc[row : row + 8], acc[row + 128 : row + 136]], axis=0
-                                )
-                                at = (yl * 4 + half * 2) * 8
-                                refs[z2][z1 * 2 + yh, at : at + 16, lanes] = both.astype(BF)
-
-            pl.when(place_ref[2] == 0)(lambda store=store: store((keep_ref, send_ref)))
-            pl.when(place_ref[2] == 1)(lambda store=store: store((send_ref, keep_ref)))
+                    for half in range(2):
+                        for yl in range(2):
+                            row = kind * 256 + yh * 128 + z1 * 32 + half * 16 + yl * 8
+                            both = jnp.concatenate(
+                                [acc[row : row + 8], acc[row + 64 : row + 72]], axis=0
+                            )
+                            at = (yl * 4 + half * 2) * 8
+                            ref[z1 * 2 + yh, at : at + 16, lanes] = both.astype(BF)
 
 
 def sum_kernel(parts_ref, basis_ref, tiled_ref):
@@ -194,13 +203,18 @@
         score_ref[e : e + 1, :] = score[e] / (diag[e : e + 1, :] + row_ref[...])
 
 
-def call(kernel, out, *args, smem=0, **kw):
+def call(kernel, out, *args, smem=0, scratch=()):
     specs = [pl.BlockSpec(memory_space=pltpu.SMEM)] * smem
     specs += [pl.BlockSpec(memory_space=pltpu.VMEM)] * (len(args) - smem)
     shapes = [jax.ShapeDtypeStruct(*o) for o in out]
     outs = [pl.BlockSpec(memory_space=pltpu.VMEM)] * len(out)
     got = pl.pallas_call(
-        kernel, out_shape=shapes, in_specs=specs, out_specs=outs, compiler_params=VMEM
+        kernel,
+        out_shape=shapes,
+        in_specs=specs,
+        out_specs=outs,
+        scratch_shapes=scratch,
+        compiler_params=VMEM,
     )(*args)
     return got[0] if len(out) == 1 else got
 
@@ -225,7 +239,7 @@
             pl.BlockSpec(memory_space=pltpu.HBM),
         ],
         out_specs=pl.BlockSpec(memory_space=pltpu.HBM),
-        scratch_shapes=[pltpu.VMEM((16, 1024), BF), pltpu.SemaphoreType.DMA((8,))],
+        scratch_shapes=[pltpu.VMEM((2, 272, 1024), BF), pltpu.SemaphoreType.DMA((6,))],
         compiler_params=VMEM,
     )(lags, seg_lengths, pltpu.with_memory_space_constraint(frames, pltpu.HBM))
     frames_h = all_to_all(halves, ("yl", "yh"))
@@ -252,6 +266,7 @@
         frames_h,
         tails,
         smem=1,
+        scratch=[pltpu.VMEM((512, 1024), BF)],
     )
     got = lax.ppermute(send, "c", [(0, 1), (1, 0)])
     pairs = (keep.astype(F32) + got.astype(F32)).astype(BF)

time: 208 us -> 143 us (0.69)
  Pallas kernels: 75.3 us -> 10.1 us
    pallas_call x1, Pallas kernels: 64.7 us -> 2.46 us  [local(): pl.pallas_call(halves_kernel, out_shape=pltpu.HBM((4, 272, 1024), BF), in...]
    pallas_call x7, Pallas kernels: 10.6 us -> 7.66 us  [call(): pl.pallas_call(kernel, out_shape=shapes, in_specs=specs, out_specs=outs,...]
  transfers between devices with their start and end apart: 6 -> 6, of which waited for: 3 -> 3; matrix products, arithmetic and copies ran while one was open for 0% -> 0% of each run, Pallas kernels for 0% -> 1%
where the time goes in v7:
time: 143 us; the launch traced here: 142 us
  blocking collectives  92.3 us (65%)
  starting transfers between devices  25.3 us (18%)
  waiting for transfers between devices  11.8 us (8%)
  Pallas kernels  10.1 us (7%)
    all_to_all x2, blocking collectives, all_to_all(): return lax.all_to_all(x, axes, split_axis=0, concat_axis=0, tiled=True)  44.5 us
    all_gather x1, blocking collectives, local(): panel_own = lax.all_gather(packed, Z8, axis=0, tiled=True)  32.7 us
    all_gather x1, blocking collectives, local(): left = lax.all_gather(basis, FE, axis=0, tiled=True)  15.1 us
    all_to_all x3, starting transfers between devices, all_to_all(): return lax.all_to_all(x, axes, split_axis=0, concat_axis=0, tiled=True)  13.6 us
    ppermute x1, starting transfers between devices, local(): got = lax.ppermute(send, 'c', [(0, 1), (1, 0)])  8.26 us
    pallas_call x7, Pallas kernels, call(): pl.pallas_call(kernel, out_shape=shapes, in_specs=specs, out_specs=outs,...  7.66 us
    ppermute x1, waiting for transfers between devices, local(): panel_other = lax.ppermute(panel_own, 'z0', [(0, 1), (1, 0)])  5.56 us
    all_to_all x3, waiting for transfers between devices, all_to_all(): return lax.all_to_all(x, axes, split_axis=0, concat_axis=0, tiled=True)  4.65 us
  transfers between devices with their start and end apart: 6, of which 3 were waited for; matrix products, arithmetic and copies ran while one was open for 0% of the time, Pallas kernels for 1%

profile of v7, /device:TPU:1, one launch (start us, length us, event | category | flops | bytes accessed | tf_op | source)
XLA Modules:
  0.0 142.0 jit_solution(244941395997874496)
XLA Ops:
  1.3 0.6 copy-done.3
  1.9 2.5 %shard_map.78 = bf16[4,272,1024]{2,1,0:T(8,128)(2,1)} custom-call(s32[1]{0:T(128)S(6)} %copy.13.lag_ref, s32[1,64]{1,0:T(1,128)S(1)} %copy-done.3, bf16[1,256,2048]{2,1,0:T(8,128)(2,1)} %frames_ref.1), custom_call_target="tpu_custom_call" | custom-call | tf_op jit(solution)/shard_map/pallas_call | solution.py:233
  4.4 5.2 %all-to-all-start = ((bf16[4,272,1024]{2,1,0:T(8,128)(2,1)}), bf16[4,272,1024]{2,1,0:T(8,128)(2,1)S(1)}, u32[]{:S(2)}, u32[]{:S(2)}) async-start(bf16[4,272,1024]{2,1,0:T(8,128)(2,1)} %shard_map.78), calls=%async_computation | async-start | bytes 4456448 | tf_op jit(solution)/shard_map/all_to_all | solution.py:223
  9.6 0.1 shard_map.77
  9.7 32.7 %all_gather.6.own_ref = bf16[256,1024]{1,0:T(8,128)(2,1)S(1)} all-gather(bf16[32,1024]{1,0:T(8,128)(2,1)S(1)} %shard_map.77), channel_id=1, replica_groups=mesh['z3'=2,'z2'=2,'z1'=2,'z0'=2,'yh'=2,'x'=4,'c'=2,'yl'=2] {'z3','z2','..., dimensions={0}, use_global_device_ids=true | all-gather | bytes 589824 | tf_op jit(solution)/shard_map/all_gather | solution.py:250
  42.4 2.8 %collective-permute-start = (bf16[256,1024]{1,0:T(8,128)(2,1)S(1)}, bf16[256,1024]{1,0:T(8,128)(2,1)S(1)}, u32[]{:S(2)}, u32[]{:S(2)}) collective-permute-start(bf16[256,1024]{1,0:T(8,128)(2,1)S(1)} %all_gather.6.own_ref), channel_id=1, source_target_pairs={{0,32},{32,0},{1,33},{33,1},{2,34},{34,2},{3,35},{35,3},{4,36},{36... | collective-permute-start | bytes 1572872 | tf_op jit(solution)/shard_map/ppermute | solution.py:251
  45.3 0.7 collective-permute-start.1
  46.1 0.9 shard_map.79.mask_ref
  46.9 5.6 %collective-permute-done.other_ref = bf16[256,1024]{1,0:T(8,128)(2,1)S(1)} collective-permute-done((bf16[256,1024]{1,0:T(8,128)(2,1)S(1)}, bf16[256,1024]{1,0:T(8,128)(2,1)S(1)}, u32[]{:S(2)}, u32[]{:S(2)}) %collective-permute-start) | collective-permute-done | bytes 524320 | tf_op jit(solution)/shard_map/ppermute | solution.py:251
  52.5 2.1 %shard_map.80 = (bf16[4,64,1152]{2,1,0:T(8,128)(2,1)S(1)}, bf16[4,64,1152]{2,1,0:T(8,128)(2,1)S(1)}) custom-call(s32[3]{0:T(128)S(1)} %pad_add_fusion.place_ref.refs_0_, bf16[256,1024]{1,0:T(8,128)(2,1)S(1)} %all_gather.6.own_ref, bf16[256,1024]{1,0:T(8,128)(2,1)S(1)} %collective-permute-done.other_ref, bf16[4,272,1024]{2,1,0:T(8,128)(2,1)S(1)} %all-to-all-done.frames_ref, ...), custom_call_target="tpu_custom_call" | custom-call | tf_op jit(solution)/shard_map/pallas_call | solution.py:211
  54.7 8.3 %collective-permute-start.2 = (bf16[4,64,1152]{2,1,0:T(8,128)(2,1)S(1)}, bf16[4,64,1152]{2,1,0:T(8,128)(2,1)S(1)}, u32[]{:S(2)}, u32[]{:S(2)}) collective-permute-start(bf16[4,64,1152]{2,1,0:T(8,128)(2,1)S(1)} %get-tuple-element.11), channel_id=1, source_target_pairs={{0,2},{2,0},{1,3},{3,1},{4,6},{6,4},{5,7},{7,5},{8,10},{10,8},{9,1... | collective-permute-start | bytes 1769480 | tf_op jit(solution)/shard_map/ppermute | solution.py:271
  62.9 1.6 %collective-permute-done.2 = bf16[4,64,1152]{2,1,0:T(8,128)(2,1)S(1)} collective-permute-done((bf16[4,64,1152]{2,1,0:T(8,128)(2,1)S(1)}, bf16[4,64,1152]{2,1,0:T(8,128)(2,1)S(1)}, u32[]{:S(2)}, u32[]{:S(2)}) %collective-permute-start.2) | collective-permute-done | bytes 589856 | tf_op jit(solution)/shard_map/ppermute | solution.py:271
  64.5 0.2 add_convert_fusion
  64.7 19.0 %all_to_all.25 = bf16[32,8,1152]{2,1,0:T(8,128)(2,1)S(1)} all-to-all(bf16[32,8,1152]{2,1,0:T(8,128)(2,1)S(1)} %bitcast.27), channel_id=1, replica_groups=mesh['z3'=2,'z2'=2,'z1'=2,'z0'=2,'yh'=2,'x'=4,'c'=2,'yl'=2] {'z0','yh','..., dimensions={0} | all-to-all | bytes 1179648 | tf_op jit(solution)/shard_map/all_to_all | solution.py:223
  83.7 0.9 shard_map.81
  84.6 3.8 %all-to-all-start.2 = ((bf16[8,16,2048]{2,1,0:T(8,128)(2,1)}), bf16[8,16,2048]{2,1,0:T(8,128)(2,1)S(1)}, u32[]{:S(2)}, u32[]{:S(2)}) async-start(bf16[8,16,2048]{2,1,0:T(8,128)(2,1)} %get-tuple-element.13), calls=%async_computation.2 | async-start | bytes 1048576 | tf_op jit(solution)/shard_map/all_to_all | solution.py:223
  88.4 15.1 %all_gather.7.left_ref = bf16[128,2176]{1,0:T(8,128)(2,1)S(1)} all-gather(bf16[16,2176]{1,0:T(8,128)(2,1)S(1)} %get-tuple-element.12), channel_id=1, replica_groups=mesh['z3'=2,'z2'=2,'z1'=2,'z0'=2,'yh'=2,'x'=4,'c'=2,'yl'=2] {'x','c'}, dimensions={0}, use_global_device_ids=true | all-gather | bytes 626688 | tf_op jit(solution)/shard_map/all_gather | solution.py:281
  103.5 1.7 %shard_map.82 = f32[8,56,128]{2,1,0:T(8,128)S(1)} custom-call(f32[8,2048]{1,0:T(8,128)S(1)} %shard_map.79.mask_ref, bf16[128,2176]{1,0:T(8,128)(2,1)S(1)} %all_gather.7.left_ref, bf16[128,2048]{1,0:T(8,128)(2,1)S(1)} %bitcast.22), custom_call_target="tpu_custom_call" | custom-call | tf_op jit(solution)/shard_map/pallas_call | solution.py:211
  105.1 25.5 %all_to_all.26.parts_ref = f32[8,56,128]{2,1,0:T(8,128)S(1)} all-to-all(f32[8,56,128]{2,1,0:T(8,128)S(1)} %shard_map.82), channel_id=1, replica_groups=mesh['z3'=2,'z2'=2,'z1'=2,'z0'=2,'yh'=2,'x'=4,'c'=2,'yl'=2] {'z3','z2','..., dimensions={0} | all-to-all | bytes 458752 | tf_op jit(solution)/shard_map/all_to_all | solution.py:223
  130.6 0.6 shard_map.83
  131.3 4.6 %all-to-all-start.4 = ((f32[8,8,128]{2,1,0:T(8,128)}), f32[8,8,128]{2,1,0:T(8,128)S(1)}, u32[]{:S(2)}, u32[]{:S(2)}) async-start(f32[8,8,128]{2,1,0:T(8,128)} %shard_map.83), calls=%async_computation.4 | async-start | bytes 65536 | tf_op jit(solution)/shard_map/all_to_all | solution.py:223
  135.9 0.1 copy.10.refs_2_
  136.0 4.6 %all-to-all-done.4.refs_1_ = f32[8,8,128]{2,1,0:T(8,128)S(1)} async-done(((f32[8,8,128]{2,1,0:T(8,128)}), f32[8,8,128]{2,1,0:T(8,128)S(1)}, u32[]{:S(2)}, u32[]{:S(2)}) %all-to-all-start.4) | async-done | bytes 32800 | tf_op jit(solution)/shard_map/all_to_all | solution.py:223
  140.6 1.4 shard_map.84
  (13 shorter events, 0.1 us)
Async XLA Ops:
  1.3 0.7 copy-start.3
  4.4 5.2 %copy-start = (bf16[2048,16]{0,1:T(8,128)(2,1)S(1)}, bf16[2048,16]{0,1:T(8,128)(2,1)}, u32[]{:S(2)}) copy-start(bf16[2048,16]{0,1:T(8,128)(2,1)} %param.7) | copy-start | bytes 196612
  4.4 5.2 %copy-start.1 = (bf16[2048,16]{0,1:T(8,128)(2,1)S(1)}, bf16[2048,16]{0,1:T(8,128)(2,1)}, u32[]{:S(2)}) copy-start(bf16[2048,16]{0,1:T(8,128)(2,1)} %param.8) | copy-start | bytes 196612
  4.4 40.8 %all-to-all-start = ((bf16[4,272,1024]{2,1,0:T(8,128)(2,1)}), bf16[4,272,1024]{2,1,0:T(8,128)(2,1)S(1)}, u32[]{:S(2)}, u32[]{:S(2)}) async-start(bf16[4,272,1024]{2,1,0:T(8,128)(2,1)} %shard_map.78), calls=%async_computation | async-start | bytes 4456448 | tf_op jit(solution)/shard_map/all_to_all | solution.py:223
  42.4 10.1 %collective-permute-start = (bf16[256,1024]{1,0:T(8,128)(2,1)S(1)}, bf16[256,1024]{1,0:T(8,128)(2,1)S(1)}, u32[]{:S(2)}, u32[]{:S(2)}) collective-permute-start(bf16[256,1024]{1,0:T(8,128)(2,1)S(1)} %all_gather.6.own_ref), channel_id=1, source_target_pairs={{0,32},{32,0},{1,33},{33,1},{2,34},{34,2},{3,35},{35,3},{4,36},{36... | collective-permute-start | bytes 1572872 | tf_op jit(solution)/shard_map/ppermute | solution.py:251
  45.3 7.2 %collective-permute-start.1 = (bf16[128,1024]{1,0:T(8,128)(2,1)S(1)}, bf16[128,1024]{1,0:T(8,128)(2,1)S(1)}, u32[]{:S(2)}, u32[]{:S(2)}) collective-permute-start(bf16[128,1024]{1,0:T(8,128)(2,1)S(1)} %bitcast.28), channel_id=1, source_target_pairs={{32,64},{96,128},{160,192},{224,256},{288,320},{352,384},{416,448}... | collective-permute-start | bytes 786440 | tf_op jit(solution)/shard_map/ppermute | solution.py:254
  54.7 9.9 %collective-permute-start.2 = (bf16[4,64,1152]{2,1,0:T(8,128)(2,1)S(1)}, bf16[4,64,1152]{2,1,0:T(8,128)(2,1)S(1)}, u32[]{:S(2)}, u32[]{:S(2)}) collective-permute-start(bf16[4,64,1152]{2,1,0:T(8,128)(2,1)S(1)} %get-tuple-element.11), channel_id=1, source_target_pairs={{0,2},{2,0},{1,3},{3,1},{4,6},{6,4},{5,7},{7,5},{8,10},{10,8},{9,1... | collective-permute-start | bytes 1769480 | tf_op jit(solution)/shard_map/ppermute | solution.py:271
  83.7 52.1 %copy-start.2 = (f32[32]{0:T(128)S(1)}, f32[32]{0:T(128)}, u32[]{:S(2)}) copy-start(f32[32]{0:T(128)} %param.11) | copy-start | bytes 388
  84.6 18.9 %all-to-all-start.2 = ((bf16[8,16,2048]{2,1,0:T(8,128)(2,1)}), bf16[8,16,2048]{2,1,0:T(8,128)(2,1)S(1)}, u32[]{:S(2)}, u32[]{:S(2)}) async-start(bf16[8,16,2048]{2,1,0:T(8,128)(2,1)} %get-tuple-element.13), calls=%async_computation.2 | async-start | bytes 1048576 | tf_op jit(solution)/shard_map/all_to_all | solution.py:223
  131.3 9.3 %all-to-all-start.4 = ((f32[8,8,128]{2,1,0:T(8,128)}), f32[8,8,128]{2,1,0:T(8,128)S(1)}, u32[]{:S(2)}, u32[]{:S(2)}) async-start(f32[8,8,128]{2,1,0:T(8,128)} %shard_map.83), calls=%async_computation.4 | async-start | bytes 65536 | tf_op jit(solution)/shard_map/all_to_all | solution.py:223

commit v8 on v7

--- a/solution.py
+++ b/solution.py
@@ -32,13 +32,16 @@
         out_ref[half * 16 : half * 16 + 16, :] = rows.astype(BF)
 
 
-def halves_kernel(lag_ref, seg_ref, frames_ref, out_ref, rows_ref, sems):
+def halves_kernel(lag_ref, seg_hbm, frames_ref, out_ref, rows_ref, seg_ref, sems):
+    seg_load = pltpu.make_async_copy(seg_hbm, seg_ref, sems.at[6])
+    seg_load.start()
     loads = []
     for half in range(2):
         part = frames_ref.at[0, :, pl.ds(half * 1024, 1024)]
         load = pltpu.make_async_copy(part, rows_ref.at[half, pl.ds(0, 256)], sems.at[half])
         load.start()
         loads.append(load)
+    seg_load.wait()
     seg = jnp.concatenate([seg_ref[...], jnp.zeros((1, 64), I32)], axis=1)
     row = lax.broadcasted_iota(I32, (16, 128), 0)
     info = jnp.where(row == 0, seg >> 8, jnp.where(row == 1, seg & 255, lag_ref[0]))
@@ -151,23 +154,22 @@
     for m, lhs in enumerate((left * start_bf, lagged * end_bf, left * end_bf)):
         block = lax.dot_general(lhs, now_bf, NT, preferred_element_type=F32)
         for d in range(8):
-            out_ref[d, m * 16 : (m + 1) * 16, :] = block[d * 16 : (d + 1) * 16, :]
+            out_ref[d % 2, d // 2, m * 16 : (m + 1) * 16, :] = block[d * 16 : (d + 1) * 16, :]
     var = lax.dot_general(
         jnp.ones((8, 2048), F32), now * now * keep_end, NT, precision=HI, preferred_element_type=F32
     )
     for d in range(8):
-        out_ref[d, 48:56, :] = var
+        out_ref[d % 2, d // 2, 48:56, :] = var
 
 
 def rows_kernel(parts_ref, out_ref):
-    total = parts_ref[0]
-    for d in range(1, 8):
-        total = total + parts_ref[d]
-    for f in range(8):
-        for m in range(3):
-            src = m * 16 + f * 2
-            out_ref[f, m * 2 : m * 2 + 2, :] = total[src : src + 2, :]
-        out_ref[f, 6:8, :] = total[48:50, :]
+    for d in range(4):
+        total = parts_ref[0, d] + parts_ref[1, d]
+        for f in range(8):
+            for m in range(3):
+                src = m * 16 + f * 2
+                out_ref[d, f, m * 2 : m * 2 + 2, :] = total[src : src + 2, :]
+            out_ref[d, f, 6:8, :] = total[48:50, :]
 
 
 def final_kernel(scale, place_ref, parts_ref, ridge_ref, row_ref, cov_ref, score_ref):
@@ -178,7 +180,8 @@
     diag = jnp.zeros((2, 1), F32)
     weighted = [jnp.zeros((32, 128), F32) for _ in range(2)]
     for f in range(8):
-        total = parts_ref[f] * scale
+        total = (parts_ref[0, f] + parts_ref[1, f]) + (parts_ref[2, f] + parts_ref[3, f])
+        total = total * scale
         for m in range(3):
             cov_ref[m, :, f * 128 : (f + 1) * 128] = total[m * 2 : m * 2 + 2, :]
         own = lane + f * 128 == first + row
@@ -235,13 +238,21 @@
         out_shape=pltpu.HBM((4, 272, 1024), BF),
         in_specs=[
             pl.BlockSpec(memory_space=pltpu.SMEM),
-            pl.BlockSpec(memory_space=pltpu.VMEM),
+            pl.BlockSpec(memory_space=pltpu.HBM),
             pl.BlockSpec(memory_space=pltpu.HBM),
         ],
         out_specs=pl.BlockSpec(memory_space=pltpu.HBM),
-        scratch_shapes=[pltpu.VMEM((2, 272, 1024), BF), pltpu.SemaphoreType.DMA((6,))],
+        scratch_shapes=[
+            pltpu.VMEM((2, 272, 1024), BF),
+            pltpu.VMEM((1, 64), I32),
+            pltpu.SemaphoreType.DMA((7,)),
+        ],
         compiler_params=VMEM,
-    )(lags, seg_lengths, pltpu.with_memory_space_constraint(frames, pltpu.HBM))
+    )(
+        lags,
+        pltpu.with_memory_space_constraint(seg_lengths, pltpu.HBM),
+        pltpu.with_memory_space_constraint(frames, pltpu.HBM),
+    )
     frames_h = all_to_all(halves, ("yl", "yh"))
 
     packed = call(
@@ -281,15 +292,15 @@
     left = lax.all_gather(basis, FE, axis=0, tiled=True)
 
     terms = call(
-        cov_kernel, [((8, 56, 128), F32)], masks, left, right.reshape(128, 2048)
-    )
-    rows = call(rows_kernel, [((8, 8, 128), F32)], all_to_all(terms, Z8))
-    by_row = all_to_all(rows, FE)
+        cov_kernel, [((2, 4, 56, 128), F32)], masks, left, right.reshape(128, 2048)
+    )
+    rows = call(rows_kernel, [((4, 8, 8, 128), F32)], all_to_all(terms, "z1"))
+    by_row = all_to_all(rows.reshape(32, 8, 128), ("z3", "z2") + FE)
     return call(
         lambda *refs: final_kernel(1.0 / 16384.0, *refs),
         [((3, 2, 1024), F32), ((2, 32), F32)],
         place,
-        by_row,
+        by_row.reshape(4, 8, 8, 128),
         ridge[:, None],
         ridge[None, :],
         smem=1,

time: 143 us -> 143 us (level)
  blocking collectives: 92.3 us -> 77.3 us
  waiting for transfers between devices: 11.8 us -> 22.5 us
  starting transfers between devices: 25.3 us -> 30.9 us
    all_to_all x2, blocking collectives: 44.5 us -> 29.6 us  [all_to_all(): return lax.all_to_all(x, axes, split_axis=0, concat_axis=0, tiled=True)]
    all_to_all x3, waiting for transfers between devices: 4.65 us -> 15.4 us  [all_to_all(): return lax.all_to_all(x, axes, split_axis=0, concat_axis=0, tiled=True)]
    all_to_all x3, starting transfers between devices: 13.6 us -> 19.1 us  [all_to_all(): return lax.all_to_all(x, axes, split_axis=0, concat_axis=0, tiled=True)]
where the time goes in v8:
time: 143 us
  blocking collectives  77.3 us (54%)
  starting transfers between devices  30.9 us (22%)
  waiting for transfers between devices  22.5 us (16%)
  Pallas kernels  10.2 us (7%)
    all_gather x1, blocking collectives, local(): panel_own = lax.all_gather(packed, Z8, axis=0, tiled=True)  32.7 us
    all_to_all x2, blocking collectives, all_to_all(): return lax.all_to_all(x, axes, split_axis=0, concat_axis=0, tiled=True)  29.6 us
    all_to_all x3, starting transfers between devices, all_to_all(): return lax.all_to_all(x, axes, split_axis=0, concat_axis=0, tiled=True)  19.1 us
    all_to_all x3, waiting for transfers between devices, all_to_all(): return lax.all_to_all(x, axes, split_axis=0, concat_axis=0, tiled=True)  15.4 us
    all_gather x1, blocking collectives, local(): left = lax.all_gather(basis, FE, axis=0, tiled=True)  15.1 us
    ppermute x1, starting transfers between devices, local(): got = lax.ppermute(send, 'c', [(0, 1), (1, 0)])  8.26 us
    pallas_call x7, Pallas kernels, call(): pl.pallas_call(kernel, out_shape=shapes, in_specs=specs, out_specs=outs,...  7.71 us
    ppermute x1, waiting for transfers between devices, local(): panel_other = lax.ppermute(panel_own, 'z0', [(0, 1), (1, 0)])  5.56 us
  transfers between devices with their start and end apart: 6, of which 3 were waited for; matrix products, arithmetic and copies ran while one was open for 0% of the time, Pallas kernels for 1%

profile of v8, /device:TPU:1, one launch (start us, length us, event | category | flops | bytes accessed | tf_op | source)
XLA Modules:
  0.0 142.7 jit_solution(6269927790619906893)
XLA Ops:
  1.3 2.5 %shard_map.78 = bf16[4,272,1024]{2,1,0:T(8,128)(2,1)} custom-call(s32[1]{0:T(128)S(6)} %copy.13.lag_ref, s32[1,64]{1,0:T(1,128)} %seg_hbm.1, bf16[1,256,2048]{2,1,0:T(8,128)(2,1)} %frames_ref.1), custom_call_target="tpu_custom_call" | custom-call | tf_op jit(solution)/shard_map/pallas_call | solution.py:236
  3.8 5.2 %all-to-all-start = ((bf16[4,272,1024]{2,1,0:T(8,128)(2,1)}), bf16[4,272,1024]{2,1,0:T(8,128)(2,1)S(1)}, u32[]{:S(2)}, u32[]{:S(2)}) async-start(bf16[4,272,1024]{2,1,0:T(8,128)(2,1)} %shard_map.78), calls=%async_computation | async-start | bytes 4456448 | tf_op jit(solution)/shard_map/all_to_all | solution.py:226
  9.0 0.1 shard_map.77
  9.1 32.7 %all_gather.6.own_ref = bf16[256,1024]{1,0:T(8,128)(2,1)S(1)} all-gather(bf16[32,1024]{1,0:T(8,128)(2,1)S(1)} %shard_map.77), channel_id=1, replica_groups=mesh['z3'=2,'z2'=2,'z1'=2,'z0'=2,'yh'=2,'x'=4,'c'=2,'yl'=2] {'z3','z2','..., dimensions={0}, use_global_device_ids=true | all-gather | bytes 589824 | tf_op jit(solution)/shard_map/all_gather | solution.py:261
  41.8 2.8 %collective-permute-start = (bf16[256,1024]{1,0:T(8,128)(2,1)S(1)}, bf16[256,1024]{1,0:T(8,128)(2,1)S(1)}, u32[]{:S(2)}, u32[]{:S(2)}) collective-permute-start(bf16[256,1024]{1,0:T(8,128)(2,1)S(1)} %all_gather.6.own_ref), channel_id=1, source_target_pairs={{0,32},{32,0},{1,33},{33,1},{2,34},{34,2},{3,35},{35,3},{4,36},{36... | collective-permute-start | bytes 1572872 | tf_op jit(solution)/shard_map/ppermute | solution.py:262
  44.7 0.7 collective-permute-start.1
  45.4 0.1 pad_add_fusion.place_ref.refs_0_
  45.4 0.9 shard_map.79.mask_ref
  46.3 5.6 %collective-permute-done.other_ref = bf16[256,1024]{1,0:T(8,128)(2,1)S(1)} collective-permute-done((bf16[256,1024]{1,0:T(8,128)(2,1)S(1)}, bf16[256,1024]{1,0:T(8,128)(2,1)S(1)}, u32[]{:S(2)}, u32[]{:S(2)}) %collective-permute-start) | collective-permute-done | bytes 524320 | tf_op jit(solution)/shard_map/ppermute | solution.py:262
  51.9 2.1 %shard_map.80 = (bf16[4,64,1152]{2,1,0:T(8,128)(2,1)S(1)}, bf16[4,64,1152]{2,1,0:T(8,128)(2,1)S(1)}) custom-call(s32[3]{0:T(128)S(1)} %pad_add_fusion.place_ref.refs_0_, bf16[256,1024]{1,0:T(8,128)(2,1)S(1)} %all_gather.6.own_ref, bf16[256,1024]{1,0:T(8,128)(2,1)S(1)} %collective-permute-done.other_ref, bf16[4,272,1024]{2,1,0:T(8,128)(2,1)S(1)} %all-to-all-done.frames_ref, ...), custom_call_target="tpu_custom_call" | custom-call | tf_op jit(solution)/shard_map/pallas_call | solution.py:214
  54.0 8.3 %collective-permute-start.2 = (bf16[4,64,1152]{2,1,0:T(8,128)(2,1)S(1)}, bf16[4,64,1152]{2,1,0:T(8,128)(2,1)S(1)}, u32[]{:S(2)}, u32[]{:S(2)}) collective-permute-start(bf16[4,64,1152]{2,1,0:T(8,128)(2,1)S(1)} %get-tuple-element.11), channel_id=1, source_target_pairs={{0,2},{2,0},{1,3},{3,1},{4,6},{6,4},{5,7},{7,5},{8,10},{10,8},{9,1... | collective-permute-start | bytes 1769480 | tf_op jit(solution)/shard_map/ppermute | solution.py:282
  62.3 1.6 %collective-permute-done.2 = bf16[4,64,1152]{2,1,0:T(8,128)(2,1)S(1)} collective-permute-done((bf16[4,64,1152]{2,1,0:T(8,128)(2,1)S(1)}, bf16[4,64,1152]{2,1,0:T(8,128)(2,1)S(1)}, u32[]{:S(2)}, u32[]{:S(2)}) %collective-permute-start.2) | collective-permute-done | bytes 589856 | tf_op jit(solution)/shard_map/ppermute | solution.py:282
  63.9 0.2 add_convert_fusion
  64.1 19.0 %all_to_all.25 = bf16[32,8,1152]{2,1,0:T(8,128)(2,1)S(1)} all-to-all(bf16[32,8,1152]{2,1,0:T(8,128)(2,1)S(1)} %bitcast.30), channel_id=1, replica_groups=mesh['z3'=2,'z2'=2,'z1'=2,'z0'=2,'yh'=2,'x'=4,'c'=2,'yl'=2] {'z0','yh','..., dimensions={0} | all-to-all | bytes 1179648 | tf_op jit(solution)/shard_map/all_to_all | solution.py:226
  83.1 0.9 shard_map.81
  84.0 3.8 %all-to-all-start.2 = ((bf16[8,16,2048]{2,1,0:T(8,128)(2,1)}), bf16[8,16,2048]{2,1,0:T(8,128)(2,1)S(1)}, u32[]{:S(2)}, u32[]{:S(2)}) async-start(bf16[8,16,2048]{2,1,0:T(8,128)(2,1)} %get-tuple-element.13), calls=%async_computation.2 | async-start | bytes 1048576 | tf_op jit(solution)/shard_map/all_to_all | solution.py:226
  87.8 15.1 %all_gather.7.left_ref = bf16[128,2176]{1,0:T(8,128)(2,1)S(1)} all-gather(bf16[16,2176]{1,0:T(8,128)(2,1)S(1)} %get-tuple-element.12), channel_id=1, replica_groups=mesh['z3'=2,'z2'=2,'z1'=2,'z0'=2,'yh'=2,'x'=4,'c'=2,'yl'=2] {'x','c'}, dimensions={0}, use_global_device_ids=true | all-gather | bytes 626688 | tf_op jit(solution)/shard_map/all_gather | solution.py:292
  102.9 1.7 %shard_map.82 = f32[2,4,56,128]{3,2,1,0:T(8,128)S(1)} custom-call(f32[8,2048]{1,0:T(8,128)S(1)} %shard_map.79.mask_ref, bf16[128,2176]{1,0:T(8,128)(2,1)S(1)} %all_gather.7.left_ref, bf16[128,2048]{1,0:T(8,128)(2,1)S(1)} %bitcast.24), custom_call_target="tpu_custom_call" | custom-call | tf_op jit(solution)/shard_map/pallas_call | solution.py:214
  104.5 10.5 %all_to_all.26.parts_ref = f32[2,4,56,128]{3,2,1,0:T(8,128)S(1)} all-to-all(f32[2,4,56,128]{3,2,1,0:T(8,128)S(1)} %shard_map.82), channel_id=1, replica_groups=mesh['z3'=2,'z2'=2,'z1'=2,'z0'=2,'yh'=2,'x'=4,'c'=2,'yl'=2] {'z1'}, dimensions={0} | all-to-all | bytes 458752 | tf_op jit(solution)/shard_map/all_to_all | solution.py:226
  115.1 0.7 shard_map.83
  115.7 10.1 %all-to-all-start.4 = ((f32[32,8,128]{2,1,0:T(8,128)}), f32[32,8,128]{2,1,0:T(8,128)S(1)}, u32[]{:S(2)}, u32[]{:S(2)}) async-start(f32[32,8,128]{2,1,0:T(8,128)} %bitcast.12), calls=%async_computation.4 | async-start | bytes 262144 | tf_op jit(solution)/shard_map/all_to_all | solution.py:226
  125.9 0.1 copy.10.refs_2_
  126.0 15.4 %all-to-all-done.4 = f32[32,8,128]{2,1,0:T(8,128)S(1)} async-done(((f32[32,8,128]{2,1,0:T(8,128)}), f32[32,8,128]{2,1,0:T(8,128)S(1)}, u32[]{:S(2)}, u32[]{:S(2)}) %all-to-all-start.4) | async-done | bytes 131104 | tf_op jit(solution)/shard_map/all_to_all | solution.py:226
  141.4 1.4 shard_map.84
  (11 shorter events, 0.0 us)
Async XLA Ops:
  3.8 5.2 %copy-start = (bf16[2048,16]{0,1:T(8,128)(2,1)S(1)}, bf16[2048,16]{0,1:T(8,128)(2,1)}, u32[]{:S(2)}) copy-start(bf16[2048,16]{0,1:T(8,128)(2,1)} %param.7) | copy-start | bytes 196612
  3.8 5.2 %copy-start.1 = (bf16[2048,16]{0,1:T(8,128)(2,1)S(1)}, bf16[2048,16]{0,1:T(8,128)(2,1)}, u32[]{:S(2)}) copy-start(bf16[2048,16]{0,1:T(8,128)(2,1)} %param.8) | copy-start | bytes 196612
  3.8 40.8 %all-to-all-start = ((bf16[4,272,1024]{2,1,0:T(8,128)(2,1)}), bf16[4,272,1024]{2,1,0:T(8,128)(2,1)S(1)}, u32[]{:S(2)}, u32[]{:S(2)}) async-start(bf16[4,272,1024]{2,1,0:T(8,128)(2,1)} %shard_map.78), calls=%async_computation | async-start | bytes 4456448 | tf_op jit(solution)/shard_map/all_to_all | solution.py:226
  41.8 10.1 %collective-permute-start = (bf16[256,1024]{1,0:T(8,128)(2,1)S(1)}, bf16[256,1024]{1,0:T(8,128)(2,1)S(1)}, u32[]{:S(2)}, u32[]{:S(2)}) collective-permute-start(bf16[256,1024]{1,0:T(8,128)(2,1)S(1)} %all_gather.6.own_ref), channel_id=1, source_target_pairs={{0,32},{32,0},{1,33},{33,1},{2,34},{34,2},{3,35},{35,3},{4,36},{36... | collective-permute-start | bytes 1572872 | tf_op jit(solution)/shard_map/ppermute | solution.py:262
  44.7 7.2 %collective-permute-start.1 = (bf16[128,1024]{1,0:T(8,128)(2,1)S(1)}, bf16[128,1024]{1,0:T(8,128)(2,1)S(1)}, u32[]{:S(2)}, u32[]{:S(2)}) collective-permute-start(bf16[128,1024]{1,0:T(8,128)(2,1)S(1)} %bitcast.31), channel_id=1, source_target_pairs={{32,64},{96,128},{160,192},{224,256},{288,320},{352,384},{416,448}... | collective-permute-start | bytes 786440 | tf_op jit(solution)/shard_map/ppermute | solution.py:265
  54.0 9.9 %collective-permute-start.2 = (bf16[4,64,1152]{2,1,0:T(8,128)(2,1)S(1)}, bf16[4,64,1152]{2,1,0:T(8,128)(2,1)S(1)}, u32[]{:S(2)}, u32[]{:S(2)}) collective-permute-start(bf16[4,64,1152]{2,1,0:T(8,128)(2,1)S(1)} %get-tuple-element.11), channel_id=1, source_target_pairs={{0,2},{2,0},{1,3},{3,1},{4,6},{6,4},{5,7},{7,5},{8,10},{10,8},{9,1... | collective-permute-start | bytes 1769480 | tf_op jit(solution)/shard_map/ppermute | solution.py:282
  83.1 42.8 %copy-start.2 = (f32[32]{0:T(128)S(1)}, f32[32]{0:T(128)}, u32[]{:S(2)}) copy-start(f32[32]{0:T(128)} %param.11) | copy-start | bytes 388
  84.0 18.9 %all-to-all-start.2 = ((bf16[8,16,2048]{2,1,0:T(8,128)(2,1)}), bf16[8,16,2048]{2,1,0:T(8,128)(2,1)S(1)}, u32[]{:S(2)}, u32[]{:S(2)}) async-start(bf16[8,16,2048]{2,1,0:T(8,128)(2,1)} %get-tuple-element.13), calls=%async_computation.2 | async-start | bytes 1048576 | tf_op jit(solution)/shard_map/all_to_all | solution.py:226
  115.7 25.6 %all-to-all-start.4 = ((f32[32,8,128]{2,1,0:T(8,128)}), f32[32,8,128]{2,1,0:T(8,128)S(1)}, u32[]{:S(2)}, u32[]{:S(2)}) async-start(f32[32,8,128]{2,1,0:T(8,128)} %bitcast.12), calls=%async_computation.4 | async-start | bytes 262144 | tf_op jit(solution)/shard_map/all_to_all | solution.py:226

commit v9 on v7

--- a/solution.py
+++ b/solution.py
@@ -16,6 +16,9 @@
 Z = ("z3", "z2", "z1", "z0")
 Z8 = ("z3", "z2", "z1")
 FE = ("x", "c")
+PLANE = ("yl", "x", "yh", "z0")
+RIGHT = ("yl", "z0", "yh")
+FAR = ("z2", "z3", "z1")
 
 
 def one_hot(rows, cols, hit):
@@ -32,13 +35,16 @@
         out_ref[half * 16 : half * 16 + 16, :] = rows.astype(BF)
 
 
-def halves_kernel(lag_ref, seg_ref, frames_ref, out_ref, rows_ref, sems):
+def halves_kernel(lag_ref, seg_hbm, frames_ref, out_ref, rows_ref, seg_ref, sems):
+    seg_load = pltpu.make_async_copy(seg_hbm, seg_ref, sems.at[6])
+    seg_load.start()
     loads = []
     for half in range(2):
         part = frames_ref.at[0, :, pl.ds(half * 1024, 1024)]
         load = pltpu.make_async_copy(part, rows_ref.at[half, pl.ds(0, 256)], sems.at[half])
         load.start()
         loads.append(load)
+    seg_load.wait()
     seg = jnp.concatenate([seg_ref[...], jnp.zeros((1, 64), I32)], axis=1)
     row = lax.broadcasted_iota(I32, (16, 128), 0)
     info = jnp.where(row == 0, seg >> 8, jnp.where(row == 1, seg & 255, lag_ref[0]))
@@ -74,24 +80,24 @@
         acc = lax.dot_general(panel, frames, NT, preferred_element_type=F32)
         for kind, ref in enumerate((keep_ref, send_ref)):
             for yh in range(2):
-                for z1 in range(2):
+                for z3 in range(2):
                     for half in range(2):
                         for yl in range(2):
-                            row = kind * 256 + yh * 128 + z1 * 32 + half * 16 + yl * 8
+                            row = kind * 256 + yh * 128 + z3 * 64 + half * 16 + yl * 8
                             both = jnp.concatenate(
-                                [acc[row : row + 8], acc[row + 64 : row + 72]], axis=0
+                                [acc[row : row + 8], acc[row + 32 : row + 40]], axis=0
                             )
-                            at = (yl * 4 + half * 2) * 8
-                            ref[z1 * 2 + yh, at : at + 16, lanes] = both.astype(BF)
+                            at = ((yl * 4 + half * 2 + z3) * 2 + yh) * 16
+                            ref[at : at + 16, lanes] = both.astype(BF)
 
 
 def sum_kernel(parts_ref, basis_ref, tiled_ref):
     for z0 in range(2):
         sums = []
         for yh in range(2):
-            total = parts_ref[z0, yh, 0, 0].astype(F32)
+            total = parts_ref[0, 0, yh, z0].astype(F32)
             for i in range(1, 8):
-                total = total + parts_ref[z0, yh, i // 4, i % 4].astype(F32)
+                total = total + parts_ref[i // 4, i % 4, yh, z0].astype(F32)
             sums.append(total)
         basis = jnp.concatenate(sums, axis=0).astype(BF)
         for rep in range(2):
@@ -129,7 +135,7 @@
         128,
         128,
         lambda r, c: c
-        == (r >> 5) * 32 + ((r >> 1) & 1) * 16 + ((r >> 2) & 7) * 2 + (r & 1),
+        == ((r >> 1) & 1) * 64 + (r >> 5) * 16 + ((r >> 2) & 7) * 2 + (r & 1),
     )
     now = jnp.dot(perm, right_ref[...], preferred_element_type=F32)
     now_bf = now.astype(BF)
@@ -151,7 +157,8 @@
     for m, lhs in enumerate((left * start_bf, lagged * end_bf, left * end_bf)):
         block = lax.dot_general(lhs, now_bf, NT, preferred_element_type=F32)
         for d in range(8):
-            out_ref[d, m * 16 : (m + 1) * 16, :] = block[d * 16 : (d + 1) * 16, :]
+            at = (d >> 1 & 1) * 4 + (d >> 2) * 2 + (d & 1)
+            out_ref[at, m * 16 : (m + 1) * 16, :] = block[d * 16 : (d + 1) * 16, :]
     var = lax.dot_general(
         jnp.ones((8, 2048), F32), now * now * keep_end, NT, precision=HI, preferred_element_type=F32
     )
@@ -187,20 +194,13 @@
         for e in range(2):
             cross = total[2 + e : 3 + e, :]
             weighted[e] = weighted[e] + (cross * cross) * inverse
-    ones = jnp.ones((8, 128), F32)
-    pad = jnp.zeros((96, 128), F32)
-    score = [
-        lax.dot_general(
-            ones,
-            jnp.concatenate([w, pad], axis=0),
-            NT,
-            precision=HI,
-            preferred_element_type=F32,
-        )[0:1, :32]
-        for w in weighted
-    ]
+    both = jnp.concatenate([*weighted, jnp.zeros((64, 128), F32)], axis=0)
+    score = lax.dot_general(
+        jnp.ones((8, 128), F32), both, NT, precision=HI, preferred_element_type=F32
+    )
     for e in range(2):
-        score_ref[e : e + 1, :] = score[e] / (diag[e : e + 1, :] + row_ref[...])
+        ridge_row = diag[e : e + 1, :] + row_ref[...]
+        score_ref[e : e + 1, :] = score[0:1, e * 32 : e * 32 + 32] / ridge_row
 
 
 def call(kernel, out, *args, smem=0, scratch=()):
@@ -235,13 +235,21 @@
         out_shape=pltpu.HBM((4, 272, 1024), BF),
         in_specs=[
             pl.BlockSpec(memory_space=pltpu.SMEM),
-            pl.BlockSpec(memory_space=pltpu.VMEM),
+            pl.BlockSpec(memory_space=pltpu.HBM),
             pl.BlockSpec(memory_space=pltpu.HBM),
         ],
         out_specs=pl.BlockSpec(memory_space=pltpu.HBM),
-        scratch_shapes=[pltpu.VMEM((2, 272, 1024), BF), pltpu.SemaphoreType.DMA((6,))],
+        scratch_shapes=[
+            pltpu.VMEM((2, 272, 1024), BF),
+            pltpu.VMEM((1, 64), I32),
+            pltpu.SemaphoreType.DMA((7,)),
+        ],
         compiler_params=VMEM,
-    )(lags, seg_lengths, pltpu.with_memory_space_constraint(frames, pltpu.HBM))
+    )(
+        lags,
+        pltpu.with_memory_space_constraint(seg_lengths, pltpu.HBM),
+        pltpu.with_memory_space_constraint(frames, pltpu.HBM),
+    )
     frames_h = all_to_all(halves, ("yl", "yh"))
 
     packed = call(
@@ -259,7 +267,7 @@
 
     keep, send = call(
         project_kernel,
-        [((4, 64, 1152), BF)] * 2,
+        [((256, 1152), BF)] * 2,
         place,
         panel_own,
         panel_other,
@@ -270,20 +278,20 @@
     )
     got = lax.ppermute(send, "c", [(0, 1), (1, 0)])
     pairs = (keep.astype(F32) + got.astype(F32)).astype(BF)
-    parts = all_to_all(pairs.reshape(32, 8, 1152), ("z0", "yh", "yl", "x"))
+    parts = all_to_all(pairs.reshape(32, 8, 1152), PLANE)
     basis, tiled = call(
         sum_kernel,
         [((16, 2176), BF), ((8, 16, 2048), BF)],
-        parts.reshape(2, 2, 2, 4, 8, 1152),
-    )
-
-    right = all_to_all(tiled, ("z0", "yh", "yl"))
+        parts.reshape(2, 4, 2, 2, 8, 1152),
+    )
+
+    right = all_to_all(tiled, RIGHT)
     left = lax.all_gather(basis, FE, axis=0, tiled=True)
 
     terms = call(
         cov_kernel, [((8, 56, 128), F32)], masks, left, right.reshape(128, 2048)
     )
-    rows = call(rows_kernel, [((8, 8, 128), F32)], all_to_all(terms, Z8))
+    rows = call(rows_kernel, [((8, 8, 128), F32)], all_to_all(terms, FAR))
     by_row = all_to_all(rows, FE)
     return call(
         lambda *refs: final_kernel(1.0 / 16384.0, *refs),

time: 143 us -> 143 us (level)
  the two profiles are of different devices: /device:TPU:1 before, /device:TPU:40 now
where the time goes in v9:
time: 143 us
  blocking collectives  96.7 us (68%)
  starting transfers between devices  22.1 us (15%)
  waiting for transfers between devices  11.9 us (8%)
  Pallas kernels  10.2 us (7%)
    all_to_all x2, blocking collectives, all_to_all(): return lax.all_to_all(x, axes, split_axis=0, concat_axis=0, tiled=True)  46.6 us
    all_gather x1, blocking collectives, local(): panel_own = lax.all_gather(packed, Z8, axis=0, tiled=True)  36.9 us
    all_to_all x3, starting transfers between devices, all_to_all(): return lax.all_to_all(x, axes, split_axis=0, concat_axis=0, tiled=True)  14.7 us
    all_gather x1, blocking collectives, local(): left = lax.all_gather(basis, FE, axis=0, tiled=True)  13.1 us
    pallas_call x7, Pallas kernels, call(): pl.pallas_call(kernel, out_shape=shapes, in_specs=specs, out_specs=outs,...  7.73 us
    all_to_all x3, waiting for transfers between devices, all_to_all(): return lax.all_to_all(x, axes, split_axis=0, concat_axis=0, tiled=True)  5.27 us
    ppermute x1, waiting for transfers between devices, local(): panel_other = lax.ppermute(panel_own, 'z0', [(0, 1), (1, 0)])  4.62 us
    ppermute x1, starting transfers between devices, local(): lax.ppermute(by_run[:, 1, 192:256].reshape(128, 1024), Z, [(i, i + 1) for...  2.91 us
  transfers between devices with their start and end apart: 6, of which 3 were waited for; matrix products, arithmetic and copies ran while one was open for 0% of the time, Pallas kernels for 1%

profile of v9, /device:TPU:40, one launch (start us, length us, event | category | flops | bytes accessed | tf_op | source)
XLA Modules:
  0.0 142.6 jit_solution(8697929272217842589)
XLA Ops:
  1.3 2.5 %shard_map.78 = bf16[4,272,1024]{2,1,0:T(8,128)(2,1)} custom-call(s32[1]{0:T(128)S(6)} %copy.13.lag_ref, s32[1,64]{1,0:T(1,128)} %seg_hbm.1, bf16[1,256,2048]{2,1,0:T(8,128)(2,1)} %frames_ref.1), custom_call_target="tpu_custom_call" | custom-call | tf_op jit(solution)/shard_map/pallas_call | solution.py:233
  3.8 5.1 %all-to-all-start = ((bf16[4,272,1024]{2,1,0:T(8,128)(2,1)}), bf16[4,272,1024]{2,1,0:T(8,128)(2,1)S(1)}, u32[]{:S(2)}, u32[]{:S(2)}) async-start(bf16[4,272,1024]{2,1,0:T(8,128)(2,1)} %shard_map.78), calls=%async_computation | async-start | bytes 4456448 | tf_op jit(solution)/shard_map/all_to_all | solution.py:223
  8.9 0.1 shard_map.77
  9.0 36.9 %all_gather.6.own_ref = bf16[256,1024]{1,0:T(8,128)(2,1)S(1)} all-gather(bf16[32,1024]{1,0:T(8,128)(2,1)S(1)} %shard_map.77), channel_id=1, replica_groups=mesh['z3'=2,'z2'=2,'z1'=2,'z0'=2,'yh'=2,'x'=4,'c'=2,'yl'=2] {'z3','z2','..., dimensions={0}, use_global_device_ids=true | all-gather | bytes 589824 | tf_op jit(solution)/shard_map/all_gather | solution.py:258
  45.9 2.5 %collective-permute-start = (bf16[256,1024]{1,0:T(8,128)(2,1)S(1)}, bf16[256,1024]{1,0:T(8,128)(2,1)S(1)}, u32[]{:S(2)}, u32[]{:S(2)}) collective-permute-start(bf16[256,1024]{1,0:T(8,128)(2,1)S(1)} %all_gather.6.own_ref), channel_id=1, source_target_pairs={{0,32},{32,0},{1,33},{33,1},{2,34},{34,2},{3,35},{35,3},{4,36},{36... | collective-permute-start | bytes 1572872 | tf_op jit(solution)/shard_map/ppermute | solution.py:259
  48.5 2.9 %collective-permute-start.1 = (bf16[128,1024]{1,0:T(8,128)(2,1)S(1)}, bf16[128,1024]{1,0:T(8,128)(2,1)S(1)}, u32[]{:S(2)}, u32[]{:S(2)}) collective-permute-start(bf16[128,1024]{1,0:T(8,128)(2,1)S(1)} %bitcast.28), channel_id=1, source_target_pairs={{32,64},{96,128},{160,192},{224,256},{288,320},{352,384},{416,448}... | collective-permute-start | bytes 786440 | tf_op jit(solution)/shard_map/ppermute | solution.py:262
  51.4 0.1 pad_add_fusion.place_ref.refs_0_
  51.5 0.9 shard_map.79.mask_ref
  52.3 4.6 %collective-permute-done.other_ref = bf16[256,1024]{1,0:T(8,128)(2,1)S(1)} collective-permute-done((bf16[256,1024]{1,0:T(8,128)(2,1)S(1)}, bf16[256,1024]{1,0:T(8,128)(2,1)S(1)}, u32[]{:S(2)}, u32[]{:S(2)}) %collective-permute-start) | collective-permute-done | bytes 524320 | tf_op jit(solution)/shard_map/ppermute | solution.py:259
  56.9 2.1 %shard_map.80 = (bf16[256,1152]{1,0:T(8,128)(2,1)S(1)}, bf16[256,1152]{1,0:T(8,128)(2,1)S(1)}) custom-call(s32[3]{0:T(128)S(1)} %pad_add_fusion.place_ref.refs_0_, bf16[256,1024]{1,0:T(8,128)(2,1)S(1)} %all_gather.6.own_ref, bf16[256,1024]{1,0:T(8,128)(2,1)S(1)} %collective-permute-done.other_ref, bf16[4,272,1024]{2,1,0:T(8,128)(2,1)S(1)} %all-to-all-done.frames_ref, ...), custom_call_target="tpu_custom_call" | custom-call | tf_op jit(solution)/shard_map/pallas_call | solution.py:211
  59.1 1.9 %collective-permute-start.2 = (bf16[256,1152]{1,0:T(8,128)(2,1)S(1)}, bf16[256,1152]{1,0:T(8,128)(2,1)S(1)}, u32[]{:S(2)}, u32[]{:S(2)}) collective-permute-start(bf16[256,1152]{1,0:T(8,128)(2,1)S(1)} %get-tuple-element.11), channel_id=1, source_target_pairs={{0,2},{2,0},{1,3},{3,1},{4,6},{6,4},{5,7},{7,5},{8,10},{10,8},{9,1... | collective-permute-start | bytes 1769480 | tf_op jit(solution)/shard_map/ppermute | solution.py:279
  61.0 2.0 %collective-permute-done.2 = bf16[256,1152]{1,0:T(8,128)(2,1)S(1)} collective-permute-done((bf16[256,1152]{1,0:T(8,128)(2,1)S(1)}, bf16[256,1152]{1,0:T(8,128)(2,1)S(1)}, u32[]{:S(2)}, u32[]{:S(2)}) %collective-permute-start.2) | collective-permute-done | bytes 589856 | tf_op jit(solution)/shard_map/ppermute | solution.py:279
  63.0 0.1 fusion
  63.1 18.7 %all_to_all.25 = bf16[32,8,1152]{2,1,0:T(8,128)(2,1)S(1)} all-to-all(bf16[32,8,1152]{2,1,0:T(8,128)(2,1)S(1)} %fusion), channel_id=1, replica_groups=mesh['z3'=2,'z2'=2,'z1'=2,'z0'=2,'yh'=2,'x'=4,'c'=2,'yl'=2] {'yl','x','y..., dimensions={0} | all-to-all | bytes 1179648 | tf_op jit(solution)/shard_map/all_to_all | solution.py:223
  81.9 0.9 shard_map.81
  82.8 6.4 %all-to-all-start.2 = ((bf16[8,16,2048]{2,1,0:T(8,128)(2,1)}), bf16[8,16,2048]{2,1,0:T(8,128)(2,1)S(1)}, u32[]{:S(2)}, u32[]{:S(2)}) async-start(bf16[8,16,2048]{2,1,0:T(8,128)(2,1)} %get-tuple-element.13), calls=%async_computation.2 | async-start | bytes 1048576 | tf_op jit(solution)/shard_map/all_to_all | solution.py:223
  89.1 13.1 %all_gather.7.left_ref = bf16[128,2176]{1,0:T(8,128)(2,1)S(1)} all-gather(bf16[16,2176]{1,0:T(8,128)(2,1)S(1)} %get-tuple-element.12), channel_id=1, replica_groups=mesh['z3'=2,'z2'=2,'z1'=2,'z0'=2,'yh'=2,'x'=4,'c'=2,'yl'=2] {'x','c'}, dimensions={0}, use_global_device_ids=true | all-gather | bytes 626688 | tf_op jit(solution)/shard_map/all_gather | solution.py:289
  102.2 1.7 %shard_map.82 = f32[8,56,128]{2,1,0:T(8,128)S(1)} custom-call(f32[8,2048]{1,0:T(8,128)S(1)} %shard_map.79.mask_ref, bf16[128,2176]{1,0:T(8,128)(2,1)S(1)} %all_gather.7.left_ref, bf16[128,2048]{1,0:T(8,128)(2,1)S(1)} %bitcast.23), custom_call_target="tpu_custom_call" | custom-call | tf_op jit(solution)/shard_map/pallas_call | solution.py:211
  103.9 27.9 %all_to_all.26.parts_ref = f32[8,56,128]{2,1,0:T(8,128)S(1)} all-to-all(f32[8,56,128]{2,1,0:T(8,128)S(1)} %shard_map.82), channel_id=1, replica_groups=mesh['z3'=2,'z2'=2,'z1'=2,'z0'=2,'yh'=2,'x'=4,'c'=2,'yl'=2] {'z2','z3','..., dimensions={0} | all-to-all | bytes 458752 | tf_op jit(solution)/shard_map/all_to_all | solution.py:223
  131.8 0.6 shard_map.83
  132.4 3.3 %all-to-all-start.4 = ((f32[8,8,128]{2,1,0:T(8,128)}), f32[8,8,128]{2,1,0:T(8,128)S(1)}, u32[]{:S(2)}, u32[]{:S(2)}) async-start(f32[8,8,128]{2,1,0:T(8,128)} %shard_map.83), calls=%async_computation.4 | async-start | bytes 65536 | tf_op jit(solution)/shard_map/all_to_all | solution.py:223
  135.8 0.1 copy.10.refs_2_
  135.9 5.3 %all-to-all-done.4.refs_1_ = f32[8,8,128]{2,1,0:T(8,128)S(1)} async-done(((f32[8,8,128]{2,1,0:T(8,128)}), f32[8,8,128]{2,1,0:T(8,128)S(1)}, u32[]{:S(2)}, u32[]{:S(2)}) %all-to-all-start.4) | async-done | bytes 32800 | tf_op jit(solution)/shard_map/all_to_all | solution.py:223
  141.1 1.4 %shard_map.84 = (f32[3,2,1024]{2,1,0:T(2,128)}, f32[2,32]{1,0:T(2,128)}) custom-call(s32[3]{0:T(128)S(1)} %pad_add_fusion.place_ref.refs_0_, f32[8,8,128]{2,1,0:T(8,128)S(1)} %all-to-all-done.4.refs_1_, f32[32,1]{1,0:T(8,128)S(1)} %copy.10.refs_2_, f32[1,32]{1,0:T(1,128)S(1)} %bitcast.27), custom_call_target="tpu_custom_call" | custom-call | tf_op jit(solution)/shard_map/pallas_call | solution.py:211
  (11 shorter events, 0.0 us)
Async XLA Ops:
  3.8 5.1 %copy-start = (bf16[2048,16]{0,1:T(8,128)(2,1)S(1)}, bf16[2048,16]{0,1:T(8,128)(2,1)}, u32[]{:S(2)}) copy-start(bf16[2048,16]{0,1:T(8,128)(2,1)} %param.7) | copy-start | bytes 196612
  3.8 5.1 %copy-start.1 = (bf16[2048,16]{0,1:T(8,128)(2,1)S(1)}, bf16[2048,16]{0,1:T(8,128)(2,1)}, u32[]{:S(2)}) copy-start(bf16[2048,16]{0,1:T(8,128)(2,1)} %param.8) | copy-start | bytes 196612
  3.8 44.6 %all-to-all-start = ((bf16[4,272,1024]{2,1,0:T(8,128)(2,1)}), bf16[4,272,1024]{2,1,0:T(8,128)(2,1)S(1)}, u32[]{:S(2)}, u32[]{:S(2)}) async-start(bf16[4,272,1024]{2,1,0:T(8,128)(2,1)} %shard_map.78), calls=%async_computation | async-start | bytes 4456448 | tf_op jit(solution)/shard_map/all_to_all | solution.py:223
  45.9 11.1 %collective-permute-start = (bf16[256,1024]{1,0:T(8,128)(2,1)S(1)}, bf16[256,1024]{1,0:T(8,128)(2,1)S(1)}, u32[]{:S(2)}, u32[]{:S(2)}) collective-permute-start(bf16[256,1024]{1,0:T(8,128)(2,1)S(1)} %all_gather.6.own_ref), channel_id=1, source_target_pairs={{0,32},{32,0},{1,33},{33,1},{2,34},{34,2},{3,35},{35,3},{4,36},{36... | collective-permute-start | bytes 1572872 | tf_op jit(solution)/shard_map/ppermute | solution.py:259
  48.5 8.5 %collective-permute-start.1 = (bf16[128,1024]{1,0:T(8,128)(2,1)S(1)}, bf16[128,1024]{1,0:T(8,128)(2,1)S(1)}, u32[]{:S(2)}, u32[]{:S(2)}) collective-permute-start(bf16[128,1024]{1,0:T(8,128)(2,1)S(1)} %bitcast.28), channel_id=1, source_target_pairs={{32,64},{96,128},{160,192},{224,256},{288,320},{352,384},{416,448}... | collective-permute-start | bytes 786440 | tf_op jit(solution)/shard_map/ppermute | solution.py:262
  59.1 3.9 %collective-permute-start.2 = (bf16[256,1152]{1,0:T(8,128)(2,1)S(1)}, bf16[256,1152]{1,0:T(8,128)(2,1)S(1)}, u32[]{:S(2)}, u32[]{:S(2)}) collective-permute-start(bf16[256,1152]{1,0:T(8,128)(2,1)S(1)} %get-tuple-element.11), channel_id=1, source_target_pairs={{0,2},{2,0},{1,3},{3,1},{4,6},{6,4},{5,7},{7,5},{8,10},{10,8},{9,1... | collective-permute-start | bytes 1769480 | tf_op jit(solution)/shard_map/ppermute | solution.py:279
  81.9 53.9 %copy-start.2 = (f32[32]{0:T(128)S(1)}, f32[32]{0:T(128)}, u32[]{:S(2)}) copy-start(f32[32]{0:T(128)} %param.11) | copy-start | bytes 388
  82.8 19.5 %all-to-all-start.2 = ((bf16[8,16,2048]{2,1,0:T(8,128)(2,1)}), bf16[8,16,2048]{2,1,0:T(8,128)(2,1)S(1)}, u32[]{:S(2)}, u32[]{:S(2)}) async-start(bf16[8,16,2048]{2,1,0:T(8,128)(2,1)} %get-tuple-element.13), calls=%async_computation.2 | async-start | bytes 1048576 | tf_op jit(solution)/shard_map/all_to_all | solution.py:223
  132.4 8.7 %all-to-all-start.4 = ((f32[8,8,128]{2,1,0:T(8,128)}), f32[8,8,128]{2,1,0:T(8,128)S(1)}, u32[]{:S(2)}, u32[]{:S(2)}) async-start(f32[8,8,128]{2,1,0:T(8,128)} %shard_map.83), calls=%async_computation.4 | async-start | bytes 65536 | tf_op jit(solution)/shard_map/all_to_all | solution.py:223

commit v10 on v9

--- a/solution.py
+++ b/solution.py
@@ -18,7 +18,7 @@
 FE = ("x", "c")
 PLANE = ("yl", "x", "yh", "z0")
 RIGHT = ("yl", "z0", "yh")
-FAR = ("z2", "z3", "z1")
+FAR = ("z1", "z2", "z3")
 
 
 def one_hot(rows, cols, hit):
@@ -36,25 +36,30 @@
 
 
 def halves_kernel(lag_ref, seg_hbm, frames_ref, out_ref, rows_ref, seg_ref, sems):
-    seg_load = pltpu.make_async_copy(seg_hbm, seg_ref, sems.at[6])
+    seg_load = pltpu.make_async_copy(seg_hbm, seg_ref, sems.at[12])
     seg_load.start()
     loads = []
-    for half in range(2):
-        part = frames_ref.at[0, :, pl.ds(half * 1024, 1024)]
-        load = pltpu.make_async_copy(part, rows_ref.at[half, pl.ds(0, 256)], sems.at[half])
+    for n in range(4):
+        half, rows = n // 2, pl.ds((n % 2) * 128, 128)
+        part = frames_ref.at[0, rows, pl.ds(half * 1024, 1024)]
+        load = pltpu.make_async_copy(part, rows_ref.at[half, rows], sems.at[n])
         load.start()
         loads.append(load)
     seg_load.wait()
     seg = jnp.concatenate([seg_ref[...], jnp.zeros((1, 64), I32)], axis=1)
     row = lax.broadcasted_iota(I32, (16, 128), 0)
     info = jnp.where(row == 0, seg >> 8, jnp.where(row == 1, seg & 255, lag_ref[0]))
-    stores = []
     for half in range(2):
         rows_ref[half, 256:, :128] = info.astype(F32).astype(BF)
         rows_ref[half, 256:, 128:] = jnp.zeros((16, 896), BF)
-        loads[half].wait()
-        for i in (half * 2, half * 2 + 1):
-            store = pltpu.make_async_copy(rows_ref.at[half], out_ref.at[i], sems.at[2 + i])
+    stores = []
+    for n in range(4):
+        half, rows = n // 2, pl.ds(0, 128) if n % 2 == 0 else pl.ds(128, 144)
+        loads[n].wait()
+        for i in range(2):
+            store = pltpu.make_async_copy(
+                rows_ref.at[half, rows], out_ref.at[half * 2 + i, rows], sems.at[4 + n * 2 + i]
+            )
             store.start()
             stores.append(store)
     for store in stores:
@@ -157,7 +162,7 @@
     for m, lhs in enumerate((left * start_bf, lagged * end_bf, left * end_bf)):
         block = lax.dot_general(lhs, now_bf, NT, preferred_element_type=F32)
         for d in range(8):
-            at = (d >> 1 & 1) * 4 + (d >> 2) * 2 + (d & 1)
+            at = sum(((d >> int(a[1]) - 1) & 1) << (2 - i) for i, a in enumerate(FAR))
             out_ref[at, m * 16 : (m + 1) * 16, :] = block[d * 16 : (d + 1) * 16, :]
     var = lax.dot_general(
         jnp.ones((8, 2048), F32), now * now * keep_end, NT, precision=HI, preferred_element_type=F32
@@ -242,7 +247,7 @@
         scratch_shapes=[
             pltpu.VMEM((2, 272, 1024), BF),
             pltpu.VMEM((1, 64), I32),
-            pltpu.SemaphoreType.DMA((7,)),
+            pltpu.SemaphoreType.DMA((13,)),
         ],
         compiler_params=VMEM,
     )(

time: 143 us -> 140 us (0.979)
  blocking collectives: 96.7 us -> 94 us
    all_to_all x2, blocking collectives: 46.6 us -> 44 us  [all_to_all(): return lax.all_to_all(x, axes, split_axis=0, concat_axis=0, tiled=True)]
where the time goes in v10:
time: 140 us
  blocking collectives  94 us (67%)
  starting transfers between devices  22.1 us (16%)
  waiting for transfers between devices  11.9 us (8%)
  Pallas kernels  10.2 us (7%)
  between operations  1.41 us (1%)
    all_to_all x2, blocking collectives, all_to_all(): return lax.all_to_all(x, axes, split_axis=0, concat_axis=0, tiled=True)  44 us
    all_gather x1, blocking collectives, local(): panel_own = lax.all_gather(packed, Z8, axis=0, tiled=True)  36.9 us
    all_to_all x3, starting transfers between devices, all_to_all(): return lax.all_to_all(x, axes, split_axis=0, concat_axis=0, tiled=True)  14.7 us
    all_gather x1, blocking collectives, local(): left = lax.all_gather(basis, FE, axis=0, tiled=True)  13.1 us
    pallas_call x7, Pallas kernels, call(): pl.pallas_call(kernel, out_shape=shapes, in_specs=specs, out_specs=outs,...  7.73 us
    all_to_all x3, waiting for transfers between devices, all_to_all(): return lax.all_to_all(x, axes, split_axis=0, concat_axis=0, tiled=True)  5.27 us
    ppermute x1, waiting for transfers between devices, local(): panel_other = lax.ppermute(panel_own, 'z0', [(0, 1), (1, 0)])  4.62 us
    ppermute x1, starting transfers between devices, local(): lax.ppermute(by_run[:, 1, 192:256].reshape(128, 1024), Z, [(i, i + 1) for...  2.91 us
  transfers between devices with their start and end apart: 6, of which 3 were waited for; matrix products, arithmetic and copies ran while one was open for 0% of the time, Pallas kernels for 1%

profile of v10, /device:TPU:40, one launch (start us, length us, event | category | flops | bytes accessed | tf_op | source)
XLA Modules:
  0.0 139.9 jit_solution(8475177005495288763)
XLA Ops:
  1.3 2.5 %shard_map.78 = bf16[4,272,1024]{2,1,0:T(8,128)(2,1)} custom-call(s32[1]{0:T(128)S(6)} %copy.13.lag_ref, s32[1,64]{1,0:T(1,128)} %seg_hbm.1, bf16[1,256,2048]{2,1,0:T(8,128)(2,1)} %frames_ref.1), custom_call_target="tpu_custom_call" | custom-call | tf_op jit(solution)/shard_map/pallas_call | solution.py:238
  3.8 5.1 %all-to-all-start = ((bf16[4,272,1024]{2,1,0:T(8,128)(2,1)}), bf16[4,272,1024]{2,1,0:T(8,128)(2,1)S(1)}, u32[]{:S(2)}, u32[]{:S(2)}) async-start(bf16[4,272,1024]{2,1,0:T(8,128)(2,1)} %shard_map.78), calls=%async_computation | async-start | bytes 4456448 | tf_op jit(solution)/shard_map/all_to_all | solution.py:228
  8.8 0.1 shard_map.77
  9.0 36.9 %all_gather.6.own_ref = bf16[256,1024]{1,0:T(8,128)(2,1)S(1)} all-gather(bf16[32,1024]{1,0:T(8,128)(2,1)S(1)} %shard_map.77), channel_id=1, replica_groups=mesh['z3'=2,'z2'=2,'z1'=2,'z0'=2,'yh'=2,'x'=4,'c'=2,'yl'=2] {'z3','z2','..., dimensions={0}, use_global_device_ids=true | all-gather | bytes 589824 | tf_op jit(solution)/shard_map/all_gather | solution.py:263
  45.8 2.5 %collective-permute-start = (bf16[256,1024]{1,0:T(8,128)(2,1)S(1)}, bf16[256,1024]{1,0:T(8,128)(2,1)S(1)}, u32[]{:S(2)}, u32[]{:S(2)}) collective-permute-start(bf16[256,1024]{1,0:T(8,128)(2,1)S(1)} %all_gather.6.own_ref), channel_id=1, source_target_pairs={{0,32},{32,0},{1,33},{33,1},{2,34},{34,2},{3,35},{35,3},{4,36},{36... | collective-permute-start | bytes 1572872 | tf_op jit(solution)/shard_map/ppermute | solution.py:264
  48.4 2.9 %collective-permute-start.1 = (bf16[128,1024]{1,0:T(8,128)(2,1)S(1)}, bf16[128,1024]{1,0:T(8,128)(2,1)S(1)}, u32[]{:S(2)}, u32[]{:S(2)}) collective-permute-start(bf16[128,1024]{1,0:T(8,128)(2,1)S(1)} %bitcast.28), channel_id=1, source_target_pairs={{32,64},{96,128},{160,192},{224,256},{288,320},{352,384},{416,448}... | collective-permute-start | bytes 786440 | tf_op jit(solution)/shard_map/ppermute | solution.py:267
  51.3 0.1 pad_add_fusion.place_ref.refs_0_
  51.4 0.9 shard_map.79.mask_ref
  52.3 4.6 %collective-permute-done.other_ref = bf16[256,1024]{1,0:T(8,128)(2,1)S(1)} collective-permute-done((bf16[256,1024]{1,0:T(8,128)(2,1)S(1)}, bf16[256,1024]{1,0:T(8,128)(2,1)S(1)}, u32[]{:S(2)}, u32[]{:S(2)}) %collective-permute-start) | collective-permute-done | bytes 524320 | tf_op jit(solution)/shard_map/ppermute | solution.py:264
  56.9 2.1 %shard_map.80 = (bf16[256,1152]{1,0:T(8,128)(2,1)S(1)}, bf16[256,1152]{1,0:T(8,128)(2,1)S(1)}) custom-call(s32[3]{0:T(128)S(1)} %pad_add_fusion.place_ref.refs_0_, bf16[256,1024]{1,0:T(8,128)(2,1)S(1)} %all_gather.6.own_ref, bf16[256,1024]{1,0:T(8,128)(2,1)S(1)} %collective-permute-done.other_ref, bf16[4,272,1024]{2,1,0:T(8,128)(2,1)S(1)} %all-to-all-done.frames_ref, ...), custom_call_target="tpu_custom_call" | custom-call | tf_op jit(solution)/shard_map/pallas_call | solution.py:216
  59.1 1.9 %collective-permute-start.2 = (bf16[256,1152]{1,0:T(8,128)(2,1)S(1)}, bf16[256,1152]{1,0:T(8,128)(2,1)S(1)}, u32[]{:S(2)}, u32[]{:S(2)}) collective-permute-start(bf16[256,1152]{1,0:T(8,128)(2,1)S(1)} %get-tuple-element.11), channel_id=1, source_target_pairs={{0,2},{2,0},{1,3},{3,1},{4,6},{6,4},{5,7},{7,5},{8,10},{10,8},{9,1... | collective-permute-start | bytes 1769480 | tf_op jit(solution)/shard_map/ppermute | solution.py:284
  61.0 2.0 %collective-permute-done.2 = bf16[256,1152]{1,0:T(8,128)(2,1)S(1)} collective-permute-done((bf16[256,1152]{1,0:T(8,128)(2,1)S(1)}, bf16[256,1152]{1,0:T(8,128)(2,1)S(1)}, u32[]{:S(2)}, u32[]{:S(2)}) %collective-permute-start.2) | collective-permute-done | bytes 589856 | tf_op jit(solution)/shard_map/ppermute | solution.py:284
  63.0 0.1 fusion
  63.1 18.7 %all_to_all.25 = bf16[32,8,1152]{2,1,0:T(8,128)(2,1)S(1)} all-to-all(bf16[32,8,1152]{2,1,0:T(8,128)(2,1)S(1)} %fusion), channel_id=1, replica_groups=mesh['z3'=2,'z2'=2,'z1'=2,'z0'=2,'yh'=2,'x'=4,'c'=2,'yl'=2] {'yl','x','y..., dimensions={0} | all-to-all | bytes 1179648 | tf_op jit(solution)/shard_map/all_to_all | solution.py:228
  81.8 0.9 shard_map.81
  82.7 6.4 %all-to-all-start.2 = ((bf16[8,16,2048]{2,1,0:T(8,128)(2,1)}), bf16[8,16,2048]{2,1,0:T(8,128)(2,1)S(1)}, u32[]{:S(2)}, u32[]{:S(2)}) async-start(bf16[8,16,2048]{2,1,0:T(8,128)(2,1)} %get-tuple-element.13), calls=%async_computation.2 | async-start | bytes 1048576 | tf_op jit(solution)/shard_map/all_to_all | solution.py:228
  89.1 13.1 %all_gather.7.left_ref = bf16[128,2176]{1,0:T(8,128)(2,1)S(1)} all-gather(bf16[16,2176]{1,0:T(8,128)(2,1)S(1)} %get-tuple-element.12), channel_id=1, replica_groups=mesh['z3'=2,'z2'=2,'z1'=2,'z0'=2,'yh'=2,'x'=4,'c'=2,'yl'=2] {'x','c'}, dimensions={0}, use_global_device_ids=true | all-gather | bytes 626688 | tf_op jit(solution)/shard_map/all_gather | solution.py:294
  102.2 1.7 %shard_map.82 = f32[8,56,128]{2,1,0:T(8,128)S(1)} custom-call(f32[8,2048]{1,0:T(8,128)S(1)} %shard_map.79.mask_ref, bf16[128,2176]{1,0:T(8,128)(2,1)S(1)} %all_gather.7.left_ref, bf16[128,2048]{1,0:T(8,128)(2,1)S(1)} %bitcast.23), custom_call_target="tpu_custom_call" | custom-call | tf_op jit(solution)/shard_map/pallas_call | solution.py:216
  103.9 25.3 %all_to_all.26.parts_ref = f32[8,56,128]{2,1,0:T(8,128)S(1)} all-to-all(f32[8,56,128]{2,1,0:T(8,128)S(1)} %shard_map.82), channel_id=1, replica_groups=mesh['z3'=2,'z2'=2,'z1'=2,'z0'=2,'yh'=2,'x'=4,'c'=2,'yl'=2] {'z1','z2','..., dimensions={0} | all-to-all | bytes 458752 | tf_op jit(solution)/shard_map/all_to_all | solution.py:228
  129.1 0.6 shard_map.83
  129.7 3.3 %all-to-all-start.4 = ((f32[8,8,128]{2,1,0:T(8,128)}), f32[8,8,128]{2,1,0:T(8,128)S(1)}, u32[]{:S(2)}, u32[]{:S(2)}) async-start(f32[8,8,128]{2,1,0:T(8,128)} %shard_map.83), calls=%async_computation.4 | async-start | bytes 65536 | tf_op jit(solution)/shard_map/all_to_all | solution.py:228
  133.1 0.1 copy.10.refs_2_
  133.2 5.3 %all-to-all-done.4.refs_1_ = f32[8,8,128]{2,1,0:T(8,128)S(1)} async-done(((f32[8,8,128]{2,1,0:T(8,128)}), f32[8,8,128]{2,1,0:T(8,128)S(1)}, u32[]{:S(2)}, u32[]{:S(2)}) %all-to-all-start.4) | async-done | bytes 32800 | tf_op jit(solution)/shard_map/all_to_all | solution.py:228
  138.4 1.4 %shard_map.84 = (f32[3,2,1024]{2,1,0:T(2,128)}, f32[2,32]{1,0:T(2,128)}) custom-call(s32[3]{0:T(128)S(1)} %pad_add_fusion.place_ref.refs_0_, f32[8,8,128]{2,1,0:T(8,128)S(1)} %all-to-all-done.4.refs_1_, f32[32,1]{1,0:T(8,128)S(1)} %copy.10.refs_2_, f32[1,32]{1,0:T(1,128)S(1)} %bitcast.27), custom_call_target="tpu_custom_call" | custom-call | tf_op jit(solution)/shard_map/pallas_call | solution.py:216
  (11 shorter events, 0.0 us)
Async XLA Ops:
  3.7 5.1 %copy-start = (bf16[2048,16]{0,1:T(8,128)(2,1)S(1)}, bf16[2048,16]{0,1:T(8,128)(2,1)}, u32[]{:S(2)}) copy-start(bf16[2048,16]{0,1:T(8,128)(2,1)} %param.7) | copy-start | bytes 196612
  3.7 5.1 %copy-start.1 = (bf16[2048,16]{0,1:T(8,128)(2,1)S(1)}, bf16[2048,16]{0,1:T(8,128)(2,1)}, u32[]{:S(2)}) copy-start(bf16[2048,16]{0,1:T(8,128)(2,1)} %param.8) | copy-start | bytes 196612
  3.8 44.6 %all-to-all-start = ((bf16[4,272,1024]{2,1,0:T(8,128)(2,1)}), bf16[4,272,1024]{2,1,0:T(8,128)(2,1)S(1)}, u32[]{:S(2)}, u32[]{:S(2)}) async-start(bf16[4,272,1024]{2,1,0:T(8,128)(2,1)} %shard_map.78), calls=%async_computation | async-start | bytes 4456448 | tf_op jit(solution)/shard_map/all_to_all | solution.py:228
  45.8 11.1 %collective-permute-start = (bf16[256,1024]{1,0:T(8,128)(2,1)S(1)}, bf16[256,1024]{1,0:T(8,128)(2,1)S(1)}, u32[]{:S(2)}, u32[]{:S(2)}) collective-permute-start(bf16[256,1024]{1,0:T(8,128)(2,1)S(1)} %all_gather.6.own_ref), channel_id=1, source_target_pairs={{0,32},{32,0},{1,33},{33,1},{2,34},{34,2},{3,35},{35,3},{4,36},{36... | collective-permute-start | bytes 1572872 | tf_op jit(solution)/shard_map/ppermute | solution.py:264
  48.4 8.5 %collective-permute-start.1 = (bf16[128,1024]{1,0:T(8,128)(2,1)S(1)}, bf16[128,1024]{1,0:T(8,128)(2,1)S(1)}, u32[]{:S(2)}, u32[]{:S(2)}) collective-permute-start(bf16[128,1024]{1,0:T(8,128)(2,1)S(1)} %bitcast.28), channel_id=1, source_target_pairs={{32,64},{96,128},{160,192},{224,256},{288,320},{352,384},{416,448}... | collective-permute-start | bytes 786440 | tf_op jit(solution)/shard_map/ppermute | solution.py:267
  59.1 3.9 %collective-permute-start.2 = (bf16[256,1152]{1,0:T(8,128)(2,1)S(1)}, bf16[256,1152]{1,0:T(8,128)(2,1)S(1)}, u32[]{:S(2)}, u32[]{:S(2)}) collective-permute-start(bf16[256,1152]{1,0:T(8,128)(2,1)S(1)} %get-tuple-element.11), channel_id=1, source_target_pairs={{0,2},{2,0},{1,3},{3,1},{4,6},{6,4},{5,7},{7,5},{8,10},{10,8},{9,1... | collective-permute-start | bytes 1769480 | tf_op jit(solution)/shard_map/ppermute | solution.py:284
  81.8 51.2 %copy-start.2 = (f32[32]{0:T(128)S(1)}, f32[32]{0:T(128)}, u32[]{:S(2)}) copy-start(f32[32]{0:T(128)} %param.11) | copy-start | bytes 388
  82.7 19.5 %all-to-all-start.2 = ((bf16[8,16,2048]{2,1,0:T(8,128)(2,1)}), bf16[8,16,2048]{2,1,0:T(8,128)(2,1)S(1)}, u32[]{:S(2)}, u32[]{:S(2)}) async-start(bf16[8,16,2048]{2,1,0:T(8,128)(2,1)} %get-tuple-element.13), calls=%async_computation.2 | async-start | bytes 1048576 | tf_op jit(solution)/shard_map/all_to_all | solution.py:228
  129.7 8.7 %all-to-all-start.4 = ((f32[8,8,128]{2,1,0:T(8,128)}), f32[8,8,128]{2,1,0:T(8,128)S(1)}, u32[]{:S(2)}, u32[]{:S(2)}) async-start(f32[8,8,128]{2,1,0:T(8,128)} %shard_map.83), calls=%async_computation.4 | async-start | bytes 65536 | tf_op jit(solution)/shard_map/all_to_all | solution.py:228

commit v11 on v10

--- a/solution.py
+++ b/solution.py
@@ -66,11 +66,9 @@
         store.wait()
 
 
-def project_kernel(
-    place_ref, own_ref, other_ref, frames_ref, tails_ref, keep_ref, send_ref, panel_ref
-):
-    own_yh = place_ref[0] & 1
-    c = place_ref[2]
+def project_kernel(own_ref, other_ref, frames_ref, tails_ref, keep_ref, send_ref, panel_ref):
+    own_yh = lax.axis_index("z0").astype(I32)
+    c = lax.axis_index("c").astype(I32)
     for kind in range(2):
         z2 = c if kind == 0 else 1 - c
         for yh, ref in ((own_yh, own_ref), (1 - own_yh, other_ref)):
@@ -115,8 +113,8 @@
             basis_ref[:, 2048:] = basis[:, 1024:]
 
 
-def mask_kernel(place_ref, info_ref, out_ref):
-    first = (place_ref[0] >> 1) * 1024
+def mask_kernel(z_ref, info_ref, out_ref):
+    first = (z_ref[0] >> 1) * 1024
     tri = lax.broadcasted_iota(I32, (64, 64), 1) <= lax.broadcasted_iota(I32, (64, 64), 0)
     for rep in range(2):
         info = info_ref[rep].astype(F32)
@@ -182,18 +180,15 @@
         out_ref[f, 6:8, :] = total[48:50, :]
 
 
-def final_kernel(scale, place_ref, parts_ref, ridge_ref, row_ref, cov_ref, score_ref):
-    first = place_ref[1]
+def final_kernel(scale, parts_ref, own_ref, ridge_ref, row_ref, cov_ref, score_ref):
     ridge = ridge_ref[...]
-    lane = lax.broadcasted_iota(I32, (2, 128), 1)
-    row = lax.broadcasted_iota(I32, (2, 128), 0)
     diag = jnp.zeros((2, 1), F32)
     weighted = [jnp.zeros((32, 128), F32) for _ in range(2)]
     for f in range(8):
         total = parts_ref[f] * scale
         for m in range(3):
             cov_ref[m, :, f * 128 : (f + 1) * 128] = total[m * 2 : m * 2 + 2, :]
-        own = lane + f * 128 == first + row
+        own = own_ref[:, f * 128 : (f + 1) * 128] > 0.0
         diag = diag + jnp.sum(jnp.where(own, total[0:2, :], 0.0), axis=1, keepdims=True)
         inverse = 1.0 / (total[6:7, :] + ridge)
         for e in range(2):
@@ -231,9 +226,9 @@
 def local(frames, panel_low, panel_high, lags, seg_lengths, ridge):
     z = lax.axis_index(Z).astype(I32)
     yl = lax.axis_index("yl").astype(I32)
-    c = lax.axis_index("c").astype(I32)
     own_first = ((z * 2 + lax.axis_index("yh")) * 8 + lax.axis_index(FE)) * 4 + yl * 2
-    place = jnp.stack([z, own_first.astype(I32), c])
+    rows = lax.broadcasted_iota(I32, (2, 1024), 0) + own_first.astype(I32)
+    own = (lax.broadcasted_iota(I32, (2, 1024), 1) == rows).astype(F32)
 
     halves = pl.pallas_call(
         halves_kernel,
@@ -267,18 +262,18 @@
     tails = lax.ppermute(
         by_run[:, 1, 192:256].reshape(128, 1024), Z, [(i, i + 1) for i in range(1, 15, 2)]
     )
-    masks = call(mask_kernel, [((8, 2048), F32)], place, by_run[:, 0, 256:, :128], smem=1)
-    panel_other, masks = lax.optimization_barrier((panel_other, masks))
+    masks = call(mask_kernel, [((8, 2048), F32)], z[None], by_run[:, 0, 256:, :128], smem=1)
+    panel_other, masks, own, ridge_column, ridge_row = lax.optimization_barrier(
+        (panel_other, masks, own, ridge[:, None], ridge[None, :])
+    )
 
     keep, send = call(
         project_kernel,
         [((256, 1152), BF)] * 2,
-        place,
         panel_own,
         panel_other,
         frames_h,
         tails,
-        smem=1,
         scratch=[pltpu.VMEM((512, 1024), BF)],
     )
     got = lax.ppermute(send, "c", [(0, 1), (1, 0)])
@@ -301,11 +296,10 @@
     return call(
         lambda *refs: final_kernel(1.0 / 16384.0, *refs),
         [((3, 2, 1024), F32), ((2, 32), F32)],
-        place,
         by_row,
-        ridge[:, None],
-        ridge[None, :],
-        smem=1,
+        own,
+        ridge_column,
+        ridge_row,
     )
 
 

time: 140 us -> 139 us (level)
  Pallas kernels: 10.2 us -> 8.54 us
    pallas_call x7, Pallas kernels: 7.73 us -> 6.09 us  [call(): pl.pallas_call(kernel, out_shape=shapes, in_specs=specs, out_specs=outs,...]
  transfers between devices with their start and end apart: 6 -> 6, of which waited for: 3 -> 3; matrix products, arithmetic and copies ran while one was open for 0% -> 0% of each run, Pallas kernels for 1% -> 0%
where the time goes in v11:
time: 139 us
  blocking collectives  94 us (68%)
  starting transfers between devices  22.1 us (16%)
  waiting for transfers between devices  12.4 us (9%)
  Pallas kernels  8.54 us (6%)
  between operations  1.42 us (1%)
    all_to_all x2, blocking collectives, all_to_all(): return lax.all_to_all(x, axes, split_axis=0, concat_axis=0, tiled=True)  44 us
    all_gather x1, blocking collectives, local(): panel_own = lax.all_gather(packed, Z8, axis=0, tiled=True)  36.9 us
    all_to_all x3, starting transfers between devices, all_to_all(): return lax.all_to_all(x, axes, split_axis=0, concat_axis=0, tiled=True)  14.7 us
    all_gather x1, blocking collectives, local(): left = lax.all_gather(basis, FE, axis=0, tiled=True)  13.1 us
    pallas_call x7, Pallas kernels, call(): pl.pallas_call(kernel, out_shape=shapes, in_specs=specs, out_specs=outs,...  6.09 us
    all_to_all x3, waiting for transfers between devices, all_to_all(): return lax.all_to_all(x, axes, split_axis=0, concat_axis=0, tiled=True)  5.27 us
    ppermute x1, waiting for transfers between devices, local(): panel_other = lax.ppermute(panel_own, 'z0', [(0, 1), (1, 0)])  5.15 us
    ppermute x1, starting transfers between devices, local(): lax.ppermute(by_run[:, 1, 192:256].reshape(128, 1024), Z, [(i, i + 1) for...  2.91 us
  transfers between devices with their start and end apart: 6, of which 3 were waited for; matrix products, arithmetic and copies ran while one was open for 0% of the time, Pallas kernels for 0%

profile of v11, /device:TPU:40, one launch (start us, length us, event | category | flops | bytes accessed | tf_op | source)
XLA Modules:
  0.0 138.8 jit_solution(12144491440466079120)
XLA Ops:
  1.3 2.5 %shard_map.78 = bf16[4,272,1024]{2,1,0:T(8,128)(2,1)} custom-call(s32[1]{0:T(128)S(6)} %copy.13.lag_ref, s32[1,64]{1,0:T(1,128)} %seg_hbm.1, bf16[1,256,2048]{2,1,0:T(8,128)(2,1)} %frames_ref.1), custom_call_target="tpu_custom_call" | custom-call | tf_op jit(solution)/shard_map/pallas_call | solution.py:233
  3.8 5.1 %all-to-all-start = ((bf16[4,272,1024]{2,1,0:T(8,128)(2,1)}), bf16[4,272,1024]{2,1,0:T(8,128)(2,1)S(1)}, u32[]{:S(2)}, u32[]{:S(2)}) async-start(bf16[4,272,1024]{2,1,0:T(8,128)(2,1)} %shard_map.78), calls=%async_computation | async-start | bytes 4456448 | tf_op jit(solution)/shard_map/all_to_all | solution.py:223
  8.8 0.1 shard_map.77
  9.0 36.9 %all_gather.6.own_ref = bf16[256,1024]{1,0:T(8,128)(2,1)S(1)} all-gather(bf16[32,1024]{1,0:T(8,128)(2,1)S(1)} %shard_map.77), channel_id=1, replica_groups=mesh['z3'=2,'z2'=2,'z1'=2,'z0'=2,'yh'=2,'x'=4,'c'=2,'yl'=2] {'z3','z2','..., dimensions={0}, use_global_device_ids=true | all-gather | bytes 589824 | tf_op jit(solution)/shard_map/all_gather | solution.py:258
  45.8 2.5 %collective-permute-start = (bf16[256,1024]{1,0:T(8,128)(2,1)S(1)}, bf16[256,1024]{1,0:T(8,128)(2,1)S(1)}, u32[]{:S(2)}, u32[]{:S(2)}) collective-permute-start(bf16[256,1024]{1,0:T(8,128)(2,1)S(1)} %all_gather.6.own_ref), channel_id=1, source_target_pairs={{0,32},{32,0},{1,33},{33,1},{2,34},{34,2},{3,35},{35,3},{4,36},{36... | collective-permute-start | bytes 1572872 | tf_op jit(solution)/shard_map/ppermute | solution.py:259
  48.4 2.9 %collective-permute-start.1 = (bf16[128,1024]{1,0:T(8,128)(2,1)S(1)}, bf16[128,1024]{1,0:T(8,128)(2,1)S(1)}, u32[]{:S(2)}, u32[]{:S(2)}) collective-permute-start(bf16[128,1024]{1,0:T(8,128)(2,1)S(1)} %bitcast.26), channel_id=1, source_target_pairs={{32,64},{96,128},{160,192},{224,256},{288,320},{352,384},{416,448}... | collective-permute-start | bytes 786440 | tf_op jit(solution)/shard_map/ppermute | solution.py:262
  51.3 0.1 compare_convert_fusion.refs_1_
  51.4 0.3 shard_map.79.mask_ref
  51.8 5.2 %collective-permute-done.other_ref = bf16[256,1024]{1,0:T(8,128)(2,1)S(1)} collective-permute-done((bf16[256,1024]{1,0:T(8,128)(2,1)S(1)}, bf16[256,1024]{1,0:T(8,128)(2,1)S(1)}, u32[]{:S(2)}, u32[]{:S(2)}) %collective-permute-start) | collective-permute-done | bytes 524320 | tf_op jit(solution)/shard_map/ppermute | solution.py:259
  56.9 1.6 %shard_map.80 = (bf16[256,1152]{1,0:T(8,128)(2,1)S(1)}, bf16[256,1152]{1,0:T(8,128)(2,1)S(1)}) custom-call(bf16[256,1024]{1,0:T(8,128)(2,1)S(1)} %all_gather.6.own_ref, bf16[256,1024]{1,0:T(8,128)(2,1)S(1)} %collective-permute-done.other_ref, bf16[4,272,1024]{2,1,0:T(8,128)(2,1)S(1)} %all-to-all-done.frames_ref, ...), custom_call_target="tpu_custom_call" | custom-call | tf_op jit(solution)/shard_map/pallas_call | solution.py:211
  58.5 1.9 %collective-permute-start.2 = (bf16[256,1152]{1,0:T(8,128)(2,1)S(1)}, bf16[256,1152]{1,0:T(8,128)(2,1)S(1)}, u32[]{:S(2)}, u32[]{:S(2)}) collective-permute-start(bf16[256,1152]{1,0:T(8,128)(2,1)S(1)} %get-tuple-element.14), channel_id=1, source_target_pairs={{0,2},{2,0},{1,3},{3,1},{4,6},{6,4},{5,7},{7,5},{8,10},{10,8},{9,1... | collective-permute-start | bytes 1769480 | tf_op jit(solution)/shard_map/ppermute | solution.py:279
  60.4 2.0 %collective-permute-done.2 = bf16[256,1152]{1,0:T(8,128)(2,1)S(1)} collective-permute-done((bf16[256,1152]{1,0:T(8,128)(2,1)S(1)}, bf16[256,1152]{1,0:T(8,128)(2,1)S(1)}, u32[]{:S(2)}, u32[]{:S(2)}) %collective-permute-start.2) | collective-permute-done | bytes 589856 | tf_op jit(solution)/shard_map/ppermute | solution.py:279
  62.4 0.1 fusion
  62.5 18.7 %all_to_all.25 = bf16[32,8,1152]{2,1,0:T(8,128)(2,1)S(1)} all-to-all(bf16[32,8,1152]{2,1,0:T(8,128)(2,1)S(1)} %fusion), channel_id=1, replica_groups=mesh['z3'=2,'z2'=2,'z1'=2,'z0'=2,'yh'=2,'x'=4,'c'=2,'yl'=2] {'yl','x','y..., dimensions={0} | all-to-all | bytes 1179648 | tf_op jit(solution)/shard_map/all_to_all | solution.py:223
  81.3 0.9 shard_map.81
  82.2 6.4 %all-to-all-start.2 = ((bf16[8,16,2048]{2,1,0:T(8,128)(2,1)}), bf16[8,16,2048]{2,1,0:T(8,128)(2,1)S(1)}, u32[]{:S(2)}, u32[]{:S(2)}) async-start(bf16[8,16,2048]{2,1,0:T(8,128)(2,1)} %get-tuple-element.16), calls=%async_computation.2 | async-start | bytes 1048576 | tf_op jit(solution)/shard_map/all_to_all | solution.py:223
  88.5 13.1 %all_gather.7.left_ref = bf16[128,2176]{1,0:T(8,128)(2,1)S(1)} all-gather(bf16[16,2176]{1,0:T(8,128)(2,1)S(1)} %get-tuple-element.15), channel_id=1, replica_groups=mesh['z3'=2,'z2'=2,'z1'=2,'z0'=2,'yh'=2,'x'=4,'c'=2,'yl'=2] {'x','c'}, dimensions={0}, use_global_device_ids=true | all-gather | bytes 626688 | tf_op jit(solution)/shard_map/all_gather | solution.py:289
  101.6 1.7 %shard_map.82 = f32[8,56,128]{2,1,0:T(8,128)S(1)} custom-call(f32[8,2048]{1,0:T(8,128)S(1)} %shard_map.79.mask_ref, bf16[128,2176]{1,0:T(8,128)(2,1)S(1)} %all_gather.7.left_ref, bf16[128,2048]{1,0:T(8,128)(2,1)S(1)} %bitcast.21), custom_call_target="tpu_custom_call" | custom-call | tf_op jit(solution)/shard_map/pallas_call | solution.py:211
  103.3 25.3 %all_to_all.26.parts_ref = f32[8,56,128]{2,1,0:T(8,128)S(1)} all-to-all(f32[8,56,128]{2,1,0:T(8,128)S(1)} %shard_map.82), channel_id=1, replica_groups=mesh['z3'=2,'z2'=2,'z1'=2,'z0'=2,'yh'=2,'x'=4,'c'=2,'yl'=2] {'z1','z2','..., dimensions={0} | all-to-all | bytes 458752 | tf_op jit(solution)/shard_map/all_to_all | solution.py:223
  128.6 0.6 shard_map.83
  129.2 3.3 %all-to-all-start.4 = ((f32[8,8,128]{2,1,0:T(8,128)}), f32[8,8,128]{2,1,0:T(8,128)S(1)}, u32[]{:S(2)}, u32[]{:S(2)}) async-start(f32[8,8,128]{2,1,0:T(8,128)} %shard_map.83), calls=%async_computation.4 | async-start | bytes 65536 | tf_op jit(solution)/shard_map/all_to_all | solution.py:223
  132.5 0.1 copy.10.refs_2_
  132.6 5.3 %all-to-all-done.4.refs_0_ = f32[8,8,128]{2,1,0:T(8,128)S(1)} async-done(((f32[8,8,128]{2,1,0:T(8,128)}), f32[8,8,128]{2,1,0:T(8,128)S(1)}, u32[]{:S(2)}, u32[]{:S(2)}) %all-to-all-start.4) | async-done | bytes 32800 | tf_op jit(solution)/shard_map/all_to_all | solution.py:223
  137.9 0.9 shard_map.84
  (12 shorter events, 0.1 us)
Async XLA Ops:
  3.7 5.1 %copy-start = (bf16[2048,16]{0,1:T(8,128)(2,1)S(1)}, bf16[2048,16]{0,1:T(8,128)(2,1)}, u32[]{:S(2)}) copy-start(bf16[2048,16]{0,1:T(8,128)(2,1)} %param.7) | copy-start | bytes 196612
  3.7 5.1 %copy-start.1 = (bf16[2048,16]{0,1:T(8,128)(2,1)S(1)}, bf16[2048,16]{0,1:T(8,128)(2,1)}, u32[]{:S(2)}) copy-start(bf16[2048,16]{0,1:T(8,128)(2,1)} %param.8) | copy-start | bytes 196612
  3.8 44.6 %all-to-all-start = ((bf16[4,272,1024]{2,1,0:T(8,128)(2,1)}), bf16[4,272,1024]{2,1,0:T(8,128)(2,1)S(1)}, u32[]{:S(2)}, u32[]{:S(2)}) async-start(bf16[4,272,1024]{2,1,0:T(8,128)(2,1)} %shard_map.78), calls=%async_computation | async-start | bytes 4456448 | tf_op jit(solution)/shard_map/all_to_all | solution.py:223
  45.8 11.1 %collective-permute-start = (bf16[256,1024]{1,0:T(8,128)(2,1)S(1)}, bf16[256,1024]{1,0:T(8,128)(2,1)S(1)}, u32[]{:S(2)}, u32[]{:S(2)}) collective-permute-start(bf16[256,1024]{1,0:T(8,128)(2,1)S(1)} %all_gather.6.own_ref), channel_id=1, source_target_pairs={{0,32},{32,0},{1,33},{33,1},{2,34},{34,2},{3,35},{35,3},{4,36},{36... | collective-permute-start | bytes 1572872 | tf_op jit(solution)/shard_map/ppermute | solution.py:259
  48.4 8.5 %collective-permute-start.1 = (bf16[128,1024]{1,0:T(8,128)(2,1)S(1)}, bf16[128,1024]{1,0:T(8,128)(2,1)S(1)}, u32[]{:S(2)}, u32[]{:S(2)}) collective-permute-start(bf16[128,1024]{1,0:T(8,128)(2,1)S(1)} %bitcast.26), channel_id=1, source_target_pairs={{32,64},{96,128},{160,192},{224,256},{288,320},{352,384},{416,448}... | collective-permute-start | bytes 786440 | tf_op jit(solution)/shard_map/ppermute | solution.py:262
  58.5 3.9 %collective-permute-start.2 = (bf16[256,1152]{1,0:T(8,128)(2,1)S(1)}, bf16[256,1152]{1,0:T(8,128)(2,1)S(1)}, u32[]{:S(2)}, u32[]{:S(2)}) collective-permute-start(bf16[256,1152]{1,0:T(8,128)(2,1)S(1)} %get-tuple-element.14), channel_id=1, source_target_pairs={{0,2},{2,0},{1,3},{3,1},{4,6},{6,4},{5,7},{7,5},{8,10},{10,8},{9,1... | collective-permute-start | bytes 1769480 | tf_op jit(solution)/shard_map/ppermute | solution.py:279
  81.3 51.2 %copy-start.2 = (f32[32]{0:T(128)S(1)}, f32[32]{0:T(128)}, u32[]{:S(2)}) copy-start(f32[32]{0:T(128)} %param.11) | copy-start | bytes 388
  82.2 19.5 %all-to-all-start.2 = ((bf16[8,16,2048]{2,1,0:T(8,128)(2,1)}), bf16[8,16,2048]{2,1,0:T(8,128)(2,1)S(1)}, u32[]{:S(2)}, u32[]{:S(2)}) async-start(bf16[8,16,2048]{2,1,0:T(8,128)(2,1)} %get-tuple-element.16), calls=%async_computation.2 | async-start | bytes 1048576 | tf_op jit(solution)/shard_map/all_to_all | solution.py:223
  129.2 8.7 %all-to-all-start.4 = ((f32[8,8,128]{2,1,0:T(8,128)}), f32[8,8,128]{2,1,0:T(8,128)S(1)}, u32[]{:S(2)}, u32[]{:S(2)}) async-start(f32[8,8,128]{2,1,0:T(8,128)} %shard_map.83), calls=%async_computation.4 | async-start | bytes 65536 | tf_op jit(solution)/shard_map/all_to_all | solution.py:223

commit v12 on v11

--- a/solution.py
+++ b/solution.py
@@ -161,23 +161,31 @@
         block = lax.dot_general(lhs, now_bf, NT, preferred_element_type=F32)
         for d in range(8):
             at = sum(((d >> int(a[1]) - 1) & 1) << (2 - i) for i, a in enumerate(FAR))
-            out_ref[at, m * 16 : (m + 1) * 16, :] = block[d * 16 : (d + 1) * 16, :]
+            value = block[d * 16 : (d + 1) * 16, :]
+            high = value.astype(BF)
+            out_ref[at, m * 16 : (m + 1) * 16, :] = high
+            out_ref[at, 48 + m * 16 : 64 + m * 16, :] = (value - high.astype(F32)).astype(BF)
     var = lax.dot_general(
         jnp.ones((8, 2048), F32), now * now * keep_end, NT, precision=HI, preferred_element_type=F32
     )
+    high = var.astype(BF).astype(F32)
+    row = lax.broadcasted_iota(I32, (8, 128), 0)
+    var = jnp.where(row == 0, high, var - high).astype(BF)
     for d in range(8):
-        out_ref[d, 48:56, :] = var
+        out_ref[d, 96:104, :] = var
 
 
 def rows_kernel(parts_ref, out_ref):
-    total = parts_ref[0]
+    total = parts_ref[0].astype(F32)
     for d in range(1, 8):
-        total = total + parts_ref[d]
+        total = total + parts_ref[d].astype(F32)
+    var = total[96:97, :] + total[97:98, :]
+    total = total[:48, :] + total[48:96, :]
     for f in range(8):
         for m in range(3):
             src = m * 16 + f * 2
             out_ref[f, m * 2 : m * 2 + 2, :] = total[src : src + 2, :]
-        out_ref[f, 6:8, :] = total[48:50, :]
+        out_ref[f, 6:8, :] = jnp.broadcast_to(var, (2, 128))
 
 
 def final_kernel(scale, parts_ref, own_ref, ridge_ref, row_ref, cov_ref, score_ref):
@@ -289,7 +297,7 @@
     left = lax.all_gather(basis, FE, axis=0, tiled=True)
 
     terms = call(
-        cov_kernel, [((8, 56, 128), F32)], masks, left, right.reshape(128, 2048)
+        cov_kernel, [((8, 104, 128), BF)], masks, left, right.reshape(128, 2048)
     )
     rows = call(rows_kernel, [((8, 8, 128), F32)], all_to_all(terms, FAR))
     by_row = all_to_all(rows, FE)

time: 139 us -> 139 us (level)
  no operation moved by 1% of the time
where the time goes in v12:
time: 139 us
  blocking collectives  93.9 us (68%)
  starting transfers between devices  22.1 us (16%)
  waiting for transfers between devices  12.4 us (9%)
  Pallas kernels  8.56 us (6%)
  between operations  1.42 us (1%)
    all_to_all x2, blocking collectives, all_to_all(): return lax.all_to_all(x, axes, split_axis=0, concat_axis=0, tiled=True)  43.9 us
    all_gather x1, blocking collectives, local(): panel_own = lax.all_gather(packed, Z8, axis=0, tiled=True)  36.9 us
    all_to_all x3, starting transfers between devices, all_to_all(): return lax.all_to_all(x, axes, split_axis=0, concat_axis=0, tiled=True)  14.7 us
    all_gather x1, blocking collectives, local(): left = lax.all_gather(basis, FE, axis=0, tiled=True)  13.1 us
    pallas_call x7, Pallas kernels, call(): pl.pallas_call(kernel, out_shape=shapes, in_specs=specs, out_specs=outs,...  6.11 us
    all_to_all x3, waiting for transfers between devices, all_to_all(): return lax.all_to_all(x, axes, split_axis=0, concat_axis=0, tiled=True)  5.27 us
    ppermute x1, waiting for transfers between devices, local(): panel_other = lax.ppermute(panel_own, 'z0', [(0, 1), (1, 0)])  5.15 us
    ppermute x1, starting transfers between devices, local(): lax.ppermute(by_run[:, 1, 192:256].reshape(128, 1024), Z, [(i, i + 1) for...  2.91 us
  transfers between devices with their start and end apart: 6, of which 3 were waited for; matrix products, arithmetic and copies ran while one was open for 0% of the time, Pallas kernels for 0%

profile of v12, /device:TPU:40, one launch (start us, length us, event | category | flops | bytes accessed | tf_op | source)
XLA Modules:
  0.0 138.7 jit_solution(7510121378384300766)
XLA Ops:
  1.3 2.5 %shard_map.78 = bf16[4,272,1024]{2,1,0:T(8,128)(2,1)} custom-call(s32[1]{0:T(128)S(6)} %copy.13.lag_ref, s32[1,64]{1,0:T(1,128)} %seg_hbm.1, bf16[1,256,2048]{2,1,0:T(8,128)(2,1)} %frames_ref.1), custom_call_target="tpu_custom_call" | custom-call | tf_op jit(solution)/shard_map/pallas_call | solution.py:241
  3.8 5.1 %all-to-all-start = ((bf16[4,272,1024]{2,1,0:T(8,128)(2,1)}), bf16[4,272,1024]{2,1,0:T(8,128)(2,1)S(1)}, u32[]{:S(2)}, u32[]{:S(2)}) async-start(bf16[4,272,1024]{2,1,0:T(8,128)(2,1)} %shard_map.78), calls=%async_computation | async-start | bytes 4456448 | tf_op jit(solution)/shard_map/all_to_all | solution.py:231
  8.8 0.1 shard_map.77
  9.0 36.9 %all_gather.6.own_ref = bf16[256,1024]{1,0:T(8,128)(2,1)S(1)} all-gather(bf16[32,1024]{1,0:T(8,128)(2,1)S(1)} %shard_map.77), channel_id=1, replica_groups=mesh['z3'=2,'z2'=2,'z1'=2,'z0'=2,'yh'=2,'x'=4,'c'=2,'yl'=2] {'z3','z2','..., dimensions={0}, use_global_device_ids=true | all-gather | bytes 589824 | tf_op jit(solution)/shard_map/all_gather | solution.py:266
  45.8 2.5 %collective-permute-start = (bf16[256,1024]{1,0:T(8,128)(2,1)S(1)}, bf16[256,1024]{1,0:T(8,128)(2,1)S(1)}, u32[]{:S(2)}, u32[]{:S(2)}) collective-permute-start(bf16[256,1024]{1,0:T(8,128)(2,1)S(1)} %all_gather.6.own_ref), channel_id=1, source_target_pairs={{0,32},{32,0},{1,33},{33,1},{2,34},{34,2},{3,35},{35,3},{4,36},{36... | collective-permute-start | bytes 1572872 | tf_op jit(solution)/shard_map/ppermute | solution.py:267
  48.4 2.9 %collective-permute-start.1 = (bf16[128,1024]{1,0:T(8,128)(2,1)S(1)}, bf16[128,1024]{1,0:T(8,128)(2,1)S(1)}, u32[]{:S(2)}, u32[]{:S(2)}) collective-permute-start(bf16[128,1024]{1,0:T(8,128)(2,1)S(1)} %bitcast.26), channel_id=1, source_target_pairs={{32,64},{96,128},{160,192},{224,256},{288,320},{352,384},{416,448}... | collective-permute-start | bytes 786440 | tf_op jit(solution)/shard_map/ppermute | solution.py:270
  51.3 0.1 compare_convert_fusion.refs_1_
  51.4 0.3 shard_map.79.mask_ref
  51.8 5.2 %collective-permute-done.other_ref = bf16[256,1024]{1,0:T(8,128)(2,1)S(1)} collective-permute-done((bf16[256,1024]{1,0:T(8,128)(2,1)S(1)}, bf16[256,1024]{1,0:T(8,128)(2,1)S(1)}, u32[]{:S(2)}, u32[]{:S(2)}) %collective-permute-start) | collective-permute-done | bytes 524320 | tf_op jit(solution)/shard_map/ppermute | solution.py:267
  56.9 1.6 %shard_map.80 = (bf16[256,1152]{1,0:T(8,128)(2,1)S(1)}, bf16[256,1152]{1,0:T(8,128)(2,1)S(1)}) custom-call(bf16[256,1024]{1,0:T(8,128)(2,1)S(1)} %all_gather.6.own_ref, bf16[256,1024]{1,0:T(8,128)(2,1)S(1)} %collective-permute-done.other_ref, bf16[4,272,1024]{2,1,0:T(8,128)(2,1)S(1)} %all-to-all-done.frames_ref, ...), custom_call_target="tpu_custom_call" | custom-call | tf_op jit(solution)/shard_map/pallas_call | solution.py:219
  58.5 1.9 %collective-permute-start.2 = (bf16[256,1152]{1,0:T(8,128)(2,1)S(1)}, bf16[256,1152]{1,0:T(8,128)(2,1)S(1)}, u32[]{:S(2)}, u32[]{:S(2)}) collective-permute-start(bf16[256,1152]{1,0:T(8,128)(2,1)S(1)} %get-tuple-element.14), channel_id=1, source_target_pairs={{0,2},{2,0},{1,3},{3,1},{4,6},{6,4},{5,7},{7,5},{8,10},{10,8},{9,1... | collective-permute-start | bytes 1769480 | tf_op jit(solution)/shard_map/ppermute | solution.py:287
  60.4 2.0 %collective-permute-done.2 = bf16[256,1152]{1,0:T(8,128)(2,1)S(1)} collective-permute-done((bf16[256,1152]{1,0:T(8,128)(2,1)S(1)}, bf16[256,1152]{1,0:T(8,128)(2,1)S(1)}, u32[]{:S(2)}, u32[]{:S(2)}) %collective-permute-start.2) | collective-permute-done | bytes 589856 | tf_op jit(solution)/shard_map/ppermute | solution.py:287
  62.4 0.1 fusion
  62.5 18.7 %all_to_all.25 = bf16[32,8,1152]{2,1,0:T(8,128)(2,1)S(1)} all-to-all(bf16[32,8,1152]{2,1,0:T(8,128)(2,1)S(1)} %fusion), channel_id=1, replica_groups=mesh['z3'=2,'z2'=2,'z1'=2,'z0'=2,'yh'=2,'x'=4,'c'=2,'yl'=2] {'yl','x','y..., dimensions={0} | all-to-all | bytes 1179648 | tf_op jit(solution)/shard_map/all_to_all | solution.py:231
  81.3 0.9 shard_map.81
  82.2 6.4 %all-to-all-start.2 = ((bf16[8,16,2048]{2,1,0:T(8,128)(2,1)}), bf16[8,16,2048]{2,1,0:T(8,128)(2,1)S(1)}, u32[]{:S(2)}, u32[]{:S(2)}) async-start(bf16[8,16,2048]{2,1,0:T(8,128)(2,1)} %get-tuple-element.16), calls=%async_computation.2 | async-start | bytes 1048576 | tf_op jit(solution)/shard_map/all_to_all | solution.py:231
  88.5 13.1 %all_gather.7.left_ref = bf16[128,2176]{1,0:T(8,128)(2,1)S(1)} all-gather(bf16[16,2176]{1,0:T(8,128)(2,1)S(1)} %get-tuple-element.15), channel_id=1, replica_groups=mesh['z3'=2,'z2'=2,'z1'=2,'z0'=2,'yh'=2,'x'=4,'c'=2,'yl'=2] {'x','c'}, dimensions={0}, use_global_device_ids=true | all-gather | bytes 626688 | tf_op jit(solution)/shard_map/all_gather | solution.py:297
  101.6 1.7 %shard_map.82 = bf16[8,104,128]{2,1,0:T(8,128)(2,1)S(1)} custom-call(f32[8,2048]{1,0:T(8,128)S(1)} %shard_map.79.mask_ref, bf16[128,2176]{1,0:T(8,128)(2,1)S(1)} %all_gather.7.left_ref, bf16[128,2048]{1,0:T(8,128)(2,1)S(1)} %bitcast.21), custom_call_target="tpu_custom_call" | custom-call | tf_op jit(solution)/shard_map/pallas_call | solution.py:219
  103.3 25.1 %all_to_all.26.parts_ref = bf16[8,104,128]{2,1,0:T(8,128)(2,1)S(1)} all-to-all(bf16[8,104,128]{2,1,0:T(8,128)(2,1)S(1)} %shard_map.82), channel_id=1, replica_groups=mesh['z3'=2,'z2'=2,'z1'=2,'z0'=2,'yh'=2,'x'=4,'c'=2,'yl'=2] {'z1','z2','..., dimensions={0} | all-to-all | bytes 425984 | tf_op jit(solution)/shard_map/all_to_all | solution.py:231
  128.4 0.6 shard_map.83
  129.1 3.3 %all-to-all-start.4 = ((f32[8,8,128]{2,1,0:T(8,128)}), f32[8,8,128]{2,1,0:T(8,128)S(1)}, u32[]{:S(2)}, u32[]{:S(2)}) async-start(f32[8,8,128]{2,1,0:T(8,128)} %shard_map.83), calls=%async_computation.4 | async-start | bytes 65536 | tf_op jit(solution)/shard_map/all_to_all | solution.py:231
  132.4 0.1 copy.10.refs_2_
  132.5 5.3 %all-to-all-done.4.refs_0_ = f32[8,8,128]{2,1,0:T(8,128)S(1)} async-done(((f32[8,8,128]{2,1,0:T(8,128)}), f32[8,8,128]{2,1,0:T(8,128)S(1)}, u32[]{:S(2)}, u32[]{:S(2)}) %all-to-all-start.4) | async-done | bytes 32800 | tf_op jit(solution)/shard_map/all_to_all | solution.py:231
  137.8 0.9 shard_map.84
  (12 shorter events, 0.1 us)
Async XLA Ops:
  3.7 5.1 %copy-start = (bf16[2048,16]{0,1:T(8,128)(2,1)S(1)}, bf16[2048,16]{0,1:T(8,128)(2,1)}, u32[]{:S(2)}) copy-start(bf16[2048,16]{0,1:T(8,128)(2,1)} %param.7) | copy-start | bytes 196612
  3.7 5.1 %copy-start.1 = (bf16[2048,16]{0,1:T(8,128)(2,1)S(1)}, bf16[2048,16]{0,1:T(8,128)(2,1)}, u32[]{:S(2)}) copy-start(bf16[2048,16]{0,1:T(8,128)(2,1)} %param.8) | copy-start | bytes 196612
  3.8 44.6 %all-to-all-start = ((bf16[4,272,1024]{2,1,0:T(8,128)(2,1)}), bf16[4,272,1024]{2,1,0:T(8,128)(2,1)S(1)}, u32[]{:S(2)}, u32[]{:S(2)}) async-start(bf16[4,272,1024]{2,1,0:T(8,128)(2,1)} %shard_map.78), calls=%async_computation | async-start | bytes 4456448 | tf_op jit(solution)/shard_map/all_to_all | solution.py:231
  45.8 11.1 %collective-permute-start = (bf16[256,1024]{1,0:T(8,128)(2,1)S(1)}, bf16[256,1024]{1,0:T(8,128)(2,1)S(1)}, u32[]{:S(2)}, u32[]{:S(2)}) collective-permute-start(bf16[256,1024]{1,0:T(8,128)(2,1)S(1)} %all_gather.6.own_ref), channel_id=1, source_target_pairs={{0,32},{32,0},{1,33},{33,1},{2,34},{34,2},{3,35},{35,3},{4,36},{36... | collective-permute-start | bytes 1572872 | tf_op jit(solution)/shard_map/ppermute | solution.py:267
  48.4 8.5 %collective-permute-start.1 = (bf16[128,1024]{1,0:T(8,128)(2,1)S(1)}, bf16[128,1024]{1,0:T(8,128)(2,1)S(1)}, u32[]{:S(2)}, u32[]{:S(2)}) collective-permute-start(bf16[128,1024]{1,0:T(8,128)(2,1)S(1)} %bitcast.26), channel_id=1, source_target_pairs={{32,64},{96,128},{160,192},{224,256},{288,320},{352,384},{416,448}... | collective-permute-start | bytes 786440 | tf_op jit(solution)/shard_map/ppermute | solution.py:270
  58.5 3.9 %collective-permute-start.2 = (bf16[256,1152]{1,0:T(8,128)(2,1)S(1)}, bf16[256,1152]{1,0:T(8,128)(2,1)S(1)}, u32[]{:S(2)}, u32[]{:S(2)}) collective-permute-start(bf16[256,1152]{1,0:T(8,128)(2,1)S(1)} %get-tuple-element.14), channel_id=1, source_target_pairs={{0,2},{2,0},{1,3},{3,1},{4,6},{6,4},{5,7},{7,5},{8,10},{10,8},{9,1... | collective-permute-start | bytes 1769480 | tf_op jit(solution)/shard_map/ppermute | solution.py:287
  81.3 51.1 %copy-start.2 = (f32[32]{0:T(128)S(1)}, f32[32]{0:T(128)}, u32[]{:S(2)}) copy-start(f32[32]{0:T(128)} %param.11) | copy-start | bytes 388
  82.2 19.5 %all-to-all-start.2 = ((bf16[8,16,2048]{2,1,0:T(8,128)(2,1)}), bf16[8,16,2048]{2,1,0:T(8,128)(2,1)S(1)}, u32[]{:S(2)}, u32[]{:S(2)}) async-start(bf16[8,16,2048]{2,1,0:T(8,128)(2,1)} %get-tuple-element.16), calls=%async_computation.2 | async-start | bytes 1048576 | tf_op jit(solution)/shard_map/all_to_all | solution.py:231
  129.1 8.7 %all-to-all-start.4 = ((f32[8,8,128]{2,1,0:T(8,128)}), f32[8,8,128]{2,1,0:T(8,128)S(1)}, u32[]{:S(2)}, u32[]{:S(2)}) async-start(f32[8,8,128]{2,1,0:T(8,128)} %shard_map.83), calls=%async_computation.4 | async-start | bytes 65536 | tf_op jit(solution)/shard_map/all_to_all | solution.py:231

commit v13 on v12

--- a/solution.py
+++ b/solution.py
@@ -165,9 +165,12 @@
             high = value.astype(BF)
             out_ref[at, m * 16 : (m + 1) * 16, :] = high
             out_ref[at, 48 + m * 16 : 64 + m * 16, :] = (value - high.astype(F32)).astype(BF)
-    var = lax.dot_general(
-        jnp.ones((8, 2048), F32), now * now * keep_end, NT, precision=HI, preferred_element_type=F32
-    )
+    square = now * now * keep_end
+    head = square.astype(BF)
+    rest = (square - head.astype(F32)).astype(BF)
+    ones = jnp.ones((8, 2048), BF)
+    var = lax.dot_general(ones, head, NT, preferred_element_type=F32)
+    var = var + lax.dot_general(ones, rest, NT, preferred_element_type=F32)
     high = var.astype(BF).astype(F32)
     row = lax.broadcasted_iota(I32, (8, 128), 0)
     var = jnp.where(row == 0, high, var - high).astype(BF)

time: 139 us -> 139 us (level)
  no operation moved by 1% of the time
where the time goes in v13:
time: 139 us; the launch traced here: 138 us
  blocking collectives  93.9 us (68%)
  starting transfers between devices  22.1 us (16%)
  waiting for transfers between devices  12.4 us (9%)
  Pallas kernels  8.06 us (6%)
  between operations  1.42 us (1%)
    all_to_all x2, blocking collectives, all_to_all(): return lax.all_to_all(x, axes, split_axis=0, concat_axis=0, tiled=True)  43.9 us
    all_gather x1, blocking collectives, local(): panel_own = lax.all_gather(packed, Z8, axis=0, tiled=True)  36.9 us
    all_to_all x3, starting transfers between devices, all_to_all(): return lax.all_to_all(x, axes, split_axis=0, concat_axis=0, tiled=True)  14.7 us
    all_gather x1, blocking collectives, local(): left = lax.all_gather(basis, FE, axis=0, tiled=True)  13.1 us
    pallas_call x7, Pallas kernels, call(): pl.pallas_call(kernel, out_shape=shapes, in_specs=specs, out_specs=outs,...  5.6 us
    all_to_all x3, waiting for transfers between devices, all_to_all(): return lax.all_to_all(x, axes, split_axis=0, concat_axis=0, tiled=True)  5.27 us
    ppermute x1, waiting for transfers between devices, local(): panel_other = lax.ppermute(panel_own, 'z0', [(0, 1), (1, 0)])  5.15 us
    ppermute x1, starting transfers between devices, local(): lax.ppermute(by_run[:, 1, 192:256].reshape(128, 1024), Z, [(i, i + 1) for...  2.91 us
  transfers between devices with their start and end apart: 6, of which 3 were waited for; matrix products, arithmetic and copies ran while one was open for 0% of the time, Pallas kernels for 0%

profile of v13, /device:TPU:40, one launch (start us, length us, event | category | flops | bytes accessed | tf_op | source)
XLA Modules:
  0.0 138.2 jit_solution(2199712814961839365)
XLA Ops:
  1.3 2.5 %shard_map.78 = bf16[4,272,1024]{2,1,0:T(8,128)(2,1)} custom-call(s32[1]{0:T(128)S(6)} %copy.13.lag_ref, s32[1,64]{1,0:T(1,128)} %seg_hbm.1, bf16[1,256,2048]{2,1,0:T(8,128)(2,1)} %frames_ref.1), custom_call_target="tpu_custom_call" | custom-call | tf_op jit(solution)/shard_map/pallas_call | solution.py:244
  3.8 5.1 %all-to-all-start = ((bf16[4,272,1024]{2,1,0:T(8,128)(2,1)}), bf16[4,272,1024]{2,1,0:T(8,128)(2,1)S(1)}, u32[]{:S(2)}, u32[]{:S(2)}) async-start(bf16[4,272,1024]{2,1,0:T(8,128)(2,1)} %shard_map.78), calls=%async_computation | async-start | bytes 4456448 | tf_op jit(solution)/shard_map/all_to_all | solution.py:234
  8.8 0.1 shard_map.77
  9.0 36.9 %all_gather.6.own_ref = bf16[256,1024]{1,0:T(8,128)(2,1)S(1)} all-gather(bf16[32,1024]{1,0:T(8,128)(2,1)S(1)} %shard_map.77), channel_id=1, replica_groups=mesh['z3'=2,'z2'=2,'z1'=2,'z0'=2,'yh'=2,'x'=4,'c'=2,'yl'=2] {'z3','z2','..., dimensions={0}, use_global_device_ids=true | all-gather | bytes 589824 | tf_op jit(solution)/shard_map/all_gather | solution.py:269
  45.8 2.5 %collective-permute-start = (bf16[256,1024]{1,0:T(8,128)(2,1)S(1)}, bf16[256,1024]{1,0:T(8,128)(2,1)S(1)}, u32[]{:S(2)}, u32[]{:S(2)}) collective-permute-start(bf16[256,1024]{1,0:T(8,128)(2,1)S(1)} %all_gather.6.own_ref), channel_id=1, source_target_pairs={{0,32},{32,0},{1,33},{33,1},{2,34},{34,2},{3,35},{35,3},{4,36},{36... | collective-permute-start | bytes 1572872 | tf_op jit(solution)/shard_map/ppermute | solution.py:270
  48.4 2.9 %collective-permute-start.1 = (bf16[128,1024]{1,0:T(8,128)(2,1)S(1)}, bf16[128,1024]{1,0:T(8,128)(2,1)S(1)}, u32[]{:S(2)}, u32[]{:S(2)}) collective-permute-start(bf16[128,1024]{1,0:T(8,128)(2,1)S(1)} %bitcast.26), channel_id=1, source_target_pairs={{32,64},{96,128},{160,192},{224,256},{288,320},{352,384},{416,448}... | collective-permute-start | bytes 786440 | tf_op jit(solution)/shard_map/ppermute | solution.py:273
  51.3 0.1 compare_convert_fusion.refs_1_
  51.4 0.3 shard_map.79.mask_ref
  51.8 5.2 %collective-permute-done.other_ref = bf16[256,1024]{1,0:T(8,128)(2,1)S(1)} collective-permute-done((bf16[256,1024]{1,0:T(8,128)(2,1)S(1)}, bf16[256,1024]{1,0:T(8,128)(2,1)S(1)}, u32[]{:S(2)}, u32[]{:S(2)}) %collective-permute-start) | collective-permute-done | bytes 524320 | tf_op jit(solution)/shard_map/ppermute | solution.py:270
  56.9 1.6 %shard_map.80 = (bf16[256,1152]{1,0:T(8,128)(2,1)S(1)}, bf16[256,1152]{1,0:T(8,128)(2,1)S(1)}) custom-call(bf16[256,1024]{1,0:T(8,128)(2,1)S(1)} %all_gather.6.own_ref, bf16[256,1024]{1,0:T(8,128)(2,1)S(1)} %collective-permute-done.other_ref, bf16[4,272,1024]{2,1,0:T(8,128)(2,1)S(1)} %all-to-all-done.frames_ref, ...), custom_call_target="tpu_custom_call" | custom-call | tf_op jit(solution)/shard_map/pallas_call | solution.py:222
  58.5 1.9 %collective-permute-start.2 = (bf16[256,1152]{1,0:T(8,128)(2,1)S(1)}, bf16[256,1152]{1,0:T(8,128)(2,1)S(1)}, u32[]{:S(2)}, u32[]{:S(2)}) collective-permute-start(bf16[256,1152]{1,0:T(8,128)(2,1)S(1)} %get-tuple-element.14), channel_id=1, source_target_pairs={{0,2},{2,0},{1,3},{3,1},{4,6},{6,4},{5,7},{7,5},{8,10},{10,8},{9,1... | collective-permute-start | bytes 1769480 | tf_op jit(solution)/shard_map/ppermute | solution.py:290
  60.4 2.0 %collective-permute-done.2 = bf16[256,1152]{1,0:T(8,128)(2,1)S(1)} collective-permute-done((bf16[256,1152]{1,0:T(8,128)(2,1)S(1)}, bf16[256,1152]{1,0:T(8,128)(2,1)S(1)}, u32[]{:S(2)}, u32[]{:S(2)}) %collective-permute-start.2) | collective-permute-done | bytes 589856 | tf_op jit(solution)/shard_map/ppermute | solution.py:290
  62.4 0.1 fusion
  62.5 18.7 %all_to_all.25 = bf16[32,8,1152]{2,1,0:T(8,128)(2,1)S(1)} all-to-all(bf16[32,8,1152]{2,1,0:T(8,128)(2,1)S(1)} %fusion), channel_id=1, replica_groups=mesh['z3'=2,'z2'=2,'z1'=2,'z0'=2,'yh'=2,'x'=4,'c'=2,'yl'=2] {'yl','x','y..., dimensions={0} | all-to-all | bytes 1179648 | tf_op jit(solution)/shard_map/all_to_all | solution.py:234
  81.3 0.9 shard_map.81
  82.2 6.4 %all-to-all-start.2 = ((bf16[8,16,2048]{2,1,0:T(8,128)(2,1)}), bf16[8,16,2048]{2,1,0:T(8,128)(2,1)S(1)}, u32[]{:S(2)}, u32[]{:S(2)}) async-start(bf16[8,16,2048]{2,1,0:T(8,128)(2,1)} %get-tuple-element.16), calls=%async_computation.2 | async-start | bytes 1048576 | tf_op jit(solution)/shard_map/all_to_all | solution.py:234
  88.5 13.1 %all_gather.7.left_ref = bf16[128,2176]{1,0:T(8,128)(2,1)S(1)} all-gather(bf16[16,2176]{1,0:T(8,128)(2,1)S(1)} %get-tuple-element.15), channel_id=1, replica_groups=mesh['z3'=2,'z2'=2,'z1'=2,'z0'=2,'yh'=2,'x'=4,'c'=2,'yl'=2] {'x','c'}, dimensions={0}, use_global_device_ids=true | all-gather | bytes 626688 | tf_op jit(solution)/shard_map/all_gather | solution.py:300
  101.6 1.1 shard_map.82
  102.8 25.1 %all_to_all.26.parts_ref = bf16[8,104,128]{2,1,0:T(8,128)(2,1)S(1)} all-to-all(bf16[8,104,128]{2,1,0:T(8,128)(2,1)S(1)} %shard_map.82), channel_id=1, replica_groups=mesh['z3'=2,'z2'=2,'z1'=2,'z0'=2,'yh'=2,'x'=4,'c'=2,'yl'=2] {'z1','z2','..., dimensions={0} | all-to-all | bytes 425984 | tf_op jit(solution)/shard_map/all_to_all | solution.py:234
  127.9 0.6 shard_map.83
  128.6 3.3 %all-to-all-start.4 = ((f32[8,8,128]{2,1,0:T(8,128)}), f32[8,8,128]{2,1,0:T(8,128)S(1)}, u32[]{:S(2)}, u32[]{:S(2)}) async-start(f32[8,8,128]{2,1,0:T(8,128)} %shard_map.83), calls=%async_computation.4 | async-start | bytes 65536 | tf_op jit(solution)/shard_map/all_to_all | solution.py:234
  131.9 0.1 copy.10.refs_2_
  132.0 5.3 %all-to-all-done.4.refs_0_ = f32[8,8,128]{2,1,0:T(8,128)S(1)} async-done(((f32[8,8,128]{2,1,0:T(8,128)}), f32[8,8,128]{2,1,0:T(8,128)S(1)}, u32[]{:S(2)}, u32[]{:S(2)}) %all-to-all-start.4) | async-done | bytes 32800 | tf_op jit(solution)/shard_map/all_to_all | solution.py:234
  137.3 0.9 shard_map.84
  (12 shorter events, 0.1 us)
Async XLA Ops:
  3.7 5.1 %copy-start = (bf16[2048,16]{0,1:T(8,128)(2,1)S(1)}, bf16[2048,16]{0,1:T(8,128)(2,1)}, u32[]{:S(2)}) copy-start(bf16[2048,16]{0,1:T(8,128)(2,1)} %param.7) | copy-start | bytes 196612
  3.7 5.1 %copy-start.1 = (bf16[2048,16]{0,1:T(8,128)(2,1)S(1)}, bf16[2048,16]{0,1:T(8,128)(2,1)}, u32[]{:S(2)}) copy-start(bf16[2048,16]{0,1:T(8,128)(2,1)} %param.8) | copy-start | bytes 196612
  3.8 44.6 %all-to-all-start = ((bf16[4,272,1024]{2,1,0:T(8,128)(2,1)}), bf16[4,272,1024]{2,1,0:T(8,128)(2,1)S(1)}, u32[]{:S(2)}, u32[]{:S(2)}) async-start(bf16[4,272,1024]{2,1,0:T(8,128)(2,1)} %shard_map.78), calls=%async_computation | async-start | bytes 4456448 | tf_op jit(solution)/shard_map/all_to_all | solution.py:234
  45.8 11.1 %collective-permute-start = (bf16[256,1024]{1,0:T(8,128)(2,1)S(1)}, bf16[256,1024]{1,0:T(8,128)(2,1)S(1)}, u32[]{:S(2)}, u32[]{:S(2)}) collective-permute-start(bf16[256,1024]{1,0:T(8,128)(2,1)S(1)} %all_gather.6.own_ref), channel_id=1, source_target_pairs={{0,32},{32,0},{1,33},{33,1},{2,34},{34,2},{3,35},{35,3},{4,36},{36... | collective-permute-start | bytes 1572872 | tf_op jit(solution)/shard_map/ppermute | solution.py:270
  48.4 8.5 %collective-permute-start.1 = (bf16[128,1024]{1,0:T(8,128)(2,1)S(1)}, bf16[128,1024]{1,0:T(8,128)(2,1)S(1)}, u32[]{:S(2)}, u32[]{:S(2)}) collective-permute-start(bf16[128,1024]{1,0:T(8,128)(2,1)S(1)} %bitcast.26), channel_id=1, source_target_pairs={{32,64},{96,128},{160,192},{224,256},{288,320},{352,384},{416,448}... | collective-permute-start | bytes 786440 | tf_op jit(solution)/shard_map/ppermute | solution.py:273
  58.5 3.9 %collective-permute-start.2 = (bf16[256,1152]{1,0:T(8,128)(2,1)S(1)}, bf16[256,1152]{1,0:T(8,128)(2,1)S(1)}, u32[]{:S(2)}, u32[]{:S(2)}) collective-permute-start(bf16[256,1152]{1,0:T(8,128)(2,1)S(1)} %get-tuple-element.14), channel_id=1, source_target_pairs={{0,2},{2,0},{1,3},{3,1},{4,6},{6,4},{5,7},{7,5},{8,10},{10,8},{9,1... | collective-permute-start | bytes 1769480 | tf_op jit(solution)/shard_map/ppermute | solution.py:290
  81.3 50.6 %copy-start.2 = (f32[32]{0:T(128)S(1)}, f32[32]{0:T(128)}, u32[]{:S(2)}) copy-start(f32[32]{0:T(128)} %param.11) | copy-start | bytes 388
  82.2 19.5 %all-to-all-start.2 = ((bf16[8,16,2048]{2,1,0:T(8,128)(2,1)}), bf16[8,16,2048]{2,1,0:T(8,128)(2,1)S(1)}, u32[]{:S(2)}, u32[]{:S(2)}) async-start(bf16[8,16,2048]{2,1,0:T(8,128)(2,1)} %get-tuple-element.16), calls=%async_computation.2 | async-start | bytes 1048576 | tf_op jit(solution)/shard_map/all_to_all | solution.py:234
  128.6 8.7 %all-to-all-start.4 = ((f32[8,8,128]{2,1,0:T(8,128)}), f32[8,8,128]{2,1,0:T(8,128)S(1)}, u32[]{:S(2)}, u32[]{:S(2)}) async-start(f32[8,8,128]{2,1,0:T(8,128)} %shard_map.83), calls=%async_computation.4 | async-start | bytes 65536 | tf_op jit(solution)/shard_map/all_to_all | solution.py:234

commit v14 on v13

--- a/solution.py
+++ b/solution.py
@@ -297,7 +297,8 @@
     )
 
     right = all_to_all(tiled, RIGHT)
-    left = lax.all_gather(basis, FE, axis=0, tiled=True)
+    left = lax.all_gather(basis, "c", axis=0, tiled=True)
+    left = lax.all_gather(left, "x", axis=0, tiled=True)
 
     terms = call(
         cov_kernel, [((8, 104, 128), BF)], masks, left, right.reshape(128, 2048)

time: 139 us -> 139 us (level)
  the two profiles are of different devices: /device:TPU:40 before, /device:TPU:1 now
where the time goes in v14:
time: 139 us; the launch traced here: 137 us
  blocking collectives  86.3 us (62%)
  starting transfers between devices  29 us (21%)
  waiting for transfers between devices  12.4 us (9%)
  Pallas kernels  8.05 us (6%)
  between operations  1.41 us (1%)
    all_to_all x2, blocking collectives, all_to_all(): return lax.all_to_all(x, axes, split_axis=0, concat_axis=0, tiled=True)  39.8 us
    all_gather x1, blocking collectives, local(): panel_own = lax.all_gather(packed, Z8, axis=0, tiled=True)  32.7 us
    all_to_all x3, starting transfers between devices, all_to_all(): return lax.all_to_all(x, axes, split_axis=0, concat_axis=0, tiled=True)  17.2 us
    all_gather x1, blocking collectives, local(): left = lax.all_gather(left, 'x', axis=0, tiled=True)  10.2 us
    ppermute x1, starting transfers between devices, local(): got = lax.ppermute(send, 'c', [(0, 1), (1, 0)])  8.26 us
    ppermute x1, waiting for transfers between devices, local(): panel_other = lax.ppermute(panel_own, 'z0', [(0, 1), (1, 0)])  6.09 us
    pallas_call x7, Pallas kernels, call(): pl.pallas_call(kernel, out_shape=shapes, in_specs=specs, out_specs=outs,...  5.6 us
    all_to_all x3, waiting for transfers between devices, all_to_all(): return lax.all_to_all(x, axes, split_axis=0, concat_axis=0, tiled=True)  4.65 us
  transfers between devices with their start and end apart: 6, of which 3 were waited for; matrix products, arithmetic and copies ran while one was open for 0% of the time, Pallas kernels for 0%

profile of v14, /device:TPU:1, one launch (start us, length us, event | category | flops | bytes accessed | tf_op | source)
XLA Modules:
  0.0 137.5 jit_solution(10823105534786237403)
XLA Ops:
  1.3 2.5 %shard_map.78 = bf16[4,272,1024]{2,1,0:T(8,128)(2,1)} custom-call(s32[1]{0:T(128)S(6)} %copy.13.lag_ref, s32[1,64]{1,0:T(1,128)} %seg_hbm.1, bf16[1,256,2048]{2,1,0:T(8,128)(2,1)} %frames_ref.1), custom_call_target="tpu_custom_call" | custom-call | tf_op jit(solution)/shard_map/pallas_call | solution.py:244
  3.8 5.2 %all-to-all-start = ((bf16[4,272,1024]{2,1,0:T(8,128)(2,1)}), bf16[4,272,1024]{2,1,0:T(8,128)(2,1)S(1)}, u32[]{:S(2)}, u32[]{:S(2)}) async-start(bf16[4,272,1024]{2,1,0:T(8,128)(2,1)} %shard_map.78), calls=%async_computation | async-start | bytes 4456448 | tf_op jit(solution)/shard_map/all_to_all | solution.py:234
  8.9 0.1 shard_map.77
  9.1 32.7 %all_gather.9.own_ref = bf16[256,1024]{1,0:T(8,128)(2,1)S(1)} all-gather(bf16[32,1024]{1,0:T(8,128)(2,1)S(1)} %shard_map.77), channel_id=1, replica_groups=mesh['z3'=2,'z2'=2,'z1'=2,'z0'=2,'yh'=2,'x'=4,'c'=2,'yl'=2] {'z3','z2','..., dimensions={0}, use_global_device_ids=true | all-gather | bytes 589824 | tf_op jit(solution)/shard_map/all_gather | solution.py:269
  41.7 2.8 %collective-permute-start = (bf16[256,1024]{1,0:T(8,128)(2,1)S(1)}, bf16[256,1024]{1,0:T(8,128)(2,1)S(1)}, u32[]{:S(2)}, u32[]{:S(2)}) collective-permute-start(bf16[256,1024]{1,0:T(8,128)(2,1)S(1)} %all_gather.9.own_ref), channel_id=1, source_target_pairs={{0,32},{32,0},{1,33},{33,1},{2,34},{34,2},{3,35},{35,3},{4,36},{36... | collective-permute-start | bytes 1572872 | tf_op jit(solution)/shard_map/ppermute | solution.py:270
  44.6 0.7 collective-permute-start.1
  45.4 0.3 shard_map.79.mask_ref
  45.7 6.1 %collective-permute-done.other_ref = bf16[256,1024]{1,0:T(8,128)(2,1)S(1)} collective-permute-done((bf16[256,1024]{1,0:T(8,128)(2,1)S(1)}, bf16[256,1024]{1,0:T(8,128)(2,1)S(1)}, u32[]{:S(2)}, u32[]{:S(2)}) %collective-permute-start) | collective-permute-done | bytes 524320 | tf_op jit(solution)/shard_map/ppermute | solution.py:270
  51.8 1.6 %shard_map.80 = (bf16[256,1152]{1,0:T(8,128)(2,1)S(1)}, bf16[256,1152]{1,0:T(8,128)(2,1)S(1)}) custom-call(bf16[256,1024]{1,0:T(8,128)(2,1)S(1)} %all_gather.9.own_ref, bf16[256,1024]{1,0:T(8,128)(2,1)S(1)} %collective-permute-done.other_ref, bf16[4,272,1024]{2,1,0:T(8,128)(2,1)S(1)} %all-to-all-done.frames_ref, ...), custom_call_target="tpu_custom_call" | custom-call | tf_op jit(solution)/shard_map/pallas_call | solution.py:222
  53.4 8.3 %collective-permute-start.2 = (bf16[256,1152]{1,0:T(8,128)(2,1)S(1)}, bf16[256,1152]{1,0:T(8,128)(2,1)S(1)}, u32[]{:S(2)}, u32[]{:S(2)}) collective-permute-start(bf16[256,1152]{1,0:T(8,128)(2,1)S(1)} %get-tuple-element.14), channel_id=1, source_target_pairs={{0,2},{2,0},{1,3},{3,1},{4,6},{6,4},{5,7},{7,5},{8,10},{10,8},{9,1... | collective-permute-start | bytes 1769480 | tf_op jit(solution)/shard_map/ppermute | solution.py:290
  61.7 1.6 %collective-permute-done.2 = bf16[256,1152]{1,0:T(8,128)(2,1)S(1)} collective-permute-done((bf16[256,1152]{1,0:T(8,128)(2,1)S(1)}, bf16[256,1152]{1,0:T(8,128)(2,1)S(1)}, u32[]{:S(2)}, u32[]{:S(2)}) %collective-permute-start.2) | collective-permute-done | bytes 589856 | tf_op jit(solution)/shard_map/ppermute | solution.py:290
  63.3 0.1 fusion
  63.4 20.2 %all_to_all.25 = bf16[32,8,1152]{2,1,0:T(8,128)(2,1)S(1)} all-to-all(bf16[32,8,1152]{2,1,0:T(8,128)(2,1)S(1)} %fusion), channel_id=1, replica_groups=mesh['z3'=2,'z2'=2,'z1'=2,'z0'=2,'yh'=2,'x'=4,'c'=2,'yl'=2] {'yl','x','y..., dimensions={0} | all-to-all | bytes 1179648 | tf_op jit(solution)/shard_map/all_to_all | solution.py:234
  83.7 0.9 shard_map.81
  84.6 3.5 %all-to-all-start.2 = ((bf16[8,16,2048]{2,1,0:T(8,128)(2,1)}), bf16[8,16,2048]{2,1,0:T(8,128)(2,1)S(1)}, u32[]{:S(2)}, u32[]{:S(2)}) async-start(bf16[8,16,2048]{2,1,0:T(8,128)(2,1)} %get-tuple-element.16), calls=%async_computation.2 | async-start | bytes 1048576 | tf_op jit(solution)/shard_map/all_to_all | solution.py:234
  88.1 3.6 %all_gather.10 = bf16[32,2176]{1,0:T(8,128)(2,1)S(1)} all-gather(bf16[16,2176]{1,0:T(8,128)(2,1)S(1)} %get-tuple-element.15), channel_id=1, replica_groups=mesh['z3'=2,'z2'=2,'z1'=2,'z0'=2,'yh'=2,'x'=4,'c'=2,'yl'=2] {'c'}, dimensions={0}, use_global_device_ids=true | all-gather | bytes 208896 | tf_op jit(solution)/shard_map/all_gather | solution.py:300
  91.6 10.2 %all_gather.11.left_ref = bf16[128,2176]{1,0:T(8,128)(2,1)S(1)} all-gather(bf16[32,2176]{1,0:T(8,128)(2,1)S(1)} %all_gather.10), channel_id=1, replica_groups=mesh['z3'=2,'z2'=2,'z1'=2,'z0'=2,'yh'=2,'x'=4,'c'=2,'yl'=2] {'x'}, dimensions={0}, use_global_device_ids=true | all-gather | bytes 696320 | tf_op jit(solution)/shard_map/all_gather | solution.py:301
  101.9 1.1 shard_map.82
  103.0 19.6 %all_to_all.26.parts_ref = bf16[8,104,128]{2,1,0:T(8,128)(2,1)S(1)} all-to-all(bf16[8,104,128]{2,1,0:T(8,128)(2,1)S(1)} %shard_map.82), channel_id=1, replica_groups=mesh['z3'=2,'z2'=2,'z1'=2,'z0'=2,'yh'=2,'x'=4,'c'=2,'yl'=2] {'z1','z2','..., dimensions={0} | all-to-all | bytes 425984 | tf_op jit(solution)/shard_map/all_to_all | solution.py:234
  122.6 0.6 shard_map.83
  123.3 8.6 %all-to-all-start.4 = ((f32[8,8,128]{2,1,0:T(8,128)}), f32[8,8,128]{2,1,0:T(8,128)S(1)}, u32[]{:S(2)}, u32[]{:S(2)}) async-start(f32[8,8,128]{2,1,0:T(8,128)} %shard_map.83), calls=%async_computation.4 | async-start | bytes 65536 | tf_op jit(solution)/shard_map/all_to_all | solution.py:234
  131.8 0.1 copy.10.refs_2_
  131.9 4.6 %all-to-all-done.4.refs_0_ = f32[8,8,128]{2,1,0:T(8,128)S(1)} async-done(((f32[8,8,128]{2,1,0:T(8,128)}), f32[8,8,128]{2,1,0:T(8,128)S(1)}, u32[]{:S(2)}, u32[]{:S(2)}) %all-to-all-start.4) | async-done | bytes 32800 | tf_op jit(solution)/shard_map/all_to_all | solution.py:234
  136.6 0.9 shard_map.84
  (13 shorter events, 0.1 us)
Async XLA Ops:
  3.7 5.2 %copy-start = (bf16[2048,16]{0,1:T(8,128)(2,1)S(1)}, bf16[2048,16]{0,1:T(8,128)(2,1)}, u32[]{:S(2)}) copy-start(bf16[2048,16]{0,1:T(8,128)(2,1)} %param.7) | copy-start | bytes 196612
  3.7 5.2 %copy-start.1 = (bf16[2048,16]{0,1:T(8,128)(2,1)S(1)}, bf16[2048,16]{0,1:T(8,128)(2,1)}, u32[]{:S(2)}) copy-start(bf16[2048,16]{0,1:T(8,128)(2,1)} %param.8) | copy-start | bytes 196612
  3.8 40.9 %all-to-all-start = ((bf16[4,272,1024]{2,1,0:T(8,128)(2,1)}), bf16[4,272,1024]{2,1,0:T(8,128)(2,1)S(1)}, u32[]{:S(2)}, u32[]{:S(2)}) async-start(bf16[4,272,1024]{2,1,0:T(8,128)(2,1)} %shard_map.78), calls=%async_computation | async-start | bytes 4456448 | tf_op jit(solution)/shard_map/all_to_all | solution.py:234
  41.7 10.1 %collective-permute-start = (bf16[256,1024]{1,0:T(8,128)(2,1)S(1)}, bf16[256,1024]{1,0:T(8,128)(2,1)S(1)}, u32[]{:S(2)}, u32[]{:S(2)}) collective-permute-start(bf16[256,1024]{1,0:T(8,128)(2,1)S(1)} %all_gather.9.own_ref), channel_id=1, source_target_pairs={{0,32},{32,0},{1,33},{33,1},{2,34},{34,2},{3,35},{35,3},{4,36},{36... | collective-permute-start | bytes 1572872 | tf_op jit(solution)/shard_map/ppermute | solution.py:270
  44.6 7.2 %collective-permute-start.1 = (bf16[128,1024]{1,0:T(8,128)(2,1)S(1)}, bf16[128,1024]{1,0:T(8,128)(2,1)S(1)}, u32[]{:S(2)}, u32[]{:S(2)}) collective-permute-start(bf16[128,1024]{1,0:T(8,128)(2,1)S(1)} %bitcast.26), channel_id=1, source_target_pairs={{32,64},{96,128},{160,192},{224,256},{288,320},{352,384},{416,448}... | collective-permute-start | bytes 786440 | tf_op jit(solution)/shard_map/ppermute | solution.py:273
  53.4 9.9 %collective-permute-start.2 = (bf16[256,1152]{1,0:T(8,128)(2,1)S(1)}, bf16[256,1152]{1,0:T(8,128)(2,1)S(1)}, u32[]{:S(2)}, u32[]{:S(2)}) collective-permute-start(bf16[256,1152]{1,0:T(8,128)(2,1)S(1)} %get-tuple-element.14), channel_id=1, source_target_pairs={{0,2},{2,0},{1,3},{3,1},{4,6},{6,4},{5,7},{7,5},{8,10},{10,8},{9,1... | collective-permute-start | bytes 1769480 | tf_op jit(solution)/shard_map/ppermute | solution.py:290
  83.7 48.2 %copy-start.2 = (f32[32]{0:T(128)S(1)}, f32[32]{0:T(128)}, u32[]{:S(2)}) copy-start(f32[32]{0:T(128)} %param.11) | copy-start | bytes 388
  84.6 17.3 %all-to-all-start.2 = ((bf16[8,16,2048]{2,1,0:T(8,128)(2,1)}), bf16[8,16,2048]{2,1,0:T(8,128)(2,1)S(1)}, u32[]{:S(2)}, u32[]{:S(2)}) async-start(bf16[8,16,2048]{2,1,0:T(8,128)(2,1)} %get-tuple-element.16), calls=%async_computation.2 | async-start | bytes 1048576 | tf_op jit(solution)/shard_map/all_to_all | solution.py:234
  123.3 13.3 %all-to-all-start.4 = ((f32[8,8,128]{2,1,0:T(8,128)}), f32[8,8,128]{2,1,0:T(8,128)S(1)}, u32[]{:S(2)}, u32[]{:S(2)}) async-start(f32[8,8,128]{2,1,0:T(8,128)} %shard_map.83), calls=%async_computation.4 | async-start | bytes 65536 | tf_op jit(solution)/shard_map/all_to_all | solution.py:234
